TPU v7x, 32 devices: a whole 2x2x4 slice. The times are simulated.
32 devices in a mesh: leaf: 8 (over z, x), row: 2 (over y), col: 2 (over core).
Axes of the slice: x: 2, y: 2, z: 4, core: 2. Of those that a mesh axis runs over, the one named last changes fastest.
Arguments:
- leaf_rhs: bfloat16 [8, 4096, 128], P('leaf', ('row', 'col')), may hold values from -6 to 6
- leaf_factor: bfloat16 [8, 4096, 4096], P('leaf', ('row', 'col')), as said below
- leaf_coupling: bfloat16 [8, 4096, 4096], P('leaf', None, ('row', 'col')), may hold values from -0.046875 to 0.046875
- border_rows: int32 [8, 4096], P('leaf'), may hold values from 0 to 4095, as said below
- border_count: int32 [8], P('leaf'), may hold values from 1024 to 4096, as said below
- separator_rhs: bfloat16 [4096, 128], P(('leaf', 'row', 'col')), may hold values from -6 to 6
- separator_factor: bfloat16 [4096, 4096], P(('leaf', 'row', 'col')), as said below
Outputs:
- leaf_solution: float32 [8, 4096, 128], P('leaf', ('row', 'col'))
- separator_solution: float32 [4096, 128], P(('leaf', 'row', 'col'))
Inputs may be any that keep to these rules, and one draw needn't show every extreme that they name: `border_rows`: the 4096 row numbers of one section are distinct. Border rows j < border_count[k] of section k are live, the others are unused; some section has all 4096 live. `leaf_factor`: lower triangular with a positive diagonal. `separator_factor`: lower triangular with a positive diagonal.
All inputs are finite; a program needn't handle non-finite values.
Results may differ from a plain program's by a relative error of at most 0.013.
Values may be sent and summed in bfloat16 or wider, within the bound.
No kernel may reach another device: no remote copies, remote signals or barrier semaphores. Data moves between devices by JAX's collectives and lax.ppermute only.
A program may use at most 64 MiB of HBM per device.

v0:
```python
import jax
import jax.numpy as jnp
from jax import lax
from jax.sharding import PartitionSpec as P


def local(
    leaf_rhs, leaf_factor, leaf_coupling, border_rows, border_count, separator_rhs, separator_factor
):
    contract_first = (((0,), (0,)), ((), ()))
    rhs_local = leaf_rhs[0]
    factor_local = leaf_factor[0]
    coupling = leaf_coupling[0]
    index_set = border_rows[0]
    live = jnp.arange(index_set.shape[0], dtype=jnp.int32) < border_count[0]
    columns = rhs_local.shape[1]
    block = factor_local
    forward = jnp.dot(
        block,
        lax.all_gather(rhs_local, ("row", "col"), axis=0, tiled=True),
        preferred_element_type=jnp.float32,
    ).astype(jnp.bfloat16)
    update = jnp.dot(coupling, forward, preferred_element_type=jnp.float32)
    update = jnp.where(live[:, None], update, 0.0)
    sep_rows = separator_factor.shape[0]
    sep_order = separator_factor.shape[1]
    position = lax.axis_index(("leaf", "row", "col")) * sep_rows
    placed = lax.dynamic_update_slice_in_dim(
        jnp.zeros((sep_order, columns), jnp.float32), separator_rhs.astype(jnp.float32), position, 0
    )
    placed = placed.at[index_set].add(-update)
    whole = lax.psum(placed, ("leaf", "row", "col")).astype(jnp.bfloat16)
    root_forward = jnp.dot(separator_factor, whole, preferred_element_type=jnp.float32).astype(
        jnp.bfloat16
    )
    partial_terms = lax.dot_general(
        separator_factor, root_forward, contract_first, preferred_element_type=jnp.float32
    )
    totals = lax.psum(partial_terms, ("leaf", "row", "col"))
    separator_solution = lax.dynamic_slice_in_dim(totals, position, sep_rows, 0)
    rounded = totals.astype(jnp.bfloat16)
    border = jnp.where(live[:, None], rounded[index_set], jnp.zeros((), jnp.bfloat16))
    corrected = (
        forward.astype(jnp.float32)
        - lax.dot_general(coupling, border, contract_first, preferred_element_type=jnp.float32)
    ).astype(jnp.bfloat16)
    block = factor_local
    solution = lax.psum_scatter(
        lax.dot_general(
            block, corrected, contract_first, preferred_element_type=jnp.float32
        ).astype(jnp.bfloat16),
        ("row", "col"),
        scatter_dimension=0,
        tiled=True,
    ).astype(jnp.float32)
    return (solution[None], separator_solution)


def solution(mesh):
    placed = (
        P("leaf", ("row", "col"), None),
        P("leaf", ("row", "col"), None),
        P("leaf", None, ("row", "col")),
        P("leaf", None),
        P("leaf"),
        P(("leaf", "row", "col"), None),
        P(("leaf", "row", "col"), None),
    )
    return jax.shard_map(
        local,
        mesh=mesh,
        in_specs=placed,
        out_specs=(P("leaf", ("row", "col"), None), P(("leaf", "row", "col"), None)),
        check_vma=False,
    )
```

profile of v0, /device:TPU:0, one launch (start us, length us, event | category | flops | bytes accessed | tf_op | source)
XLA Modules:
  0.0 322.0 jit_solution(7589405319605890312)
XLA Ops:
  7.2 0.0 copy-start
  7.2 0.0 all-gather.3.cloned.1.call-start
  7.2 0.7 all-gather.3.cloned.1.call-update
  7.9 0.0 all-reduce.3.cloned.1.call-start
  8.6 0.1 broadcast_in_dim.38
  8.9 20.2 %all-gather.3.cloned.1.call-done = bf16[1,4096,128]{2,1,0:T(8,128)(2,1)} async-done(((bf16[1,1024,128]{2,1,0:T(8,128)(2,1)}), bf16[1,4096,128]{2,1,0:T(8,128)(2,1)}) %all-gather.3.cloned.1.call-update) | async-done | bytes 1048592 | tf_op jit(solution)/shard_map/all_gather | solution.py:20
  29.0 6.1 %fusion.32 = bf16[1024,128]{1,0:T(8,128)(2,1)S(1)} fusion(bf16[1,1024,4096]{2,1,0:T(8,128)(2,1)} %param.8, bf16[1,4096,128]{2,1,0:T(8,128)(2,1)} %all-gather.3.cloned.1.call-done), kind=kOutput, calls=%fused_computation.19 | convolution fusion | flops 1073872896 | bytes 9699328 | tf_op jit(solution)/shard_map/dot_general | solution.py:18
  35.1 4.4 %fusion.17 = f32[4096,128]{1,0:T(8,128)} fusion(bf16[1024,128]{1,0:T(8,128)(2,1)S(1)} %fusion.32, bf16[1,4096,1024]{2,1,0:T(8,128)(2,1)S(1)} %copy-done.1, pred[4096]{0:T(1024)(128)(4,1)S(1)} %iota_compare_fusion), kind=kOutput, calls=%fused_computation.14 | convolution fusion | flops 1074790400 | bytes 10752000 | tf_op jit(solution)/shard_map/dot_general | solution.py:23
  39.5 23.4 %scatter_fusion = f32[4096,128]{1,0:T(8,128)S(1)} fusion(f32[4096,128]{1,0:T(8,128)S(1)} %convert_dynamic-update-slice_fusion, s32[4096]{0:T(1024)S(1)} %bitcast.59, f32[4096,128]{1,0:T(8,128)} %fusion.17), kind=kCustom, calls=%fused_computation.1 | custom fusion | flops 524288 | bytes 6307840 | tf_op jit(solution)/shard_map/scatter-add | solution.py:31
  63.0 62.4 %all-reduce.4 = bf16[4096,128]{1,0:T(8,128)(2,1)} all-reduce(f32[4096,128]{1,0:T(8,128)S(1)} %scatter_fusion), channel_id=1, replica_groups=mesh['leaf'=8,'row'=2,'col'=2] {'leaf','row','col'}, use_global_device_ids=true, to_apply=%region_1.2 | all-reduce | flops 524288 | bytes 3145728 | tf_op jit(solution)/shard_map/psum | solution.py:32
  125.3 3.9 %convolution_bitcast_fusion = f32[4096,128]{0,1:T(8,128)} fusion(bf16[128,4096]{1,0:T(8,128)(2,1)S(1)} %copy-done, bf16[4096,128]{1,0:T(8,128)(2,1)} %all-reduce.4), kind=kOutput, calls=%fused_computation.10 | convolution fusion | flops 268451840 | bytes 4194304 | tf_op jit(solution)/shard_map/dot_general | solution.py:36
  129.2 0.0 all-reduce.3.cloned.1.call-update
  129.2 0.2 reduce-scatter.2.cloned.1.call-start
  129.5 133.4 %all-reduce.3.cloned.1.call-done = f32[4096,128]{0,1:T(8,128)} async-done(((f32[4096,128]{0,1:T(8,128)}), f32[4096,128]{0,1:T(8,128)}) %all-reduce.3.cloned.1.call-update) | async-done | bytes 2097168 | tf_op jit(solution)/shard_map/psum | solution.py:39
  262.8 1.7 convert_element_type.34
  264.6 0.7 copy.12
  265.2 12.1 %gather_fusion = bf16[4096,128]{1,0:T(8,128)(2,1)S(1)} fusion(bf16[4096,128]{1,0:T(8,128)(2,1)S(1)} %copy.12, s32[4096]{0:T(1024)S(1)} %broadcast_clamp_fusion), kind=kCustom, calls=%fused_computation | custom fusion | bytes 2113536 | tf_op jit(solution)/shard_map/gather | solution.py:42
  277.4 12.4 %fusion.20 = bf16[4096,128]{0,1:T(8,128)(2,1)} fusion(bf16[1,1024,4096]{2,1,0:T(8,128)(2,1)} %param.8, bf16[1,4096,1024]{2,1,0:T(8,128)(2,1)} %param.9, bf16[4096,128]{1,0:T(8,128)(2,1)S(1)} %gather_fusion, pred[4096]{0:T(1024)(128)(4,1)S(1)} %iota_compare_fusion, bf16[1024,128]{1,0:T(8,128)(2,1)S(1)} %fusion.32), kind=kOutput, calls=%fused_computation.15 | convolution fusion | flops 2148925440 | bytes 19140608 | tf_op jit(solution)/shard_map/dot_general | solution.py:49
  289.8 0.0 reduce-scatter.2.cloned.1.call-update
  289.8 0.9 constant_dynamic-slice_fusion
  290.6 0.7 copy.14
  291.4 22.1 %reduce-scatter.2.cloned.1.call-done = bf16[1024,128]{0,1:T(8,128)(2,1)} async-done(((bf16[4096,128]{0,1:T(8,128)(2,1)}), bf16[1024,128]{0,1:T(8,128)(2,1)}) %reduce-scatter.2.cloned.1.call-update) | async-done | bytes 262160 | tf_op jit(solution)/shard_map/reduce_scatter | solution.py:48
  313.5 1.0 bitcast_convert_fusion
  314.5 1.0 copy.13
  (11 shorter events, 0.1 us)
Async XLA Ops:
  7.2 118.2 %copy-start = (bf16[128,4096]{1,0:T(8,128)(2,1)S(1)}, bf16[128,4096]{1,0:T(8,128)(2,1)}, u32[]{:S(2)}) copy-start(bf16[128,4096]{1,0:T(8,128)(2,1)} %param.13) | copy-start | bytes 3145732
  7.2 1.6 copy-start.2
  7.2 1.6 copy-start.3
  7.2 21.8 %all-gather.3.cloned.1.call-start = ((), (), s32[]{:S(2)}) async-start(), calls=%async_computation.3 | async-start | bytes 1310720 | tf_op jit(solution)/shard_map/all_gather | solution.py:20
  7.9 254.9 %all-reduce.3.cloned.1.call-start = ((), (), s32[]{:S(2)}) async-start(), calls=%async_computation.1 | async-start | bytes 4194304 | tf_op jit(solution)/shard_map/psum | solution.py:39
  29.0 6.1 %copy-start.1 = (bf16[1,4096,1024]{2,1,0:T(8,128)(2,1)S(1)}, bf16[1,4096,1024]{2,1,0:T(8,128)(2,1)}, u32[]{:S(2)}) copy-start(bf16[1,4096,1024]{2,1,0:T(8,128)(2,1)} %param.9) | copy-start | bytes 25165828
  129.2 184.3 %reduce-scatter.2.cloned.1.call-start = ((), (), s32[]{:S(2)}) async-start(), calls=%async_computation.2 | async-start | bytes 1310720 | tf_op jit(solution)/shard_map/reduce_scatter | solution.py:48
Sparse Core Ops, SparseCore 0:
  9.6 19.4 all-gather.2
  129.4 133.4 all-reduce.2
  289.9 23.5 reduce-scatter.1
where the time goes:
time: 322 us
  waiting for transfers between devices  176 us (55%)
  blocking collectives  62.4 us (19%)
  matrix products  26.7 us (8%)
  other arithmetic  26.2 us (8%)
  local copies, waits for them, and re-layouts  15.5 us (5%)
  between operations  14.5 us (5%)
    psum x1, waiting for transfers between devices, local(): totals = lax.psum(partial_terms, ('leaf', 'row', 'col'))  133 us
    psum x1, blocking collectives, local(): whole = lax.psum(placed, ('leaf', 'row', 'col')).astype(jnp.bfloat16)  62.4 us
    scatter-add x1, other arithmetic, local(): placed = placed.at[index_set].add(-update)  23.4 us
    reduce_scatter x1, waiting for transfers between devices, local(): lax.psum_scatter(lax.dot_general(block, corrected, contract_first, prefer...  22.1 us
    all_gather x1, waiting for transfers between devices, local(): lax.all_gather(rhs_local, ('row', 'col'), axis=0, tiled=True)  20.2 us
    dot_general x1, matrix products, local(): lax.dot_general(block, corrected, contract_first, preferred_element_type=...  12.4 us
    gather x1, local copies, waits for them, and re-layouts, local(): rounded[index_set]  12.1 us
  transfers between devices with their start and end apart: 3, of which 3 were waited for; matrix products, arithmetic and copies ran while one was open for 1% of the time, Pallas kernels for 0%

commit v1 on v0

v1 whole, which is shorter than its diff:
```python
import functools

import jax
import jax.numpy as jnp
from jax import lax
from jax.experimental import pallas as pl
from jax.experimental.pallas import tpu as pltpu
from jax.sharding import PartitionSpec as P

BF16 = jnp.bfloat16
F32 = jnp.float32
AXES = ("leaf", "row", "col")
FIRST = (((0,), (0,)), ((), ()))
VM = pl.BlockSpec(memory_space=pltpu.VMEM)
SM = pl.BlockSpec(memory_space=pltpu.SMEM)
UNROLL = 64


def kernel_call(body, outs, operands, scratch=(), flops=0, vmem=24, name=None):
    moved = sum(a.size * a.dtype.itemsize for a in operands)
    moved += sum(o.size * o.dtype.itemsize for o in outs)
    specs = [SM if a.dtype == jnp.int32 else VM for a in operands]
    return pl.pallas_call(
        body,
        out_shape=list(outs),
        in_specs=specs,
        out_specs=[VM] * len(outs),
        scratch_shapes=list(scratch),
        name=name,
        cost_estimate=pl.CostEstimate(flops=flops, bytes_accessed=moved, transcendentals=0),
        compiler_params=pltpu.CompilerParams(vmem_limit_bytes=vmem << 20),
    )(*operands)


def forward_kernel(blocks, index, factor, *refs):
    pieces, out = refs[:-1], refs[-1]
    rows = factor.shape[0]
    total = None
    for k in range(blocks):
        start = pl.multiple_of(index[k] * rows, rows)
        term = jnp.dot(factor[:, pl.ds(start, rows)], pieces[k][...], preferred_element_type=F32)
        total = term if total is None else total + term
    out[...] = total.astype(BF16)


def chunk_of(rows):
    return 512 if rows % 512 == 0 else rows


def update_kernel(groups, place, coupling, forward, *refs):
    own, sent, placed, held = refs[0], refs[1:groups], refs[groups], refs[groups + 1]
    order = placed.shape[0] - 8
    borders = coupling.shape[0]
    step = chunk_of(borders)
    placed[...] = jnp.zeros_like(placed)
    value = forward[...]
    for first in range(0, borders, step):
        held[...] = jnp.dot(
            coupling[first : first + step, :], value, preferred_element_type=F32
        )

        def body(i, _):
            base = i * UNROLL
            for t in range(UNROLL):
                placed[pl.ds(place[first + base + t], 1), :] = held[pl.ds(base + t, 1), :]
            return 0

        lax.fori_loop(0, step // UNROLL, body, 0)
    part = order // groups
    own[...] = placed[0:part, :]
    for k, ref in enumerate(sent):
        ref[...] = placed[(k + 1) * part : (k + 2) * part, :].astype(BF16)


def add_kernel(arrived, parts, *refs):
    own, received = refs[0], refs[1 : 1 + arrived]
    kept, sent = refs[1 + arrived], refs[2 + arrived :]
    rows = own.shape[0] // parts
    for k in range(parts):
        span = slice(k * rows, (k + 1) * rows)
        total = own[span, :]
        for ref in received:
            total = total + ref[span, :].astype(F32)
        if k == 0:
            kept[...] = total
        else:
            sent[k - 1][...] = total.astype(BF16)


def gathered_kernel(arrived, *refs):
    rhs, own, received, out = refs[0], refs[1], refs[2 : 2 + arrived], refs[-1]
    total = own[...]
    for ref in received:
        total = total + ref[...].astype(F32)
    out[...] = (rhs[...].astype(F32) - total).astype(BF16)


def finish_kernel(arrived, *refs):
    own, received = refs[0], refs[1 : 1 + arrived]
    total = own[...]
    for ref in received:
        total = total + ref[...].astype(F32)
    refs[-2][...] = total
    refs[-1][...] = total.astype(BF16)


def stack_kernel(*refs):
    out = refs[-1]
    rows = refs[0].shape[0]
    for k, ref in enumerate(refs[:-1]):
        out[k * rows : (k + 1) * rows, :] = ref[...]


def split_kernel(parts, groups, column, factor, *refs):
    size = factor.shape[0]
    for k in range(parts):
        for g in range(groups):
            start = pl.multiple_of(column[k * groups + g] * size, size)
            refs[k][:, g * size : (g + 1) * size] = factor[:, pl.ds(start, size)]


def root_forward_kernel(parts, halves, *refs):
    blocks, right = refs[:parts], refs[parts : parts + halves]
    kept, sent = refs[-2], refs[-1]
    rows = blocks[0].shape[0]
    width = right[0].shape[0]
    for k in range(parts):
        total = None
        for h in range(halves):
            term = jnp.dot(
                blocks[k][:, h * width : (h + 1) * width],
                right[h][...],
                preferred_element_type=F32,
            )
            total = term if total is None else total + term
        kept[k * rows : (k + 1) * rows, :] = total
        sent[k * rows : (k + 1) * rows, :] = total.astype(BF16)


def root_back_kernel(parts, halves, sources, *refs):
    blocks, own = refs[:parts], refs[parts]
    received = refs[parts + 1 : 2 * parts]
    outs = refs[2 * parts :]
    rows = blocks[0].shape[0]
    others = [ref[...].astype(F32) for ref in received]
    values = []
    for k in range(parts):
        total = own[k * rows : (k + 1) * rows, :]
        for other, source in zip(others, sources):
            total = total + other[source[k] * rows : (source[k] + 1) * rows, :]
        values.append(total.astype(BF16))
    width = blocks[0].shape[1] // halves
    for h in range(halves):
        total = None
        for k in range(parts):
            term = lax.dot_general(
                blocks[k][:, h * width : (h + 1) * width],
                values[k],
                FIRST,
                preferred_element_type=F32,
            )
            total = term if total is None else total + term
        outs[h][...] = total.astype(outs[h].dtype)


def border_kernel(blocks, place, index, coupling, factor, forward, *refs):
    pieces = refs[:blocks]
    corrected, sent = refs[blocks], refs[blocks + 1 : -2]
    table, held = refs[-2], refs[-1]
    rows = pieces[0].shape[0]
    order = blocks * rows
    for k in range(blocks):
        table[k * rows : (k + 1) * rows, :] = pieces[k][...].astype(F32)
    table[order : order + 8, :] = jnp.zeros((8, table.shape[1]), F32)
    borders = coupling.shape[0]
    step = chunk_of(borders)
    total = forward[...].astype(F32).T
    for first in range(0, borders, step):

        def body(i, _):
            base = pl.multiple_of(i * UNROLL, UNROLL)
            for t in range(UNROLL):
                held[pl.ds(base + t, 1), :] = table[pl.ds(place[first + base + t], 1), :]
            return 0

        lax.fori_loop(0, step // UNROLL, body, 0)
        total = total - lax.dot_general(
            held[...].astype(BF16),
            coupling[first : first + step, :],
            FIRST,
            preferred_element_type=F32,
        )
    value = total.astype(BF16)
    corrected[...] = value
    width = factor.shape[0]
    for k, ref in enumerate(sent):
        start = pl.multiple_of(index[k] * width, width)
        ref[...] = jnp.dot(
            value, factor[:, pl.ds(start, width)], preferred_element_type=F32
        ).astype(ref.dtype)


def blocks_kernel(index, factor, corrected, *outs):
    width = factor.shape[0]
    for k, ref in enumerate(outs):
        start = pl.multiple_of(index[k] * width, width)
        ref[...] = jnp.dot(
            corrected[...], factor[:, pl.ds(start, width)], preferred_element_type=F32
        ).astype(ref.dtype)


def sum_kernel(out_dtype, *refs):
    total = refs[0][...].astype(F32)
    for ref in refs[1:-1]:
        total = total + ref[...].astype(F32)
    refs[-1][...] = total.astype(out_dtype)


def last_kernel(*refs):
    total = refs[0][...].astype(F32)
    for ref in refs[1:-1]:
        total = total + ref[...].astype(F32)
    refs[-1][...] = total.T


def like(shape, dtype):
    return jax.ShapeDtypeStruct(tuple(shape), dtype)


def local(
    sizes,
    leaf_rhs,
    leaf_factor,
    leaf_coupling,
    border_rows,
    border_count,
    separator_rhs,
    separator_factor,
):
    nl, nr, nc = sizes
    nx = 2 if nl % 2 == 0 else 1
    nz = nl // nx
    rhs, factor, coupling = leaf_rhs[0], leaf_factor[0], leaf_coupling[0]
    rows, columns = rhs.shape
    borders = coupling.shape[0]
    own_rows, order = separator_factor.shape
    leaf = lax.axis_index("leaf")
    z, x = leaf // nx, leaf % nx
    y, c = lax.axis_index("row"), lax.axis_index("col")
    plane = [(dx, dy) for dx in range(nx) for dy in range(nr)]
    parts = len(plane)
    section = [(dy, dc) for dy in range(nr) for dc in range(nc)]

    def shift(value, dz=0, dx=0, dy=0, dc=0):
        pairs = []
        for a in range(nz):
            for b in range(nx):
                for d in range(nr):
                    for e in range(nc):
                        here = ((a * nx + b) * nr + d) * nc + e
                        a2, b2 = (a + dz) % nz, (b + dx) % nx
                        d2, e2 = (d + dy) % nr, (e + dc) % nc
                        pairs.append((here, ((a2 * nx + b2) * nr + d2) * nc + e2))
        return lax.ppermute(value, AXES, pairs)

    by_row = {0: rhs}
    for dy in range(1, nr):
        by_row[dy] = shift(rhs, dy=-dy)
    pieces = []
    for dy, dc in section:
        pieces.append(by_row[dy] if dc == 0 else shift(by_row[dy], dc=-dc))
    block = jnp.stack([((y + dy) % nr) * nc + (c + dc) % nc for dy, dc in section]).astype(
        jnp.int32
    )

    row = border_rows[0]
    device, inside = row // own_rows, row % own_rows
    rel_c = (device % nc - c) % nc
    rel_y = (device // nc % nr - y) % nr
    rel_x = (device // (nc * nr) % nx - x) % nx
    rel_z = (device // (nc * nr * nx) - z) % nz
    place = (((rel_c * nx + rel_x) * nr + rel_y) * nz + rel_z) * own_rows + inside
    live = jnp.arange(borders, dtype=jnp.int32) < border_count[0]
    place = jnp.where(live, place, order).astype(jnp.int32)

    groups = [(dc, dz) for dc in range(nc) for dz in range(nz)]
    wide = len(groups) * own_rows

    def owner(dx, dy, dz, dc):
        return ((((z + dz) % nz) * nx + (x + dx) % nx) * nr + (y + dy) % nr) * nc + (c + dc) % nc

    if own_rows % 128 == 0:
        column = jnp.stack(
            [owner(dx, dy, dz, dc) for dx, dy in plane for dc, dz in groups]
        ).astype(jnp.int32)
        cut = kernel_call(
            functools.partial(split_kernel, parts, len(groups)),
            [like((own_rows, wide), BF16)] * parts,
            [column, separator_factor],
            name="split",
        )
    else:
        cut = [
            jnp.concatenate(
                [
                    lax.dynamic_slice_in_dim(
                        separator_factor, owner(dx, dy, dz, dc) * own_rows, own_rows, 1
                    )
                    for dc, dz in groups
                ],
                1,
            )
            for dx, dy in plane
        ]
    root = [cut[0]]
    for (dx, dy) in plane[1:]:
        k = plane.index(((-dx) % nx, (-dy) % nr))
        root.append(shift(cut[k], dx=-dx, dy=-dy))

    forward = kernel_call(
        functools.partial(forward_kernel, len(section)),
        [like((rows, columns), BF16)],
        [block, factor, *pieces],
        flops=2 * factor.size * columns,
        name="forward",
    )[0]

    half = order // nc
    outs = kernel_call(
        functools.partial(update_kernel, nc),
        [like((half, columns), F32)] + [like((half, columns), BF16)] * (nc - 1),
        [place, coupling, forward],
        scratch=[
            pltpu.VMEM((order + 8, columns), F32),
            pltpu.VMEM((chunk_of(borders), columns), F32),
        ],
        flops=2 * coupling.size * columns,
        name="update",
    )
    received = [shift(outs[dc], dc=dc) for dc in range(1, nc)]
    size = half // parts
    outs = kernel_call(
        functools.partial(add_kernel, len(received), parts),
        [like((size, columns), F32)] + [like((size, columns), BF16)] * (parts - 1),
        [outs[0], *received],
        name="add_col",
    )
    received = [shift(outs[k], dx=plane[k][0], dy=plane[k][1]) for k in range(1, parts)]
    outs = kernel_call(
        functools.partial(add_kernel, len(received), nz),
        [like((own_rows, columns), F32)] + [like((own_rows, columns), BF16)] * (nz - 1),
        [outs[0], *received],
        name="add_plane",
    )
    received = [shift(outs[dz], dz=dz) for dz in range(1, nz)]
    gathered = kernel_call(
        functools.partial(gathered_kernel, len(received)),
        [like((own_rows, columns), BF16)],
        [separator_rhs, outs[0], *received],
        name="gathered",
    )[0]

    def along_z(value):
        values = [value] + [shift(value, dz=-dz) for dz in range(1, nz)]
        return kernel_call(
            stack_kernel, [like((nz * own_rows, columns), BF16)], values, name="stack"
        )[0]

    column_block = along_z(gathered)
    right = [column_block] + [shift(column_block, dc=-dc) for dc in range(1, nc)]
    kept, sent = kernel_call(
        functools.partial(root_forward_kernel, parts, nc),
        [like((parts * own_rows, columns), F32), like((parts * own_rows, columns), BF16)],
        [*root, *right],
        flops=2 * parts * own_rows * wide * columns,
        name="root_forward",
    )
    received, sources = [], []
    for dx, dy in plane[1:]:
        received.append(shift(sent, dx=-dx, dy=-dy))
        sources.append([plane.index(((px - dx) % nx, (py - dy) % nr)) for px, py in plane])
    outs = kernel_call(
        functools.partial(root_back_kernel, parts, nc, sources),
        [like((nz * own_rows, columns), F32)] + [like((nz * own_rows, columns), BF16)] * (nc - 1),
        [*root, kept, *received],
        flops=2 * parts * own_rows * wide * columns,
        name="root_back",
    )
    received = [shift(outs[dc], dc=dc) for dc in range(1, nc)]
    outs = kernel_call(
        functools.partial(add_kernel, len(received), nz),
        [like((own_rows, columns), F32)] + [like((own_rows, columns), BF16)] * (nz - 1),
        [outs[0], *received],
        name="add_col2",
    )
    received = [shift(outs[dz], dz=dz) for dz in range(1, nz)]
    separator_solution, rounded = kernel_call(
        functools.partial(finish_kernel, len(received)),
        [like((own_rows, columns), F32), like((own_rows, columns), BF16)],
        [outs[0], *received],
        name="finish",
    )
    layer = along_z(rounded)
    table = [layer] + [shift(layer, dx=-dx, dy=-dy) for dx, dy in plane[1:]]
    pieces = list(table)
    for dc in range(1, nc):
        pieces += [shift(value, dc=-dc) for value in table]

    far = [(dy, dc) for dy, dc in section if dy > 0]
    near = [(dy, dc) for dy, dc in section if dy == 0]
    far_block = block[nc:]
    near_block = block[:nc]
    outs = kernel_call(
        functools.partial(border_kernel, len(pieces)),
        [like((columns, rows), BF16)]
        + [like((columns, rows), F32 if dc == 0 else BF16) for dy, dc in far],
        [place, far_block, coupling, factor, forward, *pieces],
        scratch=[
            pltpu.VMEM((order + 8, columns), F32),
            pltpu.VMEM((chunk_of(borders), columns), F32),
        ],
        flops=2 * (coupling.size + factor.size * len(far) // len(section)) * columns,
        name="border",
    )
    corrected, far_parts = outs[0], dict(zip(far, outs[1:]))
    arrived = []
    for dy in range(1, nr):
        terms = [far_parts[dy, 0]] + [shift(far_parts[dy, dc], dc=dc) for dc in range(1, nc)]
        total = kernel_call(
            functools.partial(sum_kernel, BF16), [like((columns, rows), BF16)], terms, name="sum_far"
        )[0]
        arrived.append(shift(total, dy=dy))
    outs = kernel_call(
        blocks_kernel,
        [like((columns, rows), F32 if dc == 0 else BF16) for dy, dc in near],
        [near_block, factor, corrected],
        flops=2 * factor.size * len(near) // len(section) * columns,
        name="near",
    )
    terms = [outs[0]] + [shift(outs[dc], dc=dc) for dc in range(1, nc)]
    leaf_solution = kernel_call(
        last_kernel, [like((rows, columns), F32)], [*terms, *arrived], name="last"
    )[0]
    return leaf_solution[None], separator_solution


def solution(mesh):
    sizes = tuple(mesh.shape[name] for name in AXES)
    placed = (
        P("leaf", ("row", "col"), None),
        P("leaf", ("row", "col"), None),
        P("leaf", None, ("row", "col")),
        P("leaf", None),
        P("leaf"),
        P(AXES, None),
        P(AXES, None),
    )
    return jax.shard_map(
        functools.partial(local, sizes),
        mesh=mesh,
        in_specs=placed,
        out_specs=(P("leaf", ("row", "col"), None), P(AXES, None)),
        check_vma=False,
    )
```

time: 322 us -> 131 us (0.41)
  waiting for transfers between devices: 176 us -> 55.5 us
  blocking collectives: 62.4 us -> 0 us
  starting transfers between devices: 0.3 us -> 35.8 us
  matrix products: 26.7 us -> 0 us
  Pallas kernels: 0 us -> 25.4 us
  other arithmetic: 26.2 us -> 1.04 us
  between operations: 14.5 us -> 1.49 us
  local copies, waits for them, and re-layouts: 15.5 us -> 11.7 us
    psum x1 -> x0, waiting for transfers between devices: 133 us -> none  [local(): totals = lax.psum(partial_terms, ('leaf', 'row', 'col'))]
    psum x1 -> x0, blocking collectives: 62.4 us -> none  [local(): whole = lax.psum(placed, ('leaf', 'row', 'col')).astype(jnp.bfloat16)]
    ppermute x0 -> x37, waiting for transfers between devices: none -> 55.5 us  [shift(): return lax.ppermute(value, AXES, pairs)]
    ppermute x0 -> x37, starting transfers between devices: none -> 35.8 us  [shift(): return lax.ppermute(value, AXES, pairs)]
    dot_general x4 -> x0, matrix products: 26.7 us -> none  [the longest x1 12.4 us: local(): lax.dot_general(block, corrected, contract_first, preferred_element_type=...]
    pallas_call x0 -> x16, Pallas kernels: none -> 25.4 us  [kernel_call(): pl.pallas_call(body, out_shape=list(outs), in_specs=specs, out_specs=[VM]...]
    scatter-add x1 -> x0, other arithmetic: 23.4 us -> none  [local(): placed = placed.at[index_set].add(-update)]
    reduce_scatter x1 -> x0, waiting for transfers between devices: 22.1 us -> none  [local(): lax.psum_scatter(lax.dot_general(block, corrected, contract_first, prefer...]
  transfers between devices with their start and end apart: 3 -> 37, of which waited for: 3 -> 26; matrix products, arithmetic and copies ran while one was open for 1% -> 1% of each run, Pallas kernels for 0% -> 2%
where the time goes in v1:
time: 131 us
  waiting for transfers between devices  55.5 us (42%)
  starting transfers between devices  35.8 us (27%)
  Pallas kernels  25.4 us (19%)
  local copies, waits for them, and re-layouts  11.7 us (9%)
  between operations  1.49 us (1%)
    ppermute x37, waiting for transfers between devices, shift(): return lax.ppermute(value, AXES, pairs)  55.5 us
    ppermute x37, starting transfers between devices, shift(): return lax.ppermute(value, AXES, pairs)  35.8 us
    pallas_call x16, Pallas kernels, kernel_call(): pl.pallas_call(body, out_shape=list(outs), in_specs=specs, out_specs=[VM]...  25.4 us
    unnamed x14, local copies, waits for them, and re-layouts  11.6 us
  transfers between devices with their start and end apart: 37, of which 26 were waited for; matrix products, arithmetic and copies ran while one was open for 1% of the time, Pallas kernels for 2%

profile of v1, /device:TPU:0, one launch (start us, length us, event | category | flops | bytes accessed | tf_op | source)
XLA Modules:
  0.0 131.0 jit_solution(7507013287572160707)
XLA Ops:
  0.6 3.1 %collective-permute-start.1 = (bf16[1024,128]{1,0:T(8,128)(2,1)}, bf16[1024,128]{1,0:T(8,128)(2,1)S(1)}, u32[]{:S(2)}, u32[]{:S(2)}) collective-permute-start(bf16[1024,128]{1,0:T(8,128)(2,1)} %bitcast.48), channel_id=1, source_target_pairs={{0,2},{1,3},{2,0},{3,1},{4,6},{5,7},{6,4},{7,5},{8,10},{9,11},{10,... | collective-permute-start | bytes 786440 | tf_op jit(solution)/shard_map/ppermute | solution.py:264
  3.7 6.5 %collective-permute-done.1.refs_2_ = bf16[1024,128]{1,0:T(8,128)(2,1)S(1)} collective-permute-done((bf16[1024,128]{1,0:T(8,128)(2,1)}, bf16[1024,128]{1,0:T(8,128)(2,1)S(1)}, u32[]{:S(2)}, u32[]{:S(2)}) %collective-permute-start.1) | collective-permute-done | bytes 262176 | tf_op jit(solution)/shard_map/ppermute | solution.py:264
  11.8 3.4 %copy-done = bf16[1,1024,4096]{2,1,0:T(8,128)(2,1)S(1)} copy-done((bf16[1,1024,4096]{2,1,0:T(8,128)(2,1)S(1)}, bf16[1,1024,4096]{2,1,0:T(8,128)(2,1)}, u32[]{:S(2)}) %copy-start) | copy-done | bytes 8388632
  16.1 2.9 %forward.1 = bf16[1024,128]{1,0:T(8,128)(2,1)S(1)} custom-call(s32[4]{0:T(128)S(1)} %pad_add_fusion.2.index, bf16[1024,4096]{1,0:T(8,128)(2,1)S(1)} %bitcast.43, bf16[1024,128]{1,0:T(8,128)(2,1)S(1)} %bitcast.50, bf16[1024,128]{1,0:T(8,128)(2,1)S(1)} %collective-permute-done.refs_1_, bf16[1024,128]{1,0:T(8,128)(2,1)S(1)} %collective-permute-done.1.refs_2_, ...), custom_call_target="tpu_custom_call" | custom-call | flops 1073741824 | bytes 9699344 | tf_op jit(solution)/shard_map/forward/pallas_call | solution.py:23
  19.5 9.9 %update.1 = (f32[2048,128]{1,0:T(8,128)S(1)}, bf16[2048,128]{1,0:T(8,128)(2,1)S(1)}) custom-call(s32[4096]{0:T(1024)S(1)} %fusion.10.place, bf16[4096,1024]{1,0:T(8,128)(2,1)S(1)} %bitcast.46, bf16[1024,128]{1,0:T(8,128)(2,1)S(1)} %forward.1), custom_call_target="tpu_custom_call" | custom-call | flops 1073741824 | bytes 10240000 | tf_op jit(solution)/shard_map/update/pallas_call | solution.py:23
  31.6 1.8 %collective-permute-start.7 = (bf16[512,128]{1,0:T(8,128)(2,1)S(1)}, bf16[512,128]{1,0:T(8,128)(2,1)S(1)}, u32[]{:S(2)}, u32[]{:S(2)}) collective-permute-start(bf16[512,128]{1,0:T(8,128)(2,1)S(1)} %get-tuple-element.38), channel_id=1, source_target_pairs={{0,2},{1,3},{2,0},{3,1},{4,6},{5,7},{6,4},{7,5},{8,10},{9,11},{10,... | collective-permute-start | bytes 393224 | tf_op jit(solution)/shard_map/ppermute | solution.py:264
  35.3 2.2 %collective-permute-done.7.refs_1_ = bf16[512,128]{1,0:T(8,128)(2,1)S(1)} collective-permute-done((bf16[512,128]{1,0:T(8,128)(2,1)S(1)}, bf16[512,128]{1,0:T(8,128)(2,1)S(1)}, u32[]{:S(2)}, u32[]{:S(2)}) %collective-permute-start.7) | collective-permute-done | bytes 131104 | tf_op jit(solution)/shard_map/ppermute | solution.py:264
  37.4 2.3 %collective-permute-done.8.refs_2_ = bf16[512,128]{1,0:T(8,128)(2,1)S(1)} collective-permute-done((bf16[512,128]{1,0:T(8,128)(2,1)S(1)}, bf16[512,128]{1,0:T(8,128)(2,1)S(1)}, u32[]{:S(2)}, u32[]{:S(2)}) %collective-permute-start.8) | collective-permute-done | bytes 131104 | tf_op jit(solution)/shard_map/ppermute | solution.py:264
  47.7 2.6 %collective-permute-start.11 = (bf16[128,128]{1,0:T(8,128)(2,1)S(1)}, bf16[128,128]{1,0:T(8,128)(2,1)S(1)}, u32[]{:S(2)}, u32[]{:S(2)}) collective-permute-start(bf16[128,128]{1,0:T(8,128)(2,1)S(1)} %get-tuple-element.43), channel_id=1, source_target_pairs={{0,16},{1,17},{2,18},{3,19},{4,20},{5,21},{6,22},{7,23},{8,24},{9,... | collective-permute-start | bytes 98312 | tf_op jit(solution)/shard_map/ppermute | solution.py:264
  54.4 3.1 %collective-permute-start.13 = (bf16[128,128]{1,0:T(8,128)(2,1)S(1)}, bf16[128,128]{1,0:T(8,128)(2,1)S(1)}, u32[]{:S(2)}, u32[]{:S(2)}) collective-permute-start(bf16[128,128]{1,0:T(8,128)(2,1)S(1)} %gathered.1.refs_0_), channel_id=1, source_target_pairs={{0,24},{1,25},{2,26},{3,27},{4,28},{5,29},{6,30},{7,31},{8,0},{9,1... | collective-permute-start | bytes 98312 | tf_op jit(solution)/shard_map/ppermute | solution.py:264
  59.1 3.2 %collective-permute-done.14.refs_2_ = bf16[128,128]{1,0:T(8,128)(2,1)S(1)} collective-permute-done((bf16[128,128]{1,0:T(8,128)(2,1)S(1)}, bf16[128,128]{1,0:T(8,128)(2,1)S(1)}, u32[]{:S(2)}, u32[]{:S(2)}) %collective-permute-start.14) | collective-permute-done | bytes 32800 | tf_op jit(solution)/shard_map/ppermute | solution.py:264
  62.3 2.8 %collective-permute-done.15.refs_3_ = bf16[128,128]{1,0:T(8,128)(2,1)S(1)} collective-permute-done((bf16[128,128]{1,0:T(8,128)(2,1)S(1)}, bf16[128,128]{1,0:T(8,128)(2,1)S(1)}, u32[]{:S(2)}, u32[]{:S(2)}) %collective-permute-start.15) | collective-permute-done | bytes 32800 | tf_op jit(solution)/shard_map/ppermute | solution.py:264
  70.5 2.1 %collective-permute-done.17.refs_5_ = bf16[512,128]{1,0:T(8,128)(2,1)S(1)} collective-permute-done((bf16[512,128]{1,0:T(8,128)(2,1)S(1)}, bf16[512,128]{1,0:T(8,128)(2,1)S(1)}, u32[]{:S(2)}, u32[]{:S(2)}) %collective-permute-start.17) | collective-permute-done | bytes 131104 | tf_op jit(solution)/shard_map/ppermute | solution.py:264
  72.5 2.3 %collective-permute-done.18.refs_6_ = bf16[512,128]{1,0:T(8,128)(2,1)S(1)} collective-permute-done((bf16[512,128]{1,0:T(8,128)(2,1)S(1)}, bf16[512,128]{1,0:T(8,128)(2,1)S(1)}, u32[]{:S(2)}, u32[]{:S(2)}) %collective-permute-start.18) | collective-permute-done | bytes 131104 | tf_op jit(solution)/shard_map/ppermute | solution.py:264
  78.5 2.6 %collective-permute-start.22 = (bf16[128,128]{1,0:T(8,128)(2,1)S(1)}, bf16[128,128]{1,0:T(8,128)(2,1)S(1)}, u32[]{:S(2)}, u32[]{:S(2)}) collective-permute-start(bf16[128,128]{1,0:T(8,128)(2,1)S(1)} %get-tuple-element.51), channel_id=1, source_target_pairs={{0,16},{1,17},{2,18},{3,19},{4,20},{5,21},{6,22},{7,23},{8,24},{9,... | collective-permute-start | bytes 98312 | tf_op jit(solution)/shard_map/ppermute | solution.py:264
  82.3 2.1 %collective-permute-done.21.refs_1_ = bf16[128,128]{1,0:T(8,128)(2,1)S(1)} collective-permute-done((bf16[128,128]{1,0:T(8,128)(2,1)S(1)}, bf16[128,128]{1,0:T(8,128)(2,1)S(1)}, u32[]{:S(2)}, u32[]{:S(2)}) %collective-permute-start.21) | collective-permute-done | bytes 32800 | tf_op jit(solution)/shard_map/ppermute | solution.py:264
  85.7 3.0 %collective-permute-start.24 = (bf16[128,128]{1,0:T(8,128)(2,1)S(1)}, bf16[128,128]{1,0:T(8,128)(2,1)S(1)}, u32[]{:S(2)}, u32[]{:S(2)}) collective-permute-start(bf16[128,128]{1,0:T(8,128)(2,1)S(1)} %get-tuple-element.53.refs_0_), channel_id=1, source_target_pairs={{0,24},{1,25},{2,26},{3,27},{4,28},{5,29},{6,30},{7,31},{8,0},{9,1... | collective-permute-start | bytes 98312 | tf_op jit(solution)/shard_map/ppermute | solution.py:264
  90.3 3.2 %collective-permute-done.25.refs_2_ = bf16[128,128]{1,0:T(8,128)(2,1)S(1)} collective-permute-done((bf16[128,128]{1,0:T(8,128)(2,1)S(1)}, bf16[128,128]{1,0:T(8,128)(2,1)S(1)}, u32[]{:S(2)}, u32[]{:S(2)}) %collective-permute-start.25) | collective-permute-done | bytes 32800 | tf_op jit(solution)/shard_map/ppermute | solution.py:264
  98.2 2.7 %collective-permute-done.27.refs_1_ = bf16[512,128]{1,0:T(8,128)(2,1)S(1)} collective-permute-done((bf16[512,128]{1,0:T(8,128)(2,1)S(1)}, bf16[512,128]{1,0:T(8,128)(2,1)S(1)}, u32[]{:S(2)}, u32[]{:S(2)}) %collective-permute-start.27) | collective-permute-done | bytes 131104 | tf_op jit(solution)/shard_map/ppermute | solution.py:264
  101.5 2.1 %collective-permute-done.29.refs_3_ = bf16[512,128]{1,0:T(8,128)(2,1)S(1)} collective-permute-done((bf16[512,128]{1,0:T(8,128)(2,1)S(1)}, bf16[512,128]{1,0:T(8,128)(2,1)S(1)}, u32[]{:S(2)}, u32[]{:S(2)}) %collective-permute-start.29) | collective-permute-done | bytes 131104 | tf_op jit(solution)/shard_map/ppermute | solution.py:264
  105.0 3.4 %copy-done.1 = bf16[1,1024,4096]{2,1,0:T(8,128)(2,1)S(1)} copy-done((bf16[1,1024,4096]{2,1,0:T(8,128)(2,1)S(1)}, bf16[1,1024,4096]{2,1,0:T(8,128)(2,1)}, u32[]{:S(2)}) %copy-start.1) | copy-done | bytes 8388632
  108.3 3.4 %copy-done.3 = bf16[1,4096,1024]{2,1,0:T(8,128)(2,1)S(1)} copy-done((bf16[1,4096,1024]{2,1,0:T(8,128)(2,1)S(1)}, bf16[1,4096,1024]{2,1,0:T(8,128)(2,1)}, u32[]{:S(2)}) %copy-start.3) | copy-done | bytes 8388632
  111.7 7.8 %border.1 = (bf16[128,1024]{1,0:T(8,128)(2,1)S(1)}, f32[128,1024]{1,0:T(8,128)S(1)}, bf16[128,1024]{1,0:T(8,128)(2,1)S(1)}) custom-call(s32[4096]{0:T(1024)S(1)} %fusion.10.place, s32[2]{0:T(128)S(1)} %pad_add_fusion.1.index, bf16[4096,1024]{1,0:T(8,128)(2,1)S(1)} %bitcast.47, bf16[1024,4096]{1,0:T(8,128)(2,1)S(1)} %bitcast.44, ...), custom_call_target="tpu_custom_call" | custom-call | flops 1610612736 | bytes 19152904 | tf_op jit(solution)/shard_map/border/pallas_call | solution.py:23
  122.6 7.3 %collective-permute-done.36.refs_2_ = bf16[128,1024]{1,0:T(8,128)(2,1)S(1)} collective-permute-done((bf16[128,1024]{1,0:T(8,128)(2,1)S(1)}, bf16[128,1024]{1,0:T(8,128)(2,1)S(1)}, u32[]{:S(2)}, u32[]{:S(2)}) %collective-permute-start.36) | collective-permute-done | bytes 262176 | tf_op jit(solution)/shard_map/ppermute | solution.py:264
  (85 shorter events, 43.7 us)
Async XLA Ops:
  0.6 9.6 %collective-permute-start.1 = (bf16[1024,128]{1,0:T(8,128)(2,1)}, bf16[1024,128]{1,0:T(8,128)(2,1)S(1)}, u32[]{:S(2)}, u32[]{:S(2)}) collective-permute-start(bf16[1024,128]{1,0:T(8,128)(2,1)} %bitcast.48), channel_id=1, source_target_pairs={{0,2},{1,3},{2,0},{3,1},{4,6},{5,7},{6,4},{7,5},{8,10},{9,11},{10,... | collective-permute-start | bytes 786440 | tf_op jit(solution)/shard_map/ppermute | solution.py:264
  3.7 8.1 %collective-permute-start = (bf16[1024,128]{1,0:T(8,128)(2,1)}, bf16[1024,128]{1,0:T(8,128)(2,1)S(1)}, u32[]{:S(2)}, u32[]{:S(2)}) collective-permute-start(bf16[1024,128]{1,0:T(8,128)(2,1)} %bitcast.49), channel_id=1, source_target_pairs={{0,1},{1,0},{2,3},{3,2},{4,5},{5,4},{6,7},{7,6},{8,9},{9,8},{10,11... | collective-permute-start | bytes 786440 | tf_op jit(solution)/shard_map/ppermute | solution.py:264
  31.6 5.8 %collective-permute-start.7 = (bf16[512,128]{1,0:T(8,128)(2,1)S(1)}, bf16[512,128]{1,0:T(8,128)(2,1)S(1)}, u32[]{:S(2)}, u32[]{:S(2)}) collective-permute-start(bf16[512,128]{1,0:T(8,128)(2,1)S(1)} %get-tuple-element.38), channel_id=1, source_target_pairs={{0,2},{1,3},{2,0},{3,1},{4,6},{5,7},{6,4},{7,5},{8,10},{9,11},{10,... | collective-permute-start | bytes 393224 | tf_op jit(solution)/shard_map/ppermute | solution.py:264
  33.4 6.4 %collective-permute-start.8 = (bf16[512,128]{1,0:T(8,128)(2,1)S(1)}, bf16[512,128]{1,0:T(8,128)(2,1)S(1)}, u32[]{:S(2)}, u32[]{:S(2)}) collective-permute-start(bf16[512,128]{1,0:T(8,128)(2,1)S(1)} %get-tuple-element.39), channel_id=1, source_target_pairs={{0,4},{1,5},{2,6},{3,7},{4,0},{5,1},{6,2},{7,3},{8,12},{9,13},{10,... | collective-permute-start | bytes 393224 | tf_op jit(solution)/shard_map/ppermute | solution.py:264
  34.9 6.6 %collective-permute-start.9 = (bf16[512,128]{1,0:T(8,128)(2,1)S(1)}, bf16[512,128]{1,0:T(8,128)(2,1)S(1)}, u32[]{:S(2)}, u32[]{:S(2)}) collective-permute-start(bf16[512,128]{1,0:T(8,128)(2,1)S(1)} %get-tuple-element.40), channel_id=1, source_target_pairs={{0,6},{1,7},{2,4},{3,5},{4,2},{5,3},{6,0},{7,1},{8,14},{9,15},{10,... | collective-permute-start | bytes 393224 | tf_op jit(solution)/shard_map/ppermute | solution.py:264
  41.6 8.8 %collective-permute-start.10 = (bf16[128,128]{1,0:T(8,128)(2,1)S(1)}, bf16[128,128]{1,0:T(8,128)(2,1)S(1)}, u32[]{:S(2)}, u32[]{:S(2)}) collective-permute-start(bf16[128,128]{1,0:T(8,128)(2,1)S(1)} %get-tuple-element.42), channel_id=1, source_target_pairs={{0,8},{1,9},{2,10},{3,11},{4,12},{5,13},{6,14},{7,15},{8,16},{9,17... | collective-permute-start | bytes 98312 | tf_op jit(solution)/shard_map/ppermute | solution.py:264
  44.2 21.0 %collective-permute-start.3 = (bf16[128,1024]{1,0:T(8,128)(2,1)S(1)}, bf16[128,1024]{1,0:T(8,128)(2,1)S(1)}, u32[]{:S(2)}, u32[]{:S(2)}) collective-permute-start(bf16[128,1024]{1,0:T(8,128)(2,1)S(1)} %get-tuple-element.32), channel_id=1, source_target_pairs={{0,2},{1,3},{2,0},{3,1},{4,6},{5,7},{6,4},{7,5},{8,10},{9,11},{10,... | collective-permute-start | bytes 786440 | tf_op jit(solution)/shard_map/ppermute | solution.py:264
  45.8 19.4 %collective-permute-start.4 = (bf16[128,1024]{1,0:T(8,128)(2,1)S(1)}, bf16[128,1024]{1,0:T(8,128)(2,1)S(1)}, u32[]{:S(2)}, u32[]{:S(2)}) collective-permute-start(bf16[128,1024]{1,0:T(8,128)(2,1)S(1)} %get-tuple-element.33), channel_id=1, source_target_pairs={{0,4},{1,5},{2,6},{3,7},{4,0},{5,1},{6,2},{7,3},{8,12},{9,13},{10,... | collective-permute-start | bytes 786440 | tf_op jit(solution)/shard_map/ppermute | solution.py:264
  47.3 17.9 %collective-permute-start.5 = (bf16[128,1024]{1,0:T(8,128)(2,1)S(1)}, bf16[128,1024]{1,0:T(8,128)(2,1)S(1)}, u32[]{:S(2)}, u32[]{:S(2)}) collective-permute-start(bf16[128,1024]{1,0:T(8,128)(2,1)S(1)} %get-tuple-element.34), channel_id=1, source_target_pairs={{0,6},{1,7},{2,4},{3,5},{4,2},{5,3},{6,0},{7,1},{8,14},{9,15},{10,... | collective-permute-start | bytes 786440 | tf_op jit(solution)/shard_map/ppermute | solution.py:264
  47.7 4.8 %collective-permute-start.11 = (bf16[128,128]{1,0:T(8,128)(2,1)S(1)}, bf16[128,128]{1,0:T(8,128)(2,1)S(1)}, u32[]{:S(2)}, u32[]{:S(2)}) collective-permute-start(bf16[128,128]{1,0:T(8,128)(2,1)S(1)} %get-tuple-element.43), channel_id=1, source_target_pairs={{0,16},{1,17},{2,18},{3,19},{4,20},{5,21},{6,22},{7,23},{8,24},{9,... | collective-permute-start | bytes 98312 | tf_op jit(solution)/shard_map/ppermute | solution.py:264
  57.5 4.8 %collective-permute-start.14 = (bf16[128,128]{1,0:T(8,128)(2,1)S(1)}, bf16[128,128]{1,0:T(8,128)(2,1)S(1)}, u32[]{:S(2)}, u32[]{:S(2)}) collective-permute-start(bf16[128,128]{1,0:T(8,128)(2,1)S(1)} %gathered.1.refs_0_), channel_id=1, source_target_pairs={{0,16},{1,17},{2,18},{3,19},{4,20},{5,21},{6,22},{7,23},{8,24},{9,... | collective-permute-start | bytes 98312 | tf_op jit(solution)/shard_map/ppermute | solution.py:264
  59.1 6.0 %collective-permute-start.15 = (bf16[128,128]{1,0:T(8,128)(2,1)S(1)}, bf16[128,128]{1,0:T(8,128)(2,1)S(1)}, u32[]{:S(2)}, u32[]{:S(2)}) collective-permute-start(bf16[128,128]{1,0:T(8,128)(2,1)S(1)} %gathered.1.refs_0_), channel_id=1, source_target_pairs={{0,8},{1,9},{2,10},{3,11},{4,12},{5,13},{6,14},{7,15},{8,16},{9,17... | collective-permute-start | bytes 98312 | tf_op jit(solution)/shard_map/ppermute | solution.py:264
  66.9 5.6 %collective-permute-start.17 = (bf16[512,128]{1,0:T(8,128)(2,1)S(1)}, bf16[512,128]{1,0:T(8,128)(2,1)S(1)}, u32[]{:S(2)}, u32[]{:S(2)}) collective-permute-start(bf16[512,128]{1,0:T(8,128)(2,1)S(1)} %get-tuple-element.46), channel_id=1, source_target_pairs={{0,2},{1,3},{2,0},{3,1},{4,6},{5,7},{6,4},{7,5},{8,10},{9,11},{10,... | collective-permute-start | bytes 393224 | tf_op jit(solution)/shard_map/ppermute | solution.py:264
  68.5 6.4 %collective-permute-start.18 = (bf16[512,128]{1,0:T(8,128)(2,1)S(1)}, bf16[512,128]{1,0:T(8,128)(2,1)S(1)}, u32[]{:S(2)}, u32[]{:S(2)}) collective-permute-start(bf16[512,128]{1,0:T(8,128)(2,1)S(1)} %get-tuple-element.46), channel_id=1, source_target_pairs={{0,4},{1,5},{2,6},{3,7},{4,0},{5,1},{6,2},{7,3},{8,12},{9,13},{10,... | collective-permute-start | bytes 393224 | tf_op jit(solution)/shard_map/ppermute | solution.py:264
  70.0 6.5 %collective-permute-start.19 = (bf16[512,128]{1,0:T(8,128)(2,1)S(1)}, bf16[512,128]{1,0:T(8,128)(2,1)S(1)}, u32[]{:S(2)}, u32[]{:S(2)}) collective-permute-start(bf16[512,128]{1,0:T(8,128)(2,1)S(1)} %get-tuple-element.46), channel_id=1, source_target_pairs={{0,6},{1,7},{2,4},{3,5},{4,2},{5,3},{6,0},{7,1},{8,14},{9,15},{10,... | collective-permute-start | bytes 393224 | tf_op jit(solution)/shard_map/ppermute | solution.py:264
  78.5 6.0 %collective-permute-start.21 = (bf16[128,128]{1,0:T(8,128)(2,1)S(1)}, bf16[128,128]{1,0:T(8,128)(2,1)S(1)}, u32[]{:S(2)}, u32[]{:S(2)}) collective-permute-start(bf16[128,128]{1,0:T(8,128)(2,1)S(1)} %get-tuple-element.50), channel_id=1, source_target_pairs={{0,8},{1,9},{2,10},{3,11},{4,12},{5,13},{6,14},{7,15},{8,16},{9,17... | collective-permute-start | bytes 98312 | tf_op jit(solution)/shard_map/ppermute | solution.py:264
  78.5 5.9 %collective-permute-start.22 = (bf16[128,128]{1,0:T(8,128)(2,1)S(1)}, bf16[128,128]{1,0:T(8,128)(2,1)S(1)}, u32[]{:S(2)}, u32[]{:S(2)}) collective-permute-start(bf16[128,128]{1,0:T(8,128)(2,1)S(1)} %get-tuple-element.51), channel_id=1, source_target_pairs={{0,16},{1,17},{2,18},{3,19},{4,20},{5,21},{6,22},{7,23},{8,24},{9,... | collective-permute-start | bytes 98312 | tf_op jit(solution)/shard_map/ppermute | solution.py:264
  88.7 4.8 %collective-permute-start.25 = (bf16[128,128]{1,0:T(8,128)(2,1)S(1)}, bf16[128,128]{1,0:T(8,128)(2,1)S(1)}, u32[]{:S(2)}, u32[]{:S(2)}) collective-permute-start(bf16[128,128]{1,0:T(8,128)(2,1)S(1)} %get-tuple-element.53.refs_0_), channel_id=1, source_target_pairs={{0,16},{1,17},{2,18},{3,19},{4,20},{5,21},{6,22},{7,23},{8,24},{9,... | collective-permute-start | bytes 98312 | tf_op jit(solution)/shard_map/ppermute | solution.py:264
  88.9 5.7 %collective-permute-start.26 = (bf16[128,128]{1,0:T(8,128)(2,1)S(1)}, bf16[128,128]{1,0:T(8,128)(2,1)S(1)}, u32[]{:S(2)}, u32[]{:S(2)}) collective-permute-start(bf16[128,128]{1,0:T(8,128)(2,1)S(1)} %get-tuple-element.53.refs_0_), channel_id=1, source_target_pairs={{0,8},{1,9},{2,10},{3,11},{4,12},{5,13},{6,14},{7,15},{8,16},{9,17... | collective-permute-start | bytes 98312 | tf_op jit(solution)/shard_map/ppermute | solution.py:264
  94.7 6.3 %collective-permute-start.27 = (bf16[512,128]{1,0:T(8,128)(2,1)S(1)}, bf16[512,128]{1,0:T(8,128)(2,1)S(1)}, u32[]{:S(2)}, u32[]{:S(2)}) collective-permute-start(bf16[512,128]{1,0:T(8,128)(2,1)S(1)} %stack.161.refs_0_), channel_id=1, source_target_pairs={{0,2},{1,3},{2,0},{3,1},{4,6},{5,7},{6,4},{7,5},{8,10},{9,11},{10,... | collective-permute-start | bytes 393224 | tf_op jit(solution)/shard_map/ppermute | solution.py:264
  96.2 5.0 %collective-permute-start.28 = (bf16[512,128]{1,0:T(8,128)(2,1)S(1)}, bf16[512,128]{1,0:T(8,128)(2,1)S(1)}, u32[]{:S(2)}, u32[]{:S(2)}) collective-permute-start(bf16[512,128]{1,0:T(8,128)(2,1)S(1)} %stack.161.refs_0_), channel_id=1, source_target_pairs={{0,4},{1,5},{2,6},{3,7},{4,0},{5,1},{6,2},{7,3},{8,12},{9,13},{10,... | collective-permute-start | bytes 393224 | tf_op jit(solution)/shard_map/ppermute | solution.py:264
  97.7 5.9 %collective-permute-start.29 = (bf16[512,128]{1,0:T(8,128)(2,1)S(1)}, bf16[512,128]{1,0:T(8,128)(2,1)S(1)}, u32[]{:S(2)}, u32[]{:S(2)}) collective-permute-start(bf16[512,128]{1,0:T(8,128)(2,1)S(1)} %stack.161.refs_0_), channel_id=1, source_target_pairs={{0,6},{1,7},{2,4},{3,5},{4,2},{5,3},{6,0},{7,1},{8,14},{9,15},{10,... | collective-permute-start | bytes 393224 | tf_op jit(solution)/shard_map/ppermute | solution.py:264
  98.2 5.5 %collective-permute-start.30 = (bf16[512,128]{1,0:T(8,128)(2,1)S(1)}, bf16[512,128]{1,0:T(8,128)(2,1)S(1)}, u32[]{:S(2)}, u32[]{:S(2)}) collective-permute-start(bf16[512,128]{1,0:T(8,128)(2,1)S(1)} %stack.161.refs_0_), channel_id=1, source_target_pairs={{0,1},{1,0},{2,3},{3,2},{4,5},{5,4},{6,7},{7,6},{8,9},{9,8},{10,11... | collective-permute-start | bytes 393224 | tf_op jit(solution)/shard_map/ppermute | solution.py:264
  121.5 8.4 %collective-permute-start.36 = (bf16[128,1024]{1,0:T(8,128)(2,1)S(1)}, bf16[128,1024]{1,0:T(8,128)(2,1)S(1)}, u32[]{:S(2)}, u32[]{:S(2)}) collective-permute-start(bf16[128,1024]{1,0:T(8,128)(2,1)S(1)} %sum_far.1), channel_id=1, source_target_pairs={{0,2},{1,3},{2,0},{3,1},{4,6},{5,7},{6,4},{7,5},{8,10},{9,11},{10,... | collective-permute-start | bytes 786440 | tf_op jit(solution)/shard_map/ppermute | solution.py:264
  (20 other events, 111.0 us)

commit v2 on v1

v2 whole, which is shorter than its diff:
```python
import functools

import jax
import jax.numpy as jnp
from jax import lax
from jax.experimental import pallas as pl
from jax.experimental.pallas import tpu as pltpu
from jax.sharding import PartitionSpec as P


BF16 = jnp.bfloat16
F32 = jnp.float32
AXES = ("leaf", "row", "col")
FIRST = (((0,), (0,)), ((), ()))
VM = pl.BlockSpec(memory_space=pltpu.VMEM)
SM = pl.BlockSpec(memory_space=pltpu.SMEM)
ANY = pl.BlockSpec(memory_space=pltpu.HBM)


def kernel_call(body, outs, operands, scratch=(), flops=0, vmem=10, apart=()):
    moved = sum(a.size * a.dtype.itemsize for a in operands)
    moved += sum(o.size * o.dtype.itemsize for o in outs)
    specs = [
        ANY if k in apart else SM if a.dtype == jnp.int32 else VM for k, a in enumerate(operands)
    ]
    return pl.pallas_call(
        body,
        out_shape=list(outs),
        in_specs=specs,
        out_specs=[VM] * len(outs),
        scratch_shapes=list(scratch),
        cost_estimate=pl.CostEstimate(flops=flops, bytes_accessed=moved, transcendentals=0),
        compiler_params=pltpu.CompilerParams(vmem_limit_bytes=vmem << 20),
    )(*operands)


def load_kernel(section, parts, groups, block, column, factor, coupling, separator, *refs):
    wide, tall, cut, sems = refs[:section], refs[section], refs[section + 1 : -1], refs[-1]
    width, size = factor.shape[0], separator.shape[0]
    copies = []
    for k in range(section):
        start = pl.multiple_of(block[k] * width, width)
        copies.append(
            pltpu.make_async_copy(factor.at[:, pl.ds(start, width)], wide[k], sems.at[k])
        )
    for k in range(parts):
        for g in range(groups):
            start = pl.multiple_of(column[k * groups + g] * size, size)
            copies.append(
                pltpu.make_async_copy(
                    separator.at[:, pl.ds(start, size)],
                    cut[k].at[:, pl.ds(g * size, size)],
                    sems.at[len(copies)],
                )
            )
    copies.append(pltpu.make_async_copy(coupling, tall, sems.at[len(copies)]))
    for copy in copies:
        copy.start()
    for copy in copies:
        copy.wait()


def near_kernel(count, *refs):
    blocks, pieces, partial = refs[:count], refs[count : 2 * count], refs[-1]
    total = None
    for k in range(count):
        term = jnp.dot(blocks[k][...], pieces[k][...], preferred_element_type=F32)
        total = term if total is None else total + term
    partial[...] = total


def chunk_of(rows):
    return 256 if rows % 256 == 0 else rows


def update_kernel(groups, far, place, partial, coupling, *refs):
    blocks, pieces = refs[:far], refs[far : 2 * far]
    forward, own, sent = refs[2 * far], refs[2 * far + 1], refs[2 * far + 2 : -3]
    placed, held = refs[-3], refs[-2:]
    order = placed.shape[0] - 8
    borders = coupling.shape[0]
    step = chunk_of(borders)
    count = borders // step
    total = partial[...]
    for k in range(far):
        total = total + jnp.dot(blocks[k][...], pieces[k][...], preferred_element_type=F32)
    forward[...] = total.astype(BF16)
    placed[...] = jnp.zeros_like(placed)

    def multiply(k):
        held[k % 2][...] = jnp.dot(
            coupling[k * step : (k + 1) * step, :], forward[...], preferred_element_type=F32
        )

    def scatter(k):
        for t in range(step):
            placed[pl.ds(place[k * step + t], 1), :] = held[k % 2][t : t + 1, :]

    multiply(0)
    for k in range(count):
        if k + 1 < count:
            multiply(k + 1)
        scatter(k)
    part = order // groups
    own[...] = placed[0:part, :]
    for k, ref in enumerate(sent):
        ref[...] = placed[(k + 1) * part : (k + 2) * part, :].astype(BF16)


def add_kernel(arrived, parts, *refs):
    own, received = refs[0], refs[1 : 1 + arrived]
    kept, sent = refs[1 + arrived], refs[2 + arrived :]
    rows = own.shape[0] // parts
    for k in range(parts):
        span = slice(k * rows, (k + 1) * rows)
        total = own[span, :]
        for ref in received:
            total = total + ref[span, :].astype(F32)
        if k == 0:
            kept[...] = total
        else:
            sent[k - 1][...] = total.astype(BF16)


def gathered_kernel(arrived, *refs):
    rhs, own, received, out = refs[0], refs[1], refs[2 : 2 + arrived], refs[-1]
    total = own[...]
    for ref in received:
        total = total + ref[...].astype(F32)
    out[...] = (rhs[...].astype(F32) - total).astype(BF16)


def finish_kernel(arrived, *refs):
    own, received = refs[0], refs[1 : 1 + arrived]
    total = own[...]
    for ref in received:
        total = total + ref[...].astype(F32)
    refs[-2][...] = total
    refs[-1][...] = total.astype(BF16)


def stack_kernel(*refs):
    out = refs[-1]
    rows = refs[0].shape[0]
    for k, ref in enumerate(refs[:-1]):
        out[k * rows : (k + 1) * rows, :] = ref[...]


def root_forward_kernel(parts, halves, *refs):
    blocks, right = refs[:parts], refs[parts : parts + halves]
    kept, sent = refs[-2], refs[-1]
    rows = blocks[0].shape[0]
    width = right[0].shape[0]
    for k in range(parts):
        total = None
        for h in range(halves):
            term = jnp.dot(
                blocks[k][:, h * width : (h + 1) * width],
                right[h][...],
                preferred_element_type=F32,
            )
            total = term if total is None else total + term
        kept[k * rows : (k + 1) * rows, :] = total
        sent[k * rows : (k + 1) * rows, :] = total.astype(BF16)


def root_back_kernel(parts, halves, sources, *refs):
    blocks, own = refs[:parts], refs[parts]
    received = refs[parts + 1 : 2 * parts]
    outs = refs[2 * parts :]
    rows = blocks[0].shape[0]
    others = [ref[...].astype(F32) for ref in received]
    values = []
    for k in range(parts):
        total = own[k * rows : (k + 1) * rows, :]
        for other, source in zip(others, sources):
            total = total + other[source[k] * rows : (source[k] + 1) * rows, :]
        values.append(total.astype(BF16))
    width = blocks[0].shape[1] // halves
    for h in range(halves):
        total = None
        for k in range(parts):
            term = lax.dot_general(
                blocks[k][:, h * width : (h + 1) * width],
                values[k],
                FIRST,
                preferred_element_type=F32,
            )
            total = term if total is None else total + term
        outs[h][...] = total.astype(outs[h].dtype)


def border_kernel(blocks, far, place, forward, coupling, *refs):
    wide, pieces = refs[:far], refs[far : far + blocks]
    corrected, sent = refs[far + blocks], refs[far + blocks + 1 : -4]
    table, sums, held = refs[-4], refs[-3], refs[-2:]
    rows = pieces[0].shape[0]
    order = blocks * rows
    borders = coupling.shape[0]
    step = chunk_of(borders)
    count = borders // step
    for k in range(blocks):
        table[k * rows : (k + 1) * rows, :] = pieces[k][...].astype(F32)
    table[order : order + 8, :] = jnp.zeros((8, table.shape[1]), F32)
    sums[...] = forward[...].astype(F32).T

    def gather(k):
        for t in range(step):
            held[k % 2][t : t + 1, :] = table[pl.ds(place[k * step + t], 1), :]

    def multiply(k):
        sums[...] -= lax.dot_general(
            held[k % 2][...].astype(BF16),
            coupling[k * step : (k + 1) * step, :],
            FIRST,
            preferred_element_type=F32,
        )

    gather(0)
    for k in range(count):
        if k + 1 < count:
            gather(k + 1)
        multiply(k)
    corrected[...] = sums[...].astype(BF16)
    for k, ref in enumerate(sent):
        ref[...] = jnp.dot(
            corrected[...], wide[k][...], preferred_element_type=F32
        ).astype(ref.dtype)


def blocks_kernel(corrected, *refs):
    count = len(refs) // 2
    for wide, ref in zip(refs[:count], refs[count:]):
        ref[...] = jnp.dot(
            corrected[...], wide[...], preferred_element_type=F32
        ).astype(ref.dtype)


def sum_kernel(out_dtype, *refs):
    total = refs[0][...].astype(F32)
    for ref in refs[1:-1]:
        total = total + ref[...].astype(F32)
    refs[-1][...] = total.astype(out_dtype)


def last_kernel(*refs):
    total = refs[0][...].astype(F32)
    for ref in refs[1:-1]:
        total = total + ref[...].astype(F32)
    refs[-1][...] = total.T


def like(shape, dtype):
    return jax.ShapeDtypeStruct(tuple(shape), dtype)


def local(
    sizes,
    leaf_rhs,
    leaf_factor,
    leaf_coupling,
    border_rows,
    border_count,
    separator_rhs,
    separator_factor,
):
    nl, nr, nc = sizes
    nx = 2 if nl % 2 == 0 else 1
    nz = nl // nx
    rhs, factor, coupling = leaf_rhs[0], leaf_factor[0], leaf_coupling[0]
    rows, columns = rhs.shape
    borders = coupling.shape[0]
    own_rows, order = separator_factor.shape
    leaf = lax.axis_index("leaf")
    z, x = leaf // nx, leaf % nx
    y, c = lax.axis_index("row"), lax.axis_index("col")
    plane = [(dx, dy) for dx in range(nx) for dy in range(nr)]
    parts = len(plane)
    section = [(dy, dc) for dy in range(nr) for dc in range(nc)]

    def shift(value, dz=0, dx=0, dy=0, dc=0):
        pairs = []
        for a in range(nz):
            for b in range(nx):
                for d in range(nr):
                    for e in range(nc):
                        here = ((a * nx + b) * nr + d) * nc + e
                        a2, b2 = (a + dz) % nz, (b + dx) % nx
                        d2, e2 = (d + dy) % nr, (e + dc) % nc
                        pairs.append((here, ((a2 * nx + b2) * nr + d2) * nc + e2))
        return lax.ppermute(value, AXES, pairs)

    def send_z(values):
        out = []
        for dz in range(1, nz):
            out.append(shift(values[dz], dz=dz))
        return out

    by_row = {0: rhs}
    for dy in range(1, nr):
        by_row[dy] = shift(rhs, dy=-dy)
    pieces = []
    for dy, dc in section:
        pieces.append(by_row[dy] if dc == 0 else shift(by_row[dy], dc=-dc))
    block = jnp.stack([((y + dy) % nr) * nc + (c + dc) % nc for dy, dc in section]).astype(
        jnp.int32
    )

    row = border_rows[0]
    device, inside = row // own_rows, row % own_rows
    rel_c = (device % nc - c) % nc
    rel_y = (device // nc % nr - y) % nr
    rel_x = (device // (nc * nr) % nx - x) % nx
    rel_z = (device // (nc * nr * nx) - z) % nz
    place = (((rel_c * nx + rel_x) * nr + rel_y) * nz + rel_z) * own_rows + inside
    live = jnp.arange(borders, dtype=jnp.int32) < border_count[0]
    place = jnp.where(live, place, order).astype(jnp.int32)

    groups = [(dc, dz) for dc in range(nc) for dz in range(nz)]
    wide = len(groups) * own_rows

    def owner(dx, dy, dz, dc):
        return ((((z + dz) % nz) * nx + (x + dx) % nx) * nr + (y + dy) % nr) * nc + (c + dc) % nc

    direct = own_rows % 128 == 0
    column = jnp.stack(
        [owner(dx, dy, dz, dc) for dx, dy in plane for dc, dz in groups]
    ).astype(jnp.int32)
    loads = parts if direct else 0
    loaded = kernel_call(
        functools.partial(load_kernel, len(section), loads, len(groups)),
        [like((rows, rows), BF16)] * len(section)
        + [like(coupling.shape, BF16)]
        + [like((own_rows, wide), BF16)] * loads,
        [block, column, factor, coupling, separator_factor],
        scratch=[pltpu.SemaphoreType.DMA((len(section) + loads * len(groups) + 1,))],
        vmem=33,
        apart=(2, 3, 4),
    )
    wide_blocks, tall, cut = loaded[: len(section)], loaded[len(section)], loaded[-parts:]
    if not direct:
        cut = [
            jnp.concatenate(
                [
                    lax.dynamic_slice_in_dim(
                        separator_factor, owner(dx, dy, dz, dc) * own_rows, own_rows, 1
                    )
                    for dc, dz in groups
                ],
                1,
            )
            for dx, dy in plane
        ]
    root = [cut[0]]
    held = list(cut)
    late = [plane.index((dx, dy)) for dx, dy in plane if dy > 0]
    if nr > 1:
        *after, pieces[nc] = lax.optimization_barrier((*[cut[k] for k in late], pieces[nc]))
        for k, value in zip(late, after):
            held[k] = value
    for dx, dy in plane[1:]:
        k = plane.index(((-dx) % nx, (-dy) % nr))
        root.append(shift(held[k], dx=-dx, dy=-dy))

    half = order // nc
    far_count = len(section) - nc
    near = kernel_call(
        functools.partial(near_kernel, nc),
        [like((rows, columns), F32)],
        [*wide_blocks[:nc], *pieces[:nc]],
        flops=2 * rows * rows * nc * columns,
    )[0]
    outs = kernel_call(
        functools.partial(update_kernel, nc, far_count),
        [like((rows, columns), BF16), like((half, columns), F32)]
        + [like((half, columns), BF16)] * (nc - 1),
        [place, near, tall, *wide_blocks[nc:], *pieces[nc:]],
        scratch=[pltpu.VMEM((order + 8, columns), F32)]
        + [pltpu.VMEM((chunk_of(borders), columns), F32)] * 2,
        flops=2 * (coupling.size + rows * rows * far_count) * columns,
    )
    forward, outs = outs[0], outs[1:]
    received = [shift(outs[dc], dc=dc) for dc in range(1, nc)]
    size = half // parts
    outs = kernel_call(
        functools.partial(add_kernel, len(received), parts),
        [like((size, columns), F32)] + [like((size, columns), BF16)] * (parts - 1),
        [outs[0], *received],
    )
    received = []
    for k, (dx, dy) in list(enumerate(plane))[1:]:
        received.append(shift(outs[k], dx=dx, dy=dy))
    outs = kernel_call(
        functools.partial(add_kernel, len(received), nz),
        [like((own_rows, columns), F32)] + [like((own_rows, columns), BF16)] * (nz - 1),
        [outs[0], *received],
    )
    received = send_z(outs)
    gathered = kernel_call(
        functools.partial(gathered_kernel, len(received)),
        [like((own_rows, columns), BF16)],
        [separator_rhs, outs[0], *received],
    )[0]

    def along_z(value):
        values = [value]
        for dz in range(1, nz):
            values.append(shift(value, dz=-dz))
        return kernel_call(stack_kernel, [like((nz * own_rows, columns), BF16)], values)[0]

    column_block = along_z(gathered)
    right = [column_block] + [shift(column_block, dc=-dc) for dc in range(1, nc)]
    kept, sent = kernel_call(
        functools.partial(root_forward_kernel, parts, nc),
        [like((parts * own_rows, columns), F32), like((parts * own_rows, columns), BF16)],
        [*root, *right],
        flops=2 * parts * own_rows * wide * columns,
    )
    received, sources = [], []
    for k, (dx, dy) in list(enumerate(plane))[1:]:
        received.append(shift(sent, dx=-dx, dy=-dy))
        sources.append([plane.index(((px - dx) % nx, (py - dy) % nr)) for px, py in plane])
    outs = kernel_call(
        functools.partial(root_back_kernel, parts, nc, sources),
        [like((nz * own_rows, columns), F32)] + [like((nz * own_rows, columns), BF16)] * (nc - 1),
        [*root, kept, *received],
        flops=2 * parts * own_rows * wide * columns,
    )
    received = [shift(outs[dc], dc=dc) for dc in range(1, nc)]
    outs = kernel_call(
        functools.partial(add_kernel, len(received), nz),
        [like((own_rows, columns), F32)] + [like((own_rows, columns), BF16)] * (nz - 1),
        [outs[0], *received],
    )
    received = send_z(outs)
    separator_solution, rounded = kernel_call(
        functools.partial(finish_kernel, len(received)),
        [like((own_rows, columns), F32), like((own_rows, columns), BF16)],
        [outs[0], *received],
    )
    layer = along_z(rounded)
    table = [layer]
    for k, (dx, dy) in list(enumerate(plane))[1:]:
        table.append(shift(layer, dx=-dx, dy=-dy))
    pieces = list(table)
    for dc in range(1, nc):
        pieces += [shift(value, dc=-dc) for value in table]

    far = [(dy, dc) for dy, dc in section if dy > 0]
    near = [(dy, dc) for dy, dc in section if dy == 0]
    outs = kernel_call(
        functools.partial(border_kernel, len(pieces), len(far)),
        [like((columns, rows), BF16)]
        + [like((columns, rows), F32 if dc == 0 else BF16) for dy, dc in far],
        [place, forward, tall, *wide_blocks[nc:], *pieces],
        scratch=[pltpu.VMEM((order + 8, columns), F32), pltpu.VMEM((columns, rows), F32)]
        + [pltpu.VMEM((chunk_of(borders), columns), F32)] * 2,
        flops=2 * (coupling.size + factor.size * len(far) // len(section)) * columns,
    )
    corrected, far_parts = outs[0], dict(zip(far, outs[1:]))
    arrived = []
    for dy in range(1, nr):
        terms = [far_parts[dy, 0]] + [shift(far_parts[dy, dc], dc=dc) for dc in range(1, nc)]
        total = kernel_call(
            functools.partial(sum_kernel, BF16), [like((columns, rows), BF16)], terms
        )[0]
        arrived.append(shift(total, dy=dy))
    outs = kernel_call(
        blocks_kernel,
        [like((columns, rows), F32 if dc == 0 else BF16) for dy, dc in near],
        [corrected, *wide_blocks[:nc]],
        flops=2 * factor.size * len(near) // len(section) * columns,
    )
    terms = [outs[0]] + [shift(outs[dc], dc=dc) for dc in range(1, nc)]
    leaf_solution = kernel_call(last_kernel, [like((rows, columns), F32)], [*terms, *arrived])[0]
    return leaf_solution[None], separator_solution


def solution(mesh):
    sizes = tuple(mesh.shape[name] for name in AXES)
    placed = (
        P("leaf", ("row", "col"), None),
        P("leaf", ("row", "col"), None),
        P("leaf", None, ("row", "col")),
        P("leaf", None),
        P("leaf"),
        P(AXES, None),
        P(AXES, None),
    )

    def whole(*arrays):
        return local(sizes, *arrays)

    return jax.shard_map(
        whole,
        mesh=mesh,
        in_specs=placed,
        out_specs=(P("leaf", ("row", "col"), None), P(AXES, None)),
        check_vma=False,
    )
```

time: 131 us -> 109 us (0.83)
  waiting for transfers between devices: 55.5 us -> 42.7 us
  local copies, waits for them, and re-layouts: 11.7 us -> 1.34 us
  starting transfers between devices: 35.8 us -> 38.2 us
    ppermute x37, waiting for transfers between devices: 55.5 us -> 42.7 us  [shift(): return lax.ppermute(value, AXES, pairs)]
    unnamed x14 -> x8, local copies, waits for them, and re-layouts: 11.6 us -> 1.24 us
    ppermute x37, starting transfers between devices: 35.8 us -> 38.2 us  [shift(): return lax.ppermute(value, AXES, pairs)]
  transfers between devices with their start and end apart: 37 -> 37, of which waited for: 26 -> 26; matrix products, arithmetic and copies ran while one was open for 1% -> 0% of each run, Pallas kernels for 2% -> 8%
where the time goes in v2:
time: 109 us
  waiting for transfers between devices  42.7 us (39%)
  starting transfers between devices  38.2 us (35%)
  Pallas kernels  24.8 us (23%)
  between operations  1.59 us (1%)
  local copies, waits for them, and re-layouts  1.34 us (1%)
    ppermute x37, waiting for transfers between devices, shift(): return lax.ppermute(value, AXES, pairs)  42.7 us
    ppermute x37, starting transfers between devices, shift(): return lax.ppermute(value, AXES, pairs)  38.2 us
    pallas_call x16, Pallas kernels, kernel_call(): pl.pallas_call(body, out_shape=list(outs), in_specs=specs, out_specs=[VM]...  24.8 us
  transfers between devices with their start and end apart: 37, of which 26 were waited for; matrix products, arithmetic and copies ran while one was open for 0% of the time, Pallas kernels for 8%

profile of v2, /device:TPU:0, one launch (start us, length us, event | category | flops | bytes accessed | tf_op | source)
XLA Modules:
  0.0 108.9 jit_solution(407981686721146784)
XLA Ops:
  0.6 3.1 %collective-permute-start.1 = (bf16[1024,128]{1,0:T(8,128)(2,1)}, bf16[1024,128]{1,0:T(8,128)(2,1)S(1)}, u32[]{:S(2)}, u32[]{:S(2)}) collective-permute-start(bf16[1024,128]{1,0:T(8,128)(2,1)} %bitcast.43), channel_id=1, source_target_pairs={{0,2},{1,3},{2,0},{3,1},{4,6},{5,7},{6,4},{7,5},{8,10},{9,11},{10,... | collective-permute-start | bytes 786440 | tf_op jit(solution)/shard_map/ppermute | solution.py:291
  5.9 6.9 %shard_map.86 = (bf16[1024,1024]{1,0:T(8,128)(2,1)S(1)}, bf16[1024,1024]{1,0:T(8,128)(2,1)S(1)}, bf16[1024,1024]{1,0:T(8,128)(2,1)S(1)}, bf16[1024,1024]{1,0:T(8...) custom-call(s32[4]{0:T(128)S(1)} %pad_add_fusion.block, ...), custom_call_target="tpu_custom_call" | custom-call | bytes 35651728 | tf_op jit(solution)/shard_map/pallas_call | solution.py:26
  14.7 7.2 %shard_map.88 = (bf16[1024,128]{1,0:T(8,128)(2,1)S(1)}, f32[2048,128]{1,0:T(8,128)S(1)}, bf16[2048,128]{1,0:T(8,128)(2,1)S(1)}) custom-call(s32[4096]{0:T(1024)S(1)} %fusion.10.place, f32[1024,128]{1,0:T(8,128)S(1)} %shard_map.87.partial, bf16[4096,1024]{1,0:T(8,128)(2,1)S(1)} %get-tuple-element.42.coupling, ...), custom_call_target="tpu_custom_call" | custom-call | flops 1610612736 | bytes 15482880 | tf_op jit(solution)/shard_map/pallas_call | solution.py:26
  22.2 1.8 %collective-permute-done.6.refs_1_ = bf16[2048,128]{1,0:T(8,128)(2,1)S(1)} collective-permute-done((bf16[2048,128]{1,0:T(8,128)(2,1)S(1)}, bf16[2048,128]{1,0:T(8,128)(2,1)S(1)}, u32[]{:S(2)}, u32[]{:S(2)}) %collective-permute-start.6) | collective-permute-done | bytes 524320 | tf_op jit(solution)/shard_map/ppermute | solution.py:291
  24.2 2.0 %collective-permute-start.8 = (bf16[512,128]{1,0:T(8,128)(2,1)S(1)}, bf16[512,128]{1,0:T(8,128)(2,1)S(1)}, u32[]{:S(2)}, u32[]{:S(2)}) collective-permute-start(bf16[512,128]{1,0:T(8,128)(2,1)S(1)} %get-tuple-element.57), channel_id=1, source_target_pairs={{0,4},{1,5},{2,6},{3,7},{4,0},{5,1},{6,2},{7,3},{8,12},{9,13},{10,... | collective-permute-start | bytes 393224 | tf_op jit(solution)/shard_map/ppermute | solution.py:291
  27.6 2.1 %collective-permute-done.7.refs_1_ = bf16[512,128]{1,0:T(8,128)(2,1)S(1)} collective-permute-done((bf16[512,128]{1,0:T(8,128)(2,1)S(1)}, bf16[512,128]{1,0:T(8,128)(2,1)S(1)}, u32[]{:S(2)}, u32[]{:S(2)}) %collective-permute-start.7) | collective-permute-done | bytes 131104 | tf_op jit(solution)/shard_map/ppermute | solution.py:291
  30.1 3.5 %collective-permute-done.9.refs_3_ = bf16[512,128]{1,0:T(8,128)(2,1)S(1)} collective-permute-done((bf16[512,128]{1,0:T(8,128)(2,1)S(1)}, bf16[512,128]{1,0:T(8,128)(2,1)S(1)}, u32[]{:S(2)}, u32[]{:S(2)}) %collective-permute-start.9) | collective-permute-done | bytes 131104 | tf_op jit(solution)/shard_map/ppermute | solution.py:291
  33.7 1.7 %collective-permute-start.10 = (bf16[128,128]{1,0:T(8,128)(2,1)S(1)}, bf16[128,128]{1,0:T(8,128)(2,1)S(1)}, u32[]{:S(2)}, u32[]{:S(2)}) collective-permute-start(bf16[128,128]{1,0:T(8,128)(2,1)S(1)} %get-tuple-element.60), channel_id=1, source_target_pairs={{0,8},{1,9},{2,10},{3,11},{4,12},{5,13},{6,14},{7,15},{8,16},{9,17... | collective-permute-start | bytes 98312 | tf_op jit(solution)/shard_map/ppermute | solution.py:291
  38.9 2.6 %collective-permute-start.11 = (bf16[128,128]{1,0:T(8,128)(2,1)S(1)}, bf16[128,128]{1,0:T(8,128)(2,1)S(1)}, u32[]{:S(2)}, u32[]{:S(2)}) collective-permute-start(bf16[128,128]{1,0:T(8,128)(2,1)S(1)} %get-tuple-element.61), channel_id=1, source_target_pairs={{0,16},{1,17},{2,18},{3,19},{4,20},{5,21},{6,22},{7,23},{8,24},{9,... | collective-permute-start | bytes 98312 | tf_op jit(solution)/shard_map/ppermute | solution.py:291
  43.7 1.7 %collective-permute-done.12.refs_4_ = bf16[128,128]{1,0:T(8,128)(2,1)S(1)} collective-permute-done((bf16[128,128]{1,0:T(8,128)(2,1)S(1)}, bf16[128,128]{1,0:T(8,128)(2,1)S(1)}, u32[]{:S(2)}, u32[]{:S(2)}) %collective-permute-start.12) | collective-permute-done | bytes 32800 | tf_op jit(solution)/shard_map/ppermute | solution.py:291
  45.6 3.5 %collective-permute-start.14 = (bf16[128,128]{1,0:T(8,128)(2,1)S(1)}, bf16[128,128]{1,0:T(8,128)(2,1)S(1)}, u32[]{:S(2)}, u32[]{:S(2)}) collective-permute-start(bf16[128,128]{1,0:T(8,128)(2,1)S(1)} %shard_map.91.refs_0_), channel_id=1, source_target_pairs={{0,16},{1,17},{2,18},{3,19},{4,20},{5,21},{6,22},{7,23},{8,24},{9,... | collective-permute-start | bytes 98312 | tf_op jit(solution)/shard_map/ppermute | solution.py:291
  49.1 2.1 %collective-permute-done.15.refs_3_ = bf16[128,128]{1,0:T(8,128)(2,1)S(1)} collective-permute-done((bf16[128,128]{1,0:T(8,128)(2,1)S(1)}, bf16[128,128]{1,0:T(8,128)(2,1)S(1)}, u32[]{:S(2)}, u32[]{:S(2)}) %collective-permute-start.15) | collective-permute-done | bytes 32800 | tf_op jit(solution)/shard_map/ppermute | solution.py:291
  52.5 2.7 %collective-permute-done.13.refs_1_ = bf16[128,128]{1,0:T(8,128)(2,1)S(1)} collective-permute-done((bf16[128,128]{1,0:T(8,128)(2,1)S(1)}, bf16[128,128]{1,0:T(8,128)(2,1)S(1)}, u32[]{:S(2)}, u32[]{:S(2)}) %collective-permute-start.13) | collective-permute-done | bytes 32800 | tf_op jit(solution)/shard_map/ppermute | solution.py:291
  57.0 1.5 %collective-permute-start.19 = (bf16[512,128]{1,0:T(8,128)(2,1)S(1)}, bf16[512,128]{1,0:T(8,128)(2,1)S(1)}, u32[]{:S(2)}, u32[]{:S(2)}) collective-permute-start(bf16[512,128]{1,0:T(8,128)(2,1)S(1)} %get-tuple-element.64), channel_id=1, source_target_pairs={{0,6},{1,7},{2,4},{3,5},{4,2},{5,3},{6,0},{7,1},{8,14},{9,15},{10,... | collective-permute-start | bytes 393224 | tf_op jit(solution)/shard_map/ppermute | solution.py:291
  59.1 1.5 %collective-permute-start.17 = (bf16[512,128]{1,0:T(8,128)(2,1)S(1)}, bf16[512,128]{1,0:T(8,128)(2,1)S(1)}, u32[]{:S(2)}, u32[]{:S(2)}) collective-permute-start(bf16[512,128]{1,0:T(8,128)(2,1)S(1)} %get-tuple-element.64), channel_id=1, source_target_pairs={{0,2},{1,3},{2,0},{3,1},{4,6},{5,7},{6,4},{7,5},{8,10},{9,11},{10,... | collective-permute-start | bytes 393224 | tf_op jit(solution)/shard_map/ppermute | solution.py:291
  60.6 3.8 %collective-permute-done.19.refs_7_ = bf16[512,128]{1,0:T(8,128)(2,1)S(1)} collective-permute-done((bf16[512,128]{1,0:T(8,128)(2,1)S(1)}, bf16[512,128]{1,0:T(8,128)(2,1)S(1)}, u32[]{:S(2)}, u32[]{:S(2)}) %collective-permute-start.19) | collective-permute-done | bytes 131104 | tf_op jit(solution)/shard_map/ppermute | solution.py:291
  68.3 3.6 %collective-permute-start.22 = (bf16[128,128]{1,0:T(8,128)(2,1)S(1)}, bf16[128,128]{1,0:T(8,128)(2,1)S(1)}, u32[]{:S(2)}, u32[]{:S(2)}) collective-permute-start(bf16[128,128]{1,0:T(8,128)(2,1)S(1)} %get-tuple-element.69), channel_id=1, source_target_pairs={{0,16},{1,17},{2,18},{3,19},{4,20},{5,21},{6,22},{7,23},{8,24},{9,... | collective-permute-start | bytes 98312 | tf_op jit(solution)/shard_map/ppermute | solution.py:291
  72.1 2.1 %collective-permute-done.21.refs_1_ = bf16[128,128]{1,0:T(8,128)(2,1)S(1)} collective-permute-done((bf16[128,128]{1,0:T(8,128)(2,1)S(1)}, bf16[128,128]{1,0:T(8,128)(2,1)S(1)}, u32[]{:S(2)}, u32[]{:S(2)}) %collective-permute-start.21) | collective-permute-done | bytes 32800 | tf_op jit(solution)/shard_map/ppermute | solution.py:291
  77.3 1.9 %collective-permute-start.25 = (bf16[128,128]{1,0:T(8,128)(2,1)S(1)}, bf16[128,128]{1,0:T(8,128)(2,1)S(1)}, u32[]{:S(2)}, u32[]{:S(2)}) collective-permute-start(bf16[128,128]{1,0:T(8,128)(2,1)S(1)} %get-tuple-element.71.refs_0_), channel_id=1, source_target_pairs={{0,16},{1,17},{2,18},{3,19},{4,20},{5,21},{6,22},{7,23},{8,24},{9,... | collective-permute-start | bytes 98312 | tf_op jit(solution)/shard_map/ppermute | solution.py:291
  80.3 2.0 %collective-permute-done.26.refs_3_ = bf16[128,128]{1,0:T(8,128)(2,1)S(1)} collective-permute-done((bf16[128,128]{1,0:T(8,128)(2,1)S(1)}, bf16[128,128]{1,0:T(8,128)(2,1)S(1)}, u32[]{:S(2)}, u32[]{:S(2)}) %collective-permute-start.26) | collective-permute-done | bytes 32800 | tf_op jit(solution)/shard_map/ppermute | solution.py:291
  83.1 1.6 %collective-permute-start.29 = (bf16[512,128]{1,0:T(8,128)(2,1)S(1)}, bf16[512,128]{1,0:T(8,128)(2,1)S(1)}, u32[]{:S(2)}, u32[]{:S(2)}) collective-permute-start(bf16[512,128]{1,0:T(8,128)(2,1)S(1)} %shard_map.97.refs_2_), channel_id=1, source_target_pairs={{0,6},{1,7},{2,4},{3,5},{4,2},{5,3},{6,0},{7,1},{8,14},{9,15},{10,... | collective-permute-start | bytes 393224 | tf_op jit(solution)/shard_map/ppermute | solution.py:291
  86.7 2.4 %collective-permute-done.29.refs_5_ = bf16[512,128]{1,0:T(8,128)(2,1)S(1)} collective-permute-done((bf16[512,128]{1,0:T(8,128)(2,1)S(1)}, bf16[512,128]{1,0:T(8,128)(2,1)S(1)}, u32[]{:S(2)}, u32[]{:S(2)}) %collective-permute-start.29) | collective-permute-done | bytes 131104 | tf_op jit(solution)/shard_map/ppermute | solution.py:291
  91.8 6.0 %shard_map.98 = (bf16[128,1024]{1,0:T(8,128)(2,1)S(1)}, f32[128,1024]{1,0:T(8,128)S(1)}, bf16[128,1024]{1,0:T(8,128)(2,1)S(1)}) custom-call(s32[4096]{0:T(1024)S(1)} %fusion.10.place, bf16[1024,128]{1,0:T(8,128)(2,1)S(1)} %get-tuple-element.48.forward, bf16[4096,1024]{1,0:T(8,128)(2,1)S(1)} %get-tuple-element.42.coupling, ...), custom_call_target="tpu_custom_call" | custom-call | flops 1610612736 | bytes 14958592 | tf_op jit(solution)/shard_map/pallas_call | solution.py:26
  100.7 7.2 %collective-permute-done.36.refs_2_ = bf16[128,1024]{1,0:T(8,128)(2,1)S(1)} collective-permute-done((bf16[128,1024]{1,0:T(8,128)(2,1)S(1)}, bf16[128,1024]{1,0:T(8,128)(2,1)S(1)}, u32[]{:S(2)}, u32[]{:S(2)}) %collective-permute-start.36) | collective-permute-done | bytes 262176 | tf_op jit(solution)/shard_map/ppermute | solution.py:291
  (77 shorter events, 33.1 us)
Async XLA Ops:
  0.6 12.1 %collective-permute-start.1 = (bf16[1024,128]{1,0:T(8,128)(2,1)}, bf16[1024,128]{1,0:T(8,128)(2,1)S(1)}, u32[]{:S(2)}, u32[]{:S(2)}) collective-permute-start(bf16[1024,128]{1,0:T(8,128)(2,1)} %bitcast.43), channel_id=1, source_target_pairs={{0,2},{1,3},{2,0},{3,1},{4,6},{5,7},{6,4},{7,5},{8,10},{9,11},{10,... | collective-permute-start | bytes 786440 | tf_op jit(solution)/shard_map/ppermute | solution.py:291
  3.7 9.8 %collective-permute-start = (bf16[1024,128]{1,0:T(8,128)(2,1)}, bf16[1024,128]{1,0:T(8,128)(2,1)S(1)}, u32[]{:S(2)}, u32[]{:S(2)}) collective-permute-start(bf16[1024,128]{1,0:T(8,128)(2,1)} %bitcast.44), channel_id=1, source_target_pairs={{0,1},{1,0},{2,3},{3,2},{4,5},{5,4},{6,7},{7,6},{8,9},{9,8},{10,11... | collective-permute-start | bytes 786440 | tf_op jit(solution)/shard_map/ppermute | solution.py:291
  24.0 5.6 %collective-permute-start.7 = (bf16[512,128]{1,0:T(8,128)(2,1)S(1)}, bf16[512,128]{1,0:T(8,128)(2,1)S(1)}, u32[]{:S(2)}, u32[]{:S(2)}) collective-permute-start(bf16[512,128]{1,0:T(8,128)(2,1)S(1)} %get-tuple-element.56), channel_id=1, source_target_pairs={{0,2},{1,3},{2,0},{3,1},{4,6},{5,7},{6,4},{7,5},{8,10},{9,11},{10,... | collective-permute-start | bytes 393224 | tf_op jit(solution)/shard_map/ppermute | solution.py:291
  24.2 6.0 %collective-permute-start.8 = (bf16[512,128]{1,0:T(8,128)(2,1)S(1)}, bf16[512,128]{1,0:T(8,128)(2,1)S(1)}, u32[]{:S(2)}, u32[]{:S(2)}) collective-permute-start(bf16[512,128]{1,0:T(8,128)(2,1)S(1)} %get-tuple-element.57), channel_id=1, source_target_pairs={{0,4},{1,5},{2,6},{3,7},{4,0},{5,1},{6,2},{7,3},{8,12},{9,13},{10,... | collective-permute-start | bytes 393224 | tf_op jit(solution)/shard_map/ppermute | solution.py:291
  26.1 7.5 %collective-permute-start.9 = (bf16[512,128]{1,0:T(8,128)(2,1)S(1)}, bf16[512,128]{1,0:T(8,128)(2,1)S(1)}, u32[]{:S(2)}, u32[]{:S(2)}) collective-permute-start(bf16[512,128]{1,0:T(8,128)(2,1)S(1)} %get-tuple-element.58), channel_id=1, source_target_pairs={{0,6},{1,7},{2,4},{3,5},{4,2},{5,3},{6,0},{7,1},{8,14},{9,15},{10,... | collective-permute-start | bytes 393224 | tf_op jit(solution)/shard_map/ppermute | solution.py:291
  33.7 7.7 %collective-permute-start.10 = (bf16[128,128]{1,0:T(8,128)(2,1)S(1)}, bf16[128,128]{1,0:T(8,128)(2,1)S(1)}, u32[]{:S(2)}, u32[]{:S(2)}) collective-permute-start(bf16[128,128]{1,0:T(8,128)(2,1)S(1)} %get-tuple-element.60), channel_id=1, source_target_pairs={{0,8},{1,9},{2,10},{3,11},{4,12},{5,13},{6,14},{7,15},{8,16},{9,17... | collective-permute-start | bytes 98312 | tf_op jit(solution)/shard_map/ppermute | solution.py:291
  35.4 19.9 %collective-permute-start.4 = (bf16[128,1024]{1,0:T(8,128)(2,1)S(1)}, bf16[128,1024]{1,0:T(8,128)(2,1)S(1)}, u32[]{:S(2)}, u32[]{:S(2)}) collective-permute-start(bf16[128,1024]{1,0:T(8,128)(2,1)S(1)} %get-tuple-element.51), channel_id=1, source_target_pairs={{0,4},{1,5},{2,6},{3,7},{4,0},{5,1},{6,2},{7,3},{8,12},{9,13},{10,... | collective-permute-start | bytes 786440 | tf_op jit(solution)/shard_map/ppermute | solution.py:291
  36.8 18.4 %collective-permute-start.3 = (bf16[128,1024]{1,0:T(8,128)(2,1)S(1)}, bf16[128,1024]{1,0:T(8,128)(2,1)S(1)}, u32[]{:S(2)}, u32[]{:S(2)}) collective-permute-start(bf16[128,1024]{1,0:T(8,128)(2,1)S(1)} %get-tuple-element.50), channel_id=1, source_target_pairs={{0,2},{1,3},{2,0},{3,1},{4,6},{5,7},{6,4},{7,5},{8,10},{9,11},{10,... | collective-permute-start | bytes 786440 | tf_op jit(solution)/shard_map/ppermute | solution.py:291
  37.4 17.9 %collective-permute-start.5 = (bf16[128,1024]{1,0:T(8,128)(2,1)S(1)}, bf16[128,1024]{1,0:T(8,128)(2,1)S(1)}, u32[]{:S(2)}, u32[]{:S(2)}) collective-permute-start(bf16[128,1024]{1,0:T(8,128)(2,1)S(1)} %get-tuple-element.52), channel_id=1, source_target_pairs={{0,6},{1,7},{2,4},{3,5},{4,2},{5,3},{6,0},{7,1},{8,14},{9,15},{10,... | collective-permute-start | bytes 786440 | tf_op jit(solution)/shard_map/ppermute | solution.py:291
  38.9 4.8 %collective-permute-start.11 = (bf16[128,128]{1,0:T(8,128)(2,1)S(1)}, bf16[128,128]{1,0:T(8,128)(2,1)S(1)}, u32[]{:S(2)}, u32[]{:S(2)}) collective-permute-start(bf16[128,128]{1,0:T(8,128)(2,1)S(1)} %get-tuple-element.61), channel_id=1, source_target_pairs={{0,16},{1,17},{2,18},{3,19},{4,20},{5,21},{6,22},{7,23},{8,24},{9,... | collective-permute-start | bytes 98312 | tf_op jit(solution)/shard_map/ppermute | solution.py:291
  45.4 5.9 %collective-permute-start.15 = (bf16[128,128]{1,0:T(8,128)(2,1)S(1)}, bf16[128,128]{1,0:T(8,128)(2,1)S(1)}, u32[]{:S(2)}, u32[]{:S(2)}) collective-permute-start(bf16[128,128]{1,0:T(8,128)(2,1)S(1)} %shard_map.91.refs_0_), channel_id=1, source_target_pairs={{0,8},{1,9},{2,10},{3,11},{4,12},{5,13},{6,14},{7,15},{8,16},{9,17... | collective-permute-start | bytes 98312 | tf_op jit(solution)/shard_map/ppermute | solution.py:291
  45.6 6.8 %collective-permute-start.14 = (bf16[128,128]{1,0:T(8,128)(2,1)S(1)}, bf16[128,128]{1,0:T(8,128)(2,1)S(1)}, u32[]{:S(2)}, u32[]{:S(2)}) collective-permute-start(bf16[128,128]{1,0:T(8,128)(2,1)S(1)} %shard_map.91.refs_0_), channel_id=1, source_target_pairs={{0,16},{1,17},{2,18},{3,19},{4,20},{5,21},{6,22},{7,23},{8,24},{9,... | collective-permute-start | bytes 98312 | tf_op jit(solution)/shard_map/ppermute | solution.py:291
  57.0 7.3 %collective-permute-start.19 = (bf16[512,128]{1,0:T(8,128)(2,1)S(1)}, bf16[512,128]{1,0:T(8,128)(2,1)S(1)}, u32[]{:S(2)}, u32[]{:S(2)}) collective-permute-start(bf16[512,128]{1,0:T(8,128)(2,1)S(1)} %get-tuple-element.64), channel_id=1, source_target_pairs={{0,6},{1,7},{2,4},{3,5},{4,2},{5,3},{6,0},{7,1},{8,14},{9,15},{10,... | collective-permute-start | bytes 393224 | tf_op jit(solution)/shard_map/ppermute | solution.py:291
  58.5 6.9 %collective-permute-start.18 = (bf16[512,128]{1,0:T(8,128)(2,1)S(1)}, bf16[512,128]{1,0:T(8,128)(2,1)S(1)}, u32[]{:S(2)}, u32[]{:S(2)}) collective-permute-start(bf16[512,128]{1,0:T(8,128)(2,1)S(1)} %get-tuple-element.64), channel_id=1, source_target_pairs={{0,4},{1,5},{2,6},{3,7},{4,0},{5,1},{6,2},{7,3},{8,12},{9,13},{10,... | collective-permute-start | bytes 393224 | tf_op jit(solution)/shard_map/ppermute | solution.py:291
  59.1 7.3 %collective-permute-start.17 = (bf16[512,128]{1,0:T(8,128)(2,1)S(1)}, bf16[512,128]{1,0:T(8,128)(2,1)S(1)}, u32[]{:S(2)}, u32[]{:S(2)}) collective-permute-start(bf16[512,128]{1,0:T(8,128)(2,1)S(1)} %get-tuple-element.64), channel_id=1, source_target_pairs={{0,2},{1,3},{2,0},{3,1},{4,6},{5,7},{6,4},{7,5},{8,10},{9,11},{10,... | collective-permute-start | bytes 393224 | tf_op jit(solution)/shard_map/ppermute | solution.py:291
  68.3 6.0 %collective-permute-start.21 = (bf16[128,128]{1,0:T(8,128)(2,1)S(1)}, bf16[128,128]{1,0:T(8,128)(2,1)S(1)}, u32[]{:S(2)}, u32[]{:S(2)}) collective-permute-start(bf16[128,128]{1,0:T(8,128)(2,1)S(1)} %get-tuple-element.68), channel_id=1, source_target_pairs={{0,8},{1,9},{2,10},{3,11},{4,12},{5,13},{6,14},{7,15},{8,16},{9,17... | collective-permute-start | bytes 98312 | tf_op jit(solution)/shard_map/ppermute | solution.py:291
  68.3 6.5 %collective-permute-start.22 = (bf16[128,128]{1,0:T(8,128)(2,1)S(1)}, bf16[128,128]{1,0:T(8,128)(2,1)S(1)}, u32[]{:S(2)}, u32[]{:S(2)}) collective-permute-start(bf16[128,128]{1,0:T(8,128)(2,1)S(1)} %get-tuple-element.69), channel_id=1, source_target_pairs={{0,16},{1,17},{2,18},{3,19},{4,20},{5,21},{6,22},{7,23},{8,24},{9,... | collective-permute-start | bytes 98312 | tf_op jit(solution)/shard_map/ppermute | solution.py:291
  76.4 5.8 %collective-permute-start.26 = (bf16[128,128]{1,0:T(8,128)(2,1)S(1)}, bf16[128,128]{1,0:T(8,128)(2,1)S(1)}, u32[]{:S(2)}, u32[]{:S(2)}) collective-permute-start(bf16[128,128]{1,0:T(8,128)(2,1)S(1)} %get-tuple-element.71.refs_0_), channel_id=1, source_target_pairs={{0,8},{1,9},{2,10},{3,11},{4,12},{5,13},{6,14},{7,15},{8,16},{9,17... | collective-permute-start | bytes 98312 | tf_op jit(solution)/shard_map/ppermute | solution.py:291
  77.3 5.5 %collective-permute-start.25 = (bf16[128,128]{1,0:T(8,128)(2,1)S(1)}, bf16[128,128]{1,0:T(8,128)(2,1)S(1)}, u32[]{:S(2)}, u32[]{:S(2)}) collective-permute-start(bf16[128,128]{1,0:T(8,128)(2,1)S(1)} %get-tuple-element.71.refs_0_), channel_id=1, source_target_pairs={{0,16},{1,17},{2,18},{3,19},{4,20},{5,21},{6,22},{7,23},{8,24},{9,... | collective-permute-start | bytes 98312 | tf_op jit(solution)/shard_map/ppermute | solution.py:291
  79.2 4.0 %collective-permute-start.24 = (bf16[128,128]{1,0:T(8,128)(2,1)S(1)}, bf16[128,128]{1,0:T(8,128)(2,1)S(1)}, u32[]{:S(2)}, u32[]{:S(2)}) collective-permute-start(bf16[128,128]{1,0:T(8,128)(2,1)S(1)} %get-tuple-element.71.refs_0_), channel_id=1, source_target_pairs={{0,24},{1,25},{2,26},{3,27},{4,28},{5,29},{6,30},{7,31},{8,0},{9,1... | collective-permute-start | bytes 98312 | tf_op jit(solution)/shard_map/ppermute | solution.py:291
  83.1 6.0 %collective-permute-start.29 = (bf16[512,128]{1,0:T(8,128)(2,1)S(1)}, bf16[512,128]{1,0:T(8,128)(2,1)S(1)}, u32[]{:S(2)}, u32[]{:S(2)}) collective-permute-start(bf16[512,128]{1,0:T(8,128)(2,1)S(1)} %shard_map.97.refs_2_), channel_id=1, source_target_pairs={{0,6},{1,7},{2,4},{3,5},{4,2},{5,3},{6,0},{7,1},{8,14},{9,15},{10,... | collective-permute-start | bytes 393224 | tf_op jit(solution)/shard_map/ppermute | solution.py:291
  84.7 5.0 %collective-permute-start.28 = (bf16[512,128]{1,0:T(8,128)(2,1)S(1)}, bf16[512,128]{1,0:T(8,128)(2,1)S(1)}, u32[]{:S(2)}, u32[]{:S(2)}) collective-permute-start(bf16[512,128]{1,0:T(8,128)(2,1)S(1)} %shard_map.97.refs_2_), channel_id=1, source_target_pairs={{0,4},{1,5},{2,6},{3,7},{4,0},{5,1},{6,2},{7,3},{8,12},{9,13},{10,... | collective-permute-start | bytes 393224 | tf_op jit(solution)/shard_map/ppermute | solution.py:291
  85.2 5.2 %collective-permute-start.27 = (bf16[512,128]{1,0:T(8,128)(2,1)S(1)}, bf16[512,128]{1,0:T(8,128)(2,1)S(1)}, u32[]{:S(2)}, u32[]{:S(2)}) collective-permute-start(bf16[512,128]{1,0:T(8,128)(2,1)S(1)} %shard_map.97.refs_2_), channel_id=1, source_target_pairs={{0,2},{1,3},{2,0},{3,1},{4,6},{5,7},{6,4},{7,5},{8,10},{9,11},{10,... | collective-permute-start | bytes 393224 | tf_op jit(solution)/shard_map/ppermute | solution.py:291
  99.5 8.4 %collective-permute-start.36 = (bf16[128,1024]{1,0:T(8,128)(2,1)S(1)}, bf16[128,1024]{1,0:T(8,128)(2,1)S(1)}, u32[]{:S(2)}, u32[]{:S(2)}) collective-permute-start(bf16[128,1024]{1,0:T(8,128)(2,1)S(1)} %shard_map.100), channel_id=1, source_target_pairs={{0,2},{1,3},{2,0},{3,1},{4,6},{5,7},{6,4},{7,5},{8,10},{9,11},{10,... | collective-permute-start | bytes 786440 | tf_op jit(solution)/shard_map/ppermute | solution.py:291
  (17 other events, 69.6 us)

commit v3 on v2

--- a/solution.py
+++ b/solution.py
@@ -22,6 +22,10 @@
     moved += sum(o.size * o.dtype.itemsize for o in outs)
     specs = [
         ANY if k in apart else SM if a.dtype == jnp.int32 else VM for k, a in enumerate(operands)
+    ]
+    operands = [
+        pltpu.with_memory_space_constraint(a, pltpu.HBM) if k in apart and a.size > 100000 else a
+        for k, a in enumerate(operands)
     ]
     return pl.pallas_call(
         body,
@@ -34,15 +38,16 @@
     )(*operands)
 
 
-def load_kernel(section, parts, groups, block, column, factor, coupling, separator, *refs):
-    wide, tall, cut, sems = refs[:section], refs[section], refs[section + 1 : -1], refs[-1]
-    width, size = factor.shape[0], separator.shape[0]
+def columns_copy(factor, index, k, target, sem):
+    width = target.shape[1]
+    start = pl.multiple_of(index[k] * width, width)
+    return pltpu.make_async_copy(factor.at[:, pl.ds(start, width)], target, sem)
+
+
+def load_kernel(count, parts, groups, block, column, factor, separator, *refs):
+    wide, cut, sems = refs[:count], refs[count:-1], refs[-1]
+    size = separator.shape[0]
     copies = []
-    for k in range(section):
-        start = pl.multiple_of(block[k] * width, width)
-        copies.append(
-            pltpu.make_async_copy(factor.at[:, pl.ds(start, width)], wide[k], sems.at[k])
-        )
     for k in range(parts):
         for g in range(groups):
             start = pl.multiple_of(column[k * groups + g] * size, size)
@@ -53,43 +58,68 @@
                     sems.at[len(copies)],
                 )
             )
-    copies.append(pltpu.make_async_copy(coupling, tall, sems.at[len(copies)]))
+    for k in range(count):
+        copies.append(columns_copy(factor, block, k, wide[k], sems.at[len(copies)]))
     for copy in copies:
         copy.start()
     for copy in copies:
         copy.wait()
 
 
-def near_kernel(count, *refs):
-    blocks, pieces, partial = refs[:count], refs[count : 2 * count], refs[-1]
+def near_kernel(count, far, block, factor, coupling, *refs):
+    blocks, pieces = refs[:count], refs[count : 2 * count]
+    partial, tall, wide, sems = refs[2 * count], refs[2 * count + 1], refs[2 * count + 2 : -1], refs[-1]
+    copies = [
+        columns_copy(factor, block, count + k, wide[k], sems.at[k]) for k in range(far)
+    ]
+    copies.append(
+        pltpu.make_async_copy(coupling.at[pl.ds(0, tall.shape[0]), :], tall, sems.at[far])
+    )
+    for copy in copies:
+        copy.start()
     total = None
     for k in range(count):
         term = jnp.dot(blocks[k][...], pieces[k][...], preferred_element_type=F32)
         total = term if total is None else total + term
     partial[...] = total
+    for copy in copies:
+        copy.wait()
 
 
 def chunk_of(rows):
     return 256 if rows % 256 == 0 else rows
 
 
-def update_kernel(groups, far, place, partial, coupling, *refs):
+def update_kernel(groups, far, place_far, coupling, partial, upper, *refs):
     blocks, pieces = refs[:far], refs[far : 2 * far]
-    forward, own, sent = refs[2 * far], refs[2 * far + 1], refs[2 * far + 2 : -3]
-    placed, held = refs[-3], refs[-2:]
+    forward, lower, own = refs[2 * far : 2 * far + 3]
+    sent = refs[2 * far + 3 : -5]
+    place, sems, placed, held = refs[-5], refs[-4], refs[-3], refs[-2:]
     order = placed.shape[0] - 8
-    borders = coupling.shape[0]
-    step = chunk_of(borders)
-    count = borders // step
+    split = upper.shape[0]
+    step = chunk_of(split)
+    count = (split + lower.shape[0]) // step
+    index_copy = pltpu.make_async_copy(place_far, place, sems.at[0])
+    lower_copy = pltpu.make_async_copy(
+        coupling.at[pl.ds(split, lower.shape[0]), :], lower, sems.at[1]
+    )
+    index_copy.start()
+    lower_copy.start()
+    placed[...] = jnp.zeros_like(placed)
     total = partial[...]
     for k in range(far):
         total = total + jnp.dot(blocks[k][...], pieces[k][...], preferred_element_type=F32)
     forward[...] = total.astype(BF16)
-    placed[...] = jnp.zeros_like(placed)
+    index_copy.wait()
 
     def multiply(k):
+        first = k * step
+        if first == split:
+            lower_copy.wait()
+        source = upper if first < split else lower
+        first = first if first < split else first - split
         held[k % 2][...] = jnp.dot(
-            coupling[k * step : (k + 1) * step, :], forward[...], preferred_element_type=F32
+            source[first : first + step, :], forward[...], preferred_element_type=F32
         )
 
     def scatter(k):
@@ -190,28 +220,34 @@
         outs[h][...] = total.astype(outs[h].dtype)
 
 
-def border_kernel(blocks, far, place, forward, coupling, *refs):
+def border_kernel(blocks, far, place_far, forward, upper, lower, *refs):
     wide, pieces = refs[:far], refs[far : far + blocks]
-    corrected, sent = refs[far + blocks], refs[far + blocks + 1 : -4]
-    table, sums, held = refs[-4], refs[-3], refs[-2:]
+    corrected, sent = refs[far + blocks], refs[far + blocks + 1 : -6]
+    place, sem, table, sums, held = refs[-6], refs[-5], refs[-4], refs[-3], refs[-2:]
+    index_copy = pltpu.make_async_copy(place_far, place, sem.at[0])
+    index_copy.start()
     rows = pieces[0].shape[0]
     order = blocks * rows
-    borders = coupling.shape[0]
-    step = chunk_of(borders)
-    count = borders // step
+    split = upper.shape[0]
+    step = chunk_of(split)
+    count = (split + lower.shape[0]) // step
     for k in range(blocks):
         table[k * rows : (k + 1) * rows, :] = pieces[k][...].astype(F32)
     table[order : order + 8, :] = jnp.zeros((8, table.shape[1]), F32)
     sums[...] = forward[...].astype(F32).T
+    index_copy.wait()
 
     def gather(k):
         for t in range(step):
             held[k % 2][t : t + 1, :] = table[pl.ds(place[k * step + t], 1), :]
 
     def multiply(k):
+        first = k * step
+        source = upper if first < split else lower
+        first = first if first < split else first - split
         sums[...] -= lax.dot_general(
             held[k % 2][...].astype(BF16),
-            coupling[k * step : (k + 1) * step, :],
+            source[first : first + step, :],
             FIRST,
             preferred_element_type=F32,
         )
@@ -328,16 +364,13 @@
     ).astype(jnp.int32)
     loads = parts if direct else 0
     loaded = kernel_call(
-        functools.partial(load_kernel, len(section), loads, len(groups)),
-        [like((rows, rows), BF16)] * len(section)
-        + [like(coupling.shape, BF16)]
-        + [like((own_rows, wide), BF16)] * loads,
-        [block, column, factor, coupling, separator_factor],
-        scratch=[pltpu.SemaphoreType.DMA((len(section) + loads * len(groups) + 1,))],
-        vmem=33,
-        apart=(2, 3, 4),
-    )
-    wide_blocks, tall, cut = loaded[: len(section)], loaded[len(section)], loaded[-parts:]
+        functools.partial(load_kernel, nc, loads, len(groups)),
+        [like((rows, rows), BF16)] * nc + [like((own_rows, wide), BF16)] * loads,
+        [block, column, factor, separator_factor],
+        scratch=[pltpu.SemaphoreType.DMA((nc + loads * len(groups),))],
+        apart=(2, 3),
+    )
+    near_blocks, cut = loaded[:nc], loaded[nc:]
     if not direct:
         cut = [
             jnp.concatenate(
@@ -364,22 +397,36 @@
 
     half = order // nc
     far_count = len(section) - nc
-    near = kernel_call(
-        functools.partial(near_kernel, nc),
-        [like((rows, columns), F32)],
-        [*wide_blocks[:nc], *pieces[:nc]],
+    split = borders // 2
+    loaded = kernel_call(
+        functools.partial(near_kernel, nc, far_count),
+        [like((rows, columns), F32), like((split, rows), BF16)]
+        + [like((rows, rows), BF16)] * far_count,
+        [block, factor, coupling, *near_blocks, *pieces[:nc]],
+        scratch=[pltpu.SemaphoreType.DMA((far_count + 1,))],
         flops=2 * rows * rows * nc * columns,
-    )[0]
+        apart=(1, 2),
+    )
+    near, upper, far_blocks = loaded[0], loaded[1], loaded[2:]
     outs = kernel_call(
         functools.partial(update_kernel, nc, far_count),
-        [like((rows, columns), BF16), like((half, columns), F32)]
+        [
+            like((rows, columns), BF16),
+            like((borders - split, rows), BF16),
+            like((half, columns), F32),
+        ]
         + [like((half, columns), BF16)] * (nc - 1),
-        [place, near, tall, *wide_blocks[nc:], *pieces[nc:]],
-        scratch=[pltpu.VMEM((order + 8, columns), F32)]
-        + [pltpu.VMEM((chunk_of(borders), columns), F32)] * 2,
+        [place, coupling, near, upper, *far_blocks, *pieces[nc:]],
+        scratch=[
+            pltpu.SMEM(place.shape, jnp.int32),
+            pltpu.SemaphoreType.DMA((2,)),
+            pltpu.VMEM((order + 8, columns), F32),
+        ]
+        + [pltpu.VMEM((chunk_of(split), columns), F32)] * 2,
         flops=2 * (coupling.size + rows * rows * far_count) * columns,
-    )
-    forward, outs = outs[0], outs[1:]
+        apart=(0, 1),
+    )
+    forward, lower, outs = outs[0], outs[1], outs[2:]
     received = [shift(outs[dc], dc=dc) for dc in range(1, nc)]
     size = half // parts
     outs = kernel_call(
@@ -452,10 +499,16 @@
         functools.partial(border_kernel, len(pieces), len(far)),
         [like((columns, rows), BF16)]
         + [like((columns, rows), F32 if dc == 0 else BF16) for dy, dc in far],
-        [place, forward, tall, *wide_blocks[nc:], *pieces],
-        scratch=[pltpu.VMEM((order + 8, columns), F32), pltpu.VMEM((columns, rows), F32)]
-        + [pltpu.VMEM((chunk_of(borders), columns), F32)] * 2,
+        [place, forward, upper, lower, *far_blocks, *pieces],
+        scratch=[
+            pltpu.SMEM(place.shape, jnp.int32),
+            pltpu.SemaphoreType.DMA((1,)),
+            pltpu.VMEM((order + 8, columns), F32),
+            pltpu.VMEM((columns, rows), F32),
+        ]
+        + [pltpu.VMEM((chunk_of(split), columns), F32)] * 2,
         flops=2 * (coupling.size + factor.size * len(far) // len(section)) * columns,
+        apart=(0,),
     )
     corrected, far_parts = outs[0], dict(zip(far, outs[1:]))
     arrived = []
@@ -468,7 +521,7 @@
     outs = kernel_call(
         blocks_kernel,
         [like((columns, rows), F32 if dc == 0 else BF16) for dy, dc in near],
-        [corrected, *wide_blocks[:nc]],
+        [corrected, *near_blocks],
         flops=2 * factor.size * len(near) // len(section) * columns,
     )
     terms = [outs[0]] + [shift(outs[dc], dc=dc) for dc in range(1, nc)]

time: 109 us -> 111 us (1.018)
  waiting for transfers between devices: 42.7 us -> 45.5 us
  local copies, waits for them, and re-layouts: 1.34 us -> 0.13 us
    ppermute x37, waiting for transfers between devices: 42.7 us -> 45.5 us  [shift(): return lax.ppermute(value, AXES, pairs)]
    unnamed x8 -> x6, local copies, waits for them, and re-layouts: 1.24 us -> 0.02 us
  transfers between devices with their start and end apart: 37 -> 37, of which waited for: 26 -> 26; matrix products, arithmetic and copies ran while one was open for 0% -> 0% of each run, Pallas kernels for 8% -> 9%
where the time goes in v3:
time: 111 us; the launch traced here: 110 us
  waiting for transfers between devices  45.5 us (41%)
  starting transfers between devices  38.1 us (34%)
  Pallas kernels  24.9 us (22%)
  between operations  1.6 us (1%)
    ppermute x37, waiting for transfers between devices, shift(): return lax.ppermute(value, AXES, pairs)  45.5 us
    ppermute x37, starting transfers between devices, shift(): return lax.ppermute(value, AXES, pairs)  38.1 us
    pallas_call x16, Pallas kernels, kernel_call(): pl.pallas_call(body, out_shape=list(outs), in_specs=specs, out_specs=[VM]...  24.9 us
  transfers between devices with their start and end apart: 37, of which 26 were waited for; matrix products, arithmetic and copies ran while one was open for 0% of the time, Pallas kernels for 9%

profile of v3, /device:TPU:0, one launch (start us, length us, event | category | flops | bytes accessed | tf_op | source)
XLA Modules:
  0.0 110.4 jit_solution(14797581545168382010)
XLA Ops:
  0.6 3.1 %collective-permute-start.1 = (bf16[1024,128]{1,0:T(8,128)(2,1)}, bf16[1024,128]{1,0:T(8,128)(2,1)S(1)}, u32[]{:S(2)}, u32[]{:S(2)}) collective-permute-start(bf16[1024,128]{1,0:T(8,128)(2,1)} %bitcast.43), channel_id=1, source_target_pairs={{0,2},{1,3},{2,0},{3,1},{4,6},{5,7},{6,4},{7,5},{8,10},{9,11},{10,... | collective-permute-start | bytes 786440 | tf_op jit(solution)/shard_map/ppermute | solution.py:327
  4.7 3.6 %shard_map.86 = (bf16[1024,1024]{1,0:T(8,128)(2,1)S(1)}, bf16[1024,1024]{1,0:T(8,128)(2,1)S(1)}, bf16[128,1024]{1,0:T(8,128)(2,1)S(1)}, bf16[128,1024]{1,0:T(8,1...) custom-call(s32[4]{0:T(128)S(1)} %pad_add_fusion.block, s32[32]{0:T(128)S(1)} %stack.151.column, ...), custom_call_target="tpu_custom_call" | custom-call | bytes 14680208 | tf_op jit(solution)/shard_map/pallas_call | solution.py:30
  8.2 2.0 %collective-permute-done.1.refs_2_ = bf16[1024,128]{1,0:T(8,128)(2,1)S(1)} collective-permute-done((bf16[1024,128]{1,0:T(8,128)(2,1)}, bf16[1024,128]{1,0:T(8,128)(2,1)S(1)}, u32[]{:S(2)}, u32[]{:S(2)}) %collective-permute-start.1) | collective-permute-done | bytes 262176 | tf_op jit(solution)/shard_map/ppermute | solution.py:327
  10.3 5.2 %shard_map.87 = (f32[1024,128]{1,0:T(8,128)S(1)}, bf16[2048,1024]{1,0:T(8,128)(2,1)S(1)}, bf16[1024,1024]{1,0:T(8,128)(2,1)S(1)}, bf16[1024,1024]{1,0:T(8,128)(2,1)S(1)}) custom-call(s32[4]{0:T(128)S(1)} %pad_add_fusion.block, bf16[1024,4096]{1,0:T(8,128)(2,1)} %bitcast.49, bf16[4096,1024]{1,0:T(8,128)(2,1)} %bitcast.46, ...), custom_call_target="tpu_custom_call" | custom-call | flops 536870912 | bytes 30408720 | tf_op jit(solution)/shard_map/pallas_call | solution.py:30
  15.5 7.2 %shard_map.88 = (bf16[1024,128]{1,0:T(8,128)(2,1)S(1)}, bf16[2048,1024]{1,0:T(8,128)(2,1)S(1)}, f32[2048,128]{1,0:T(8,128)S(1)}, bf16[2048,128]{1,0:T(8,128)(2,1)S(1)}) custom-call(s32[4096]{0:T(1024)S(1)} %fusion.10.place_far, bf16[4096,1024]{1,0:T(8,128)(2,1)} %bitcast.47, f32[1024,128]{1,0:T(8,128)S(1)} %get-tuple-element.44.partial, ...), custom_call_target="tpu_custom_call" | custom-call | flops 1610612736 | bytes 23871488 | tf_op jit(solution)/shard_map/pallas_call | solution.py:30
  24.9 1.8 %collective-permute-start.7 = (bf16[512,128]{1,0:T(8,128)(2,1)S(1)}, bf16[512,128]{1,0:T(8,128)(2,1)S(1)}, u32[]{:S(2)}, u32[]{:S(2)}) collective-permute-start(bf16[512,128]{1,0:T(8,128)(2,1)S(1)} %get-tuple-element.60), channel_id=1, source_target_pairs={{0,2},{1,3},{2,0},{3,1},{4,6},{5,7},{6,4},{7,5},{8,10},{9,11},{10,... | collective-permute-start | bytes 393224 | tf_op jit(solution)/shard_map/ppermute | solution.py:327
  28.5 2.3 %collective-permute-done.7.refs_1_ = bf16[512,128]{1,0:T(8,128)(2,1)S(1)} collective-permute-done((bf16[512,128]{1,0:T(8,128)(2,1)S(1)}, bf16[512,128]{1,0:T(8,128)(2,1)S(1)}, u32[]{:S(2)}, u32[]{:S(2)}) %collective-permute-start.7) | collective-permute-done | bytes 131104 | tf_op jit(solution)/shard_map/ppermute | solution.py:327
  30.7 2.3 %collective-permute-done.8.refs_2_ = bf16[512,128]{1,0:T(8,128)(2,1)S(1)} collective-permute-done((bf16[512,128]{1,0:T(8,128)(2,1)S(1)}, bf16[512,128]{1,0:T(8,128)(2,1)S(1)}, u32[]{:S(2)}, u32[]{:S(2)}) %collective-permute-start.8) | collective-permute-done | bytes 131104 | tf_op jit(solution)/shard_map/ppermute | solution.py:327
  34.9 1.8 %collective-permute-start.10 = (bf16[128,128]{1,0:T(8,128)(2,1)S(1)}, bf16[128,128]{1,0:T(8,128)(2,1)S(1)}, u32[]{:S(2)}, u32[]{:S(2)}) collective-permute-start(bf16[128,128]{1,0:T(8,128)(2,1)S(1)} %get-tuple-element.64), channel_id=1, source_target_pairs={{0,8},{1,9},{2,10},{3,11},{4,12},{5,13},{6,14},{7,15},{8,16},{9,17... | collective-permute-start | bytes 98312 | tf_op jit(solution)/shard_map/ppermute | solution.py:327
  40.1 2.6 %collective-permute-start.11 = (bf16[128,128]{1,0:T(8,128)(2,1)S(1)}, bf16[128,128]{1,0:T(8,128)(2,1)S(1)}, u32[]{:S(2)}, u32[]{:S(2)}) collective-permute-start(bf16[128,128]{1,0:T(8,128)(2,1)S(1)} %get-tuple-element.65), channel_id=1, source_target_pairs={{0,16},{1,17},{2,18},{3,19},{4,20},{5,21},{6,22},{7,23},{8,24},{9,... | collective-permute-start | bytes 98312 | tf_op jit(solution)/shard_map/ppermute | solution.py:327
  46.9 3.6 %collective-permute-start.14 = (bf16[128,128]{1,0:T(8,128)(2,1)S(1)}, bf16[128,128]{1,0:T(8,128)(2,1)S(1)}, u32[]{:S(2)}, u32[]{:S(2)}) collective-permute-start(bf16[128,128]{1,0:T(8,128)(2,1)S(1)} %shard_map.91.refs_0_), channel_id=1, source_target_pairs={{0,16},{1,17},{2,18},{3,19},{4,20},{5,21},{6,22},{7,23},{8,24},{9,... | collective-permute-start | bytes 98312 | tf_op jit(solution)/shard_map/ppermute | solution.py:327
  50.5 2.0 %collective-permute-done.15.refs_3_ = bf16[128,128]{1,0:T(8,128)(2,1)S(1)} collective-permute-done((bf16[128,128]{1,0:T(8,128)(2,1)S(1)}, bf16[128,128]{1,0:T(8,128)(2,1)S(1)}, u32[]{:S(2)}, u32[]{:S(2)}) %collective-permute-start.15) | collective-permute-done | bytes 32800 | tf_op jit(solution)/shard_map/ppermute | solution.py:327
  53.9 2.6 %collective-permute-done.13.refs_1_ = bf16[128,128]{1,0:T(8,128)(2,1)S(1)} collective-permute-done((bf16[128,128]{1,0:T(8,128)(2,1)S(1)}, bf16[128,128]{1,0:T(8,128)(2,1)S(1)}, u32[]{:S(2)}, u32[]{:S(2)}) %collective-permute-start.13) | collective-permute-done | bytes 32800 | tf_op jit(solution)/shard_map/ppermute | solution.py:327
  58.3 2.5 %collective-permute-start.19 = (bf16[512,128]{1,0:T(8,128)(2,1)S(1)}, bf16[512,128]{1,0:T(8,128)(2,1)S(1)}, u32[]{:S(2)}, u32[]{:S(2)}) collective-permute-start(bf16[512,128]{1,0:T(8,128)(2,1)S(1)} %get-tuple-element.68), channel_id=1, source_target_pairs={{0,6},{1,7},{2,4},{3,5},{4,2},{5,3},{6,0},{7,1},{8,14},{9,15},{10,... | collective-permute-start | bytes 393224 | tf_op jit(solution)/shard_map/ppermute | solution.py:327
  61.9 3.8 %collective-permute-done.19.refs_7_ = bf16[512,128]{1,0:T(8,128)(2,1)S(1)} collective-permute-done((bf16[512,128]{1,0:T(8,128)(2,1)S(1)}, bf16[512,128]{1,0:T(8,128)(2,1)S(1)}, u32[]{:S(2)}, u32[]{:S(2)}) %collective-permute-start.19) | collective-permute-done | bytes 131104 | tf_op jit(solution)/shard_map/ppermute | solution.py:327
  65.6 2.0 %collective-permute-done.18.refs_6_ = bf16[512,128]{1,0:T(8,128)(2,1)S(1)} collective-permute-done((bf16[512,128]{1,0:T(8,128)(2,1)S(1)}, bf16[512,128]{1,0:T(8,128)(2,1)S(1)}, u32[]{:S(2)}, u32[]{:S(2)}) %collective-permute-start.18) | collective-permute-done | bytes 131104 | tf_op jit(solution)/shard_map/ppermute | solution.py:327
  69.7 3.6 %collective-permute-start.22 = (bf16[128,128]{1,0:T(8,128)(2,1)S(1)}, bf16[128,128]{1,0:T(8,128)(2,1)S(1)}, u32[]{:S(2)}, u32[]{:S(2)}) collective-permute-start(bf16[128,128]{1,0:T(8,128)(2,1)S(1)} %get-tuple-element.73), channel_id=1, source_target_pairs={{0,16},{1,17},{2,18},{3,19},{4,20},{5,21},{6,22},{7,23},{8,24},{9,... | collective-permute-start | bytes 98312 | tf_op jit(solution)/shard_map/ppermute | solution.py:327
  73.5 2.0 %collective-permute-done.21.refs_1_ = bf16[128,128]{1,0:T(8,128)(2,1)S(1)} collective-permute-done((bf16[128,128]{1,0:T(8,128)(2,1)S(1)}, bf16[128,128]{1,0:T(8,128)(2,1)S(1)}, u32[]{:S(2)}, u32[]{:S(2)}) %collective-permute-start.21) | collective-permute-done | bytes 32800 | tf_op jit(solution)/shard_map/ppermute | solution.py:327
  78.6 2.0 %collective-permute-start.25 = (bf16[128,128]{1,0:T(8,128)(2,1)S(1)}, bf16[128,128]{1,0:T(8,128)(2,1)S(1)}, u32[]{:S(2)}, u32[]{:S(2)}) collective-permute-start(bf16[128,128]{1,0:T(8,128)(2,1)S(1)} %get-tuple-element.75.refs_0_), channel_id=1, source_target_pairs={{0,16},{1,17},{2,18},{3,19},{4,20},{5,21},{6,22},{7,23},{8,24},{9,... | collective-permute-start | bytes 98312 | tf_op jit(solution)/shard_map/ppermute | solution.py:327
  81.7 2.0 %collective-permute-done.26.refs_3_ = bf16[128,128]{1,0:T(8,128)(2,1)S(1)} collective-permute-done((bf16[128,128]{1,0:T(8,128)(2,1)S(1)}, bf16[128,128]{1,0:T(8,128)(2,1)S(1)}, u32[]{:S(2)}, u32[]{:S(2)}) %collective-permute-start.26) | collective-permute-done | bytes 32800 | tf_op jit(solution)/shard_map/ppermute | solution.py:327
  84.5 2.5 %collective-permute-start.29 = (bf16[512,128]{1,0:T(8,128)(2,1)S(1)}, bf16[512,128]{1,0:T(8,128)(2,1)S(1)}, u32[]{:S(2)}, u32[]{:S(2)}) collective-permute-start(bf16[512,128]{1,0:T(8,128)(2,1)S(1)} %shard_map.97.refs_2_), channel_id=1, source_target_pairs={{0,6},{1,7},{2,4},{3,5},{4,2},{5,3},{6,0},{7,1},{8,14},{9,15},{10,... | collective-permute-start | bytes 393224 | tf_op jit(solution)/shard_map/ppermute | solution.py:327
  88.1 2.4 %collective-permute-done.29.refs_5_ = bf16[512,128]{1,0:T(8,128)(2,1)S(1)} collective-permute-done((bf16[512,128]{1,0:T(8,128)(2,1)S(1)}, bf16[512,128]{1,0:T(8,128)(2,1)S(1)}, u32[]{:S(2)}, u32[]{:S(2)}) %collective-permute-start.29) | collective-permute-done | bytes 131104 | tf_op jit(solution)/shard_map/ppermute | solution.py:327
  93.8 5.5 %shard_map.98 = (bf16[128,1024]{1,0:T(8,128)(2,1)S(1)}, f32[128,1024]{1,0:T(8,128)S(1)}, bf16[128,1024]{1,0:T(8,128)(2,1)S(1)}) custom-call(s32[4096]{0:T(1024)S(1)} %fusion.10.place_far, bf16[1024,128]{1,0:T(8,128)(2,1)S(1)} %get-tuple-element.51.forward, bf16[2048,1024]{1,0:T(8,128)(2,1)S(1)} %get-tuple-element.45.upper, ...), custom_call_target="tpu_custom_call" | custom-call | flops 1610612736 | bytes 14958592 | tf_op jit(solution)/shard_map/pallas_call | solution.py:30
  101.9 7.5 %collective-permute-done.36.refs_2_ = bf16[128,1024]{1,0:T(8,128)(2,1)S(1)} collective-permute-done((bf16[128,1024]{1,0:T(8,128)(2,1)S(1)}, bf16[128,1024]{1,0:T(8,128)(2,1)S(1)}, u32[]{:S(2)}, u32[]{:S(2)}) %collective-permute-start.36) | collective-permute-done | bytes 262176 | tf_op jit(solution)/shard_map/ppermute | solution.py:327
  (75 shorter events, 33.1 us)
Async XLA Ops:
  0.6 9.6 %collective-permute-start.1 = (bf16[1024,128]{1,0:T(8,128)(2,1)}, bf16[1024,128]{1,0:T(8,128)(2,1)S(1)}, u32[]{:S(2)}, u32[]{:S(2)}) collective-permute-start(bf16[1024,128]{1,0:T(8,128)(2,1)} %bitcast.43), channel_id=1, source_target_pairs={{0,2},{1,3},{2,0},{3,1},{4,6},{5,7},{6,4},{7,5},{8,10},{9,11},{10,... | collective-permute-start | bytes 786440 | tf_op jit(solution)/shard_map/ppermute | solution.py:327
  3.7 6.6 %collective-permute-start = (bf16[1024,128]{1,0:T(8,128)(2,1)}, bf16[1024,128]{1,0:T(8,128)(2,1)S(1)}, u32[]{:S(2)}, u32[]{:S(2)}) collective-permute-start(bf16[1024,128]{1,0:T(8,128)(2,1)} %bitcast.44), channel_id=1, source_target_pairs={{0,1},{1,0},{2,3},{3,2},{4,5},{5,4},{6,7},{7,6},{8,9},{9,8},{10,11... | collective-permute-start | bytes 786440 | tf_op jit(solution)/shard_map/ppermute | solution.py:327
  10.2 5.3 %collective-permute-start.2 = (bf16[1024,128]{1,0:T(8,128)(2,1)S(1)}, bf16[1024,128]{1,0:T(8,128)(2,1)S(1)}, u32[]{:S(2)}, u32[]{:S(2)}) collective-permute-start(bf16[1024,128]{1,0:T(8,128)(2,1)S(1)} %collective-permute-done.1.refs_2_), channel_id=1, source_target_pairs={{0,1},{1,0},{2,3},{3,2},{4,5},{5,4},{6,7},{7,6},{8,9},{9,8},{10,11... | collective-permute-start | bytes 786440 | tf_op jit(solution)/shard_map/ppermute | solution.py:327
  24.9 5.8 %collective-permute-start.7 = (bf16[512,128]{1,0:T(8,128)(2,1)S(1)}, bf16[512,128]{1,0:T(8,128)(2,1)S(1)}, u32[]{:S(2)}, u32[]{:S(2)}) collective-permute-start(bf16[512,128]{1,0:T(8,128)(2,1)S(1)} %get-tuple-element.60), channel_id=1, source_target_pairs={{0,2},{1,3},{2,0},{3,1},{4,6},{5,7},{6,4},{7,5},{8,10},{9,11},{10,... | collective-permute-start | bytes 393224 | tf_op jit(solution)/shard_map/ppermute | solution.py:327
  26.7 6.4 %collective-permute-start.8 = (bf16[512,128]{1,0:T(8,128)(2,1)S(1)}, bf16[512,128]{1,0:T(8,128)(2,1)S(1)}, u32[]{:S(2)}, u32[]{:S(2)}) collective-permute-start(bf16[512,128]{1,0:T(8,128)(2,1)S(1)} %get-tuple-element.61), channel_id=1, source_target_pairs={{0,4},{1,5},{2,6},{3,7},{4,0},{5,1},{6,2},{7,3},{8,12},{9,13},{10,... | collective-permute-start | bytes 393224 | tf_op jit(solution)/shard_map/ppermute | solution.py:327
  28.2 6.6 %collective-permute-start.9 = (bf16[512,128]{1,0:T(8,128)(2,1)S(1)}, bf16[512,128]{1,0:T(8,128)(2,1)S(1)}, u32[]{:S(2)}, u32[]{:S(2)}) collective-permute-start(bf16[512,128]{1,0:T(8,128)(2,1)S(1)} %get-tuple-element.62), channel_id=1, source_target_pairs={{0,6},{1,7},{2,4},{3,5},{4,2},{5,3},{6,0},{7,1},{8,14},{9,15},{10,... | collective-permute-start | bytes 393224 | tf_op jit(solution)/shard_map/ppermute | solution.py:327
  34.9 7.9 %collective-permute-start.10 = (bf16[128,128]{1,0:T(8,128)(2,1)S(1)}, bf16[128,128]{1,0:T(8,128)(2,1)S(1)}, u32[]{:S(2)}, u32[]{:S(2)}) collective-permute-start(bf16[128,128]{1,0:T(8,128)(2,1)S(1)} %get-tuple-element.64), channel_id=1, source_target_pairs={{0,8},{1,9},{2,10},{3,11},{4,12},{5,13},{6,14},{7,15},{8,16},{9,17... | collective-permute-start | bytes 98312 | tf_op jit(solution)/shard_map/ppermute | solution.py:327
  36.6 19.9 %collective-permute-start.4 = (bf16[128,1024]{1,0:T(8,128)(2,1)S(1)}, bf16[128,1024]{1,0:T(8,128)(2,1)S(1)}, u32[]{:S(2)}, u32[]{:S(2)}) collective-permute-start(bf16[128,1024]{1,0:T(8,128)(2,1)S(1)} %get-tuple-element.55), channel_id=1, source_target_pairs={{0,4},{1,5},{2,6},{3,7},{4,0},{5,1},{6,2},{7,3},{8,12},{9,13},{10,... | collective-permute-start | bytes 786440 | tf_op jit(solution)/shard_map/ppermute | solution.py:327
  38.1 18.4 %collective-permute-start.3 = (bf16[128,1024]{1,0:T(8,128)(2,1)S(1)}, bf16[128,1024]{1,0:T(8,128)(2,1)S(1)}, u32[]{:S(2)}, u32[]{:S(2)}) collective-permute-start(bf16[128,1024]{1,0:T(8,128)(2,1)S(1)} %get-tuple-element.54), channel_id=1, source_target_pairs={{0,2},{1,3},{2,0},{3,1},{4,6},{5,7},{6,4},{7,5},{8,10},{9,11},{10,... | collective-permute-start | bytes 786440 | tf_op jit(solution)/shard_map/ppermute | solution.py:327
  39.6 16.9 %collective-permute-start.5 = (bf16[128,1024]{1,0:T(8,128)(2,1)S(1)}, bf16[128,1024]{1,0:T(8,128)(2,1)S(1)}, u32[]{:S(2)}, u32[]{:S(2)}) collective-permute-start(bf16[128,1024]{1,0:T(8,128)(2,1)S(1)} %get-tuple-element.56), channel_id=1, source_target_pairs={{0,6},{1,7},{2,4},{3,5},{4,2},{5,3},{6,0},{7,1},{8,14},{9,15},{10,... | collective-permute-start | bytes 786440 | tf_op jit(solution)/shard_map/ppermute | solution.py:327
  40.1 4.8 %collective-permute-start.11 = (bf16[128,128]{1,0:T(8,128)(2,1)S(1)}, bf16[128,128]{1,0:T(8,128)(2,1)S(1)}, u32[]{:S(2)}, u32[]{:S(2)}) collective-permute-start(bf16[128,128]{1,0:T(8,128)(2,1)S(1)} %get-tuple-element.65), channel_id=1, source_target_pairs={{0,16},{1,17},{2,18},{3,19},{4,20},{5,21},{6,22},{7,23},{8,24},{9,... | collective-permute-start | bytes 98312 | tf_op jit(solution)/shard_map/ppermute | solution.py:327
  46.7 5.9 %collective-permute-start.15 = (bf16[128,128]{1,0:T(8,128)(2,1)S(1)}, bf16[128,128]{1,0:T(8,128)(2,1)S(1)}, u32[]{:S(2)}, u32[]{:S(2)}) collective-permute-start(bf16[128,128]{1,0:T(8,128)(2,1)S(1)} %shard_map.91.refs_0_), channel_id=1, source_target_pairs={{0,8},{1,9},{2,10},{3,11},{4,12},{5,13},{6,14},{7,15},{8,16},{9,17... | collective-permute-start | bytes 98312 | tf_op jit(solution)/shard_map/ppermute | solution.py:327
  46.9 6.9 %collective-permute-start.14 = (bf16[128,128]{1,0:T(8,128)(2,1)S(1)}, bf16[128,128]{1,0:T(8,128)(2,1)S(1)}, u32[]{:S(2)}, u32[]{:S(2)}) collective-permute-start(bf16[128,128]{1,0:T(8,128)(2,1)S(1)} %shard_map.91.refs_0_), channel_id=1, source_target_pairs={{0,16},{1,17},{2,18},{3,19},{4,20},{5,21},{6,22},{7,23},{8,24},{9,... | collective-permute-start | bytes 98312 | tf_op jit(solution)/shard_map/ppermute | solution.py:327
  58.3 7.3 %collective-permute-start.19 = (bf16[512,128]{1,0:T(8,128)(2,1)S(1)}, bf16[512,128]{1,0:T(8,128)(2,1)S(1)}, u32[]{:S(2)}, u32[]{:S(2)}) collective-permute-start(bf16[512,128]{1,0:T(8,128)(2,1)S(1)} %get-tuple-element.68), channel_id=1, source_target_pairs={{0,6},{1,7},{2,4},{3,5},{4,2},{5,3},{6,0},{7,1},{8,14},{9,15},{10,... | collective-permute-start | bytes 393224 | tf_op jit(solution)/shard_map/ppermute | solution.py:327
  60.8 6.9 %collective-permute-start.18 = (bf16[512,128]{1,0:T(8,128)(2,1)S(1)}, bf16[512,128]{1,0:T(8,128)(2,1)S(1)}, u32[]{:S(2)}, u32[]{:S(2)}) collective-permute-start(bf16[512,128]{1,0:T(8,128)(2,1)S(1)} %get-tuple-element.68), channel_id=1, source_target_pairs={{0,4},{1,5},{2,6},{3,7},{4,0},{5,1},{6,2},{7,3},{8,12},{9,13},{10,... | collective-permute-start | bytes 393224 | tf_op jit(solution)/shard_map/ppermute | solution.py:327
  61.4 6.3 %collective-permute-start.17 = (bf16[512,128]{1,0:T(8,128)(2,1)S(1)}, bf16[512,128]{1,0:T(8,128)(2,1)S(1)}, u32[]{:S(2)}, u32[]{:S(2)}) collective-permute-start(bf16[512,128]{1,0:T(8,128)(2,1)S(1)} %get-tuple-element.68), channel_id=1, source_target_pairs={{0,2},{1,3},{2,0},{3,1},{4,6},{5,7},{6,4},{7,5},{8,10},{9,11},{10,... | collective-permute-start | bytes 393224 | tf_op jit(solution)/shard_map/ppermute | solution.py:327
  69.6 5.9 %collective-permute-start.21 = (bf16[128,128]{1,0:T(8,128)(2,1)S(1)}, bf16[128,128]{1,0:T(8,128)(2,1)S(1)}, u32[]{:S(2)}, u32[]{:S(2)}) collective-permute-start(bf16[128,128]{1,0:T(8,128)(2,1)S(1)} %get-tuple-element.72), channel_id=1, source_target_pairs={{0,8},{1,9},{2,10},{3,11},{4,12},{5,13},{6,14},{7,15},{8,16},{9,17... | collective-permute-start | bytes 98312 | tf_op jit(solution)/shard_map/ppermute | solution.py:327
  69.7 6.7 %collective-permute-start.22 = (bf16[128,128]{1,0:T(8,128)(2,1)S(1)}, bf16[128,128]{1,0:T(8,128)(2,1)S(1)}, u32[]{:S(2)}, u32[]{:S(2)}) collective-permute-start(bf16[128,128]{1,0:T(8,128)(2,1)S(1)} %get-tuple-element.73), channel_id=1, source_target_pairs={{0,16},{1,17},{2,18},{3,19},{4,20},{5,21},{6,22},{7,23},{8,24},{9,... | collective-permute-start | bytes 98312 | tf_op jit(solution)/shard_map/ppermute | solution.py:327
  77.9 5.8 %collective-permute-start.26 = (bf16[128,128]{1,0:T(8,128)(2,1)S(1)}, bf16[128,128]{1,0:T(8,128)(2,1)S(1)}, u32[]{:S(2)}, u32[]{:S(2)}) collective-permute-start(bf16[128,128]{1,0:T(8,128)(2,1)S(1)} %get-tuple-element.75.refs_0_), channel_id=1, source_target_pairs={{0,8},{1,9},{2,10},{3,11},{4,12},{5,13},{6,14},{7,15},{8,16},{9,17... | collective-permute-start | bytes 98312 | tf_op jit(solution)/shard_map/ppermute | solution.py:327
  78.6 5.5 %collective-permute-start.25 = (bf16[128,128]{1,0:T(8,128)(2,1)S(1)}, bf16[128,128]{1,0:T(8,128)(2,1)S(1)}, u32[]{:S(2)}, u32[]{:S(2)}) collective-permute-start(bf16[128,128]{1,0:T(8,128)(2,1)S(1)} %get-tuple-element.75.refs_0_), channel_id=1, source_target_pairs={{0,16},{1,17},{2,18},{3,19},{4,20},{5,21},{6,22},{7,23},{8,24},{9,... | collective-permute-start | bytes 98312 | tf_op jit(solution)/shard_map/ppermute | solution.py:327
  84.5 5.9 %collective-permute-start.29 = (bf16[512,128]{1,0:T(8,128)(2,1)S(1)}, bf16[512,128]{1,0:T(8,128)(2,1)S(1)}, u32[]{:S(2)}, u32[]{:S(2)}) collective-permute-start(bf16[512,128]{1,0:T(8,128)(2,1)S(1)} %shard_map.97.refs_2_), channel_id=1, source_target_pairs={{0,6},{1,7},{2,4},{3,5},{4,2},{5,3},{6,0},{7,1},{8,14},{9,15},{10,... | collective-permute-start | bytes 393224 | tf_op jit(solution)/shard_map/ppermute | solution.py:327
  87.0 5.0 %collective-permute-start.28 = (bf16[512,128]{1,0:T(8,128)(2,1)S(1)}, bf16[512,128]{1,0:T(8,128)(2,1)S(1)}, u32[]{:S(2)}, u32[]{:S(2)}) collective-permute-start(bf16[512,128]{1,0:T(8,128)(2,1)S(1)} %shard_map.97.refs_2_), channel_id=1, source_target_pairs={{0,4},{1,5},{2,6},{3,7},{4,0},{5,1},{6,2},{7,3},{8,12},{9,13},{10,... | collective-permute-start | bytes 393224 | tf_op jit(solution)/shard_map/ppermute | solution.py:327
  87.5 5.0 %collective-permute-start.27 = (bf16[512,128]{1,0:T(8,128)(2,1)S(1)}, bf16[512,128]{1,0:T(8,128)(2,1)S(1)}, u32[]{:S(2)}, u32[]{:S(2)}) collective-permute-start(bf16[512,128]{1,0:T(8,128)(2,1)S(1)} %shard_map.97.refs_2_), channel_id=1, source_target_pairs={{0,2},{1,3},{2,0},{3,1},{4,6},{5,7},{6,4},{7,5},{8,10},{9,11},{10,... | collective-permute-start | bytes 393224 | tf_op jit(solution)/shard_map/ppermute | solution.py:327
  101.0 8.4 %collective-permute-start.36 = (bf16[128,1024]{1,0:T(8,128)(2,1)S(1)}, bf16[128,1024]{1,0:T(8,128)(2,1)S(1)}, u32[]{:S(2)}, u32[]{:S(2)}) collective-permute-start(bf16[128,1024]{1,0:T(8,128)(2,1)S(1)} %shard_map.100), channel_id=1, source_target_pairs={{0,2},{1,3},{2,0},{3,1},{4,6},{5,7},{6,4},{7,5},{8,10},{9,11},{10,... | collective-permute-start | bytes 786440 | tf_op jit(solution)/shard_map/ppermute | solution.py:327
  (16 other events, 75.4 us)

commit v4 on v3

--- a/solution.py
+++ b/solution.py
@@ -17,14 +17,15 @@
 ANY = pl.BlockSpec(memory_space=pltpu.HBM)
 
 
-def kernel_call(body, outs, operands, scratch=(), flops=0, vmem=10, apart=()):
+def kernel_call(body, outs, operands, scratch=(), flops=0, vmem=10, name=None, apart=(), vector=()):
     moved = sum(a.size * a.dtype.itemsize for a in operands)
     moved += sum(o.size * o.dtype.itemsize for o in outs)
     specs = [
-        ANY if k in apart else SM if a.dtype == jnp.int32 else VM for k, a in enumerate(operands)
+        ANY if k in apart else SM if a.dtype == jnp.int32 and k not in vector else VM
+        for k, a in enumerate(operands)
     ]
     operands = [
-        pltpu.with_memory_space_constraint(a, pltpu.HBM) if k in apart and a.size > 100000 else a
+        pltpu.with_memory_space_constraint(a, pltpu.HBM) if k in apart and name == "near" else a
         for k, a in enumerate(operands)
     ]
     return pl.pallas_call(
@@ -44,45 +45,79 @@
     return pltpu.make_async_copy(factor.at[:, pl.ds(start, width)], target, sem)
 
 
-def load_kernel(count, parts, groups, block, column, factor, separator, *refs):
-    wide, cut, sems = refs[:count], refs[count:-1], refs[-1]
+def quotient(value, size):
+    return value >> (size.bit_length() - 1) if size & (size - 1) == 0 else value // size
+
+
+def remainder(value, size):
+    return value & (size - 1) if size & (size - 1) == 0 else lax.rem(value, size)
+
+
+def near_kernel(
+    sizes,
+    count,
+    far,
+    parts,
+    groups,
+    block,
+    column,
+    here,
+    factor,
+    separator,
+    border,
+    coupling,
+    rhs,
+    *refs,
+):
+    pieces, refs = refs[: count - 1], refs[count - 1 :]
+    partial, place, tall, refs = refs[0], refs[1], refs[2], refs[3:]
+    wide, cut = refs[: count + far], refs[count + far : -3]
+    rows_held, rhs_held, sems = refs[-3], refs[-2], refs[-1]
+    pieces = (rhs_held, *pieces)
     size = separator.shape[0]
-    copies = []
+    copies = [columns_copy(factor, block, k, wide[k], sems.at[k]) for k in range(count + far)]
+    rest = [pltpu.make_async_copy(border, rows_held, sems.at[count + far])]
     for k in range(parts):
         for g in range(groups):
             start = pl.multiple_of(column[k * groups + g] * size, size)
-            copies.append(
+            rest.append(
                 pltpu.make_async_copy(
                     separator.at[:, pl.ds(start, size)],
                     cut[k].at[:, pl.ds(g * size, size)],
-                    sems.at[len(copies)],
+                    sems.at[count + far + len(rest)],
                 )
             )
-    for k in range(count):
-        copies.append(columns_copy(factor, block, k, wide[k], sems.at[len(copies)]))
-    for copy in copies:
+    early = pltpu.make_async_copy(rhs, rhs_held, sems.at[count + far + len(rest)])
+    late = pltpu.make_async_copy(coupling, tall, sems.at[count + far + len(rest) + 1])
+    for copy in [early] + copies[:count] + rest:
         copy.start()
-    for copy in copies:
-        copy.wait()
-
-
-def near_kernel(count, far, block, factor, coupling, *refs):
-    blocks, pieces = refs[:count], refs[count : 2 * count]
-    partial, tall, wide, sems = refs[2 * count], refs[2 * count + 1], refs[2 * count + 2 : -1], refs[-1]
-    copies = [
-        columns_copy(factor, block, count + k, wide[k], sems.at[k]) for k in range(far)
-    ]
-    copies.append(
-        pltpu.make_async_copy(coupling.at[pl.ds(0, tall.shape[0]), :], tall, sems.at[far])
-    )
-    for copy in copies:
-        copy.start()
+    early.wait()
     total = None
     for k in range(count):
-        term = jnp.dot(blocks[k][...], pieces[k][...], preferred_element_type=F32)
+        copies[k].wait()
+        if k == 0:
+            for copy in copies[count:] + [late]:
+                copy.start()
+        term = jnp.dot(wide[k][...], pieces[k][...], preferred_element_type=F32)
         total = term if total is None else total + term
     partial[...] = total
-    for copy in copies:
+    rest[0].wait()
+    row = rows_held[...]
+    device, inside = quotient(row, size), remainder(row, size)
+    digits = []
+    for axis in range(3):
+        length = sizes[axis]
+        digits.append(remainder(remainder(device, length) - here[axis] + length, length))
+        device = quotient(device, length)
+    digits.append(remainder(device - here[3] + sizes[3], sizes[3]))
+    first = digits[0]
+    for axis in (2, 1, 3):
+        first = first * sizes[axis] + digits[axis]
+    position = lax.broadcasted_iota(jnp.int32, row.shape, 0) * row.shape[1]
+    position = position + lax.broadcasted_iota(jnp.int32, row.shape, 1)
+    order = size * sizes[0] * sizes[1] * sizes[2] * sizes[3]
+    place[...] = jnp.where(position < here[4], first * size + inside, order)
+    for copy in rest[1:] + copies[count:] + [late]:
         copy.wait()
 
 
@@ -90,21 +125,15 @@
     return 256 if rows % 256 == 0 else rows
 
 
-def update_kernel(groups, far, place_far, coupling, partial, upper, *refs):
+def update_kernel(groups, far, place_far, tall, partial, *refs):
     blocks, pieces = refs[:far], refs[far : 2 * far]
-    forward, lower, own = refs[2 * far : 2 * far + 3]
-    sent = refs[2 * far + 3 : -5]
+    forward, own, sent = refs[2 * far], refs[2 * far + 1], refs[2 * far + 2 : -5]
     place, sems, placed, held = refs[-5], refs[-4], refs[-3], refs[-2:]
     order = placed.shape[0] - 8
-    split = upper.shape[0]
-    step = chunk_of(split)
-    count = (split + lower.shape[0]) // step
+    step = chunk_of(tall.shape[0])
+    count = tall.shape[0] // step
     index_copy = pltpu.make_async_copy(place_far, place, sems.at[0])
-    lower_copy = pltpu.make_async_copy(
-        coupling.at[pl.ds(split, lower.shape[0]), :], lower, sems.at[1]
-    )
     index_copy.start()
-    lower_copy.start()
     placed[...] = jnp.zeros_like(placed)
     total = partial[...]
     for k in range(far):
@@ -113,18 +142,16 @@
     index_copy.wait()
 
     def multiply(k):
-        first = k * step
-        if first == split:
-            lower_copy.wait()
-        source = upper if first < split else lower
-        first = first if first < split else first - split
         held[k % 2][...] = jnp.dot(
-            source[first : first + step, :], forward[...], preferred_element_type=F32
+            tall[k * step : (k + 1) * step, :], forward[...], preferred_element_type=F32
         )
 
+    lanes = place.shape[1]
+
     def scatter(k):
-        for t in range(step):
-            placed[pl.ds(place[k * step + t], 1), :] = held[k % 2][t : t + 1, :]
+        for t in range(k * step, (k + 1) * step):
+            row = place[t // lanes, t % lanes]
+            placed[pl.ds(row, 1), :] = held[k % 2][t - k * step : t - k * step + 1, :]
 
     multiply(0)
     for k in range(count):
@@ -165,8 +192,7 @@
     total = own[...]
     for ref in received:
         total = total + ref[...].astype(F32)
-    refs[-2][...] = total
-    refs[-1][...] = total.astype(BF16)
+    refs[-1][...] = total.astype(refs[-1].dtype)
 
 
 def stack_kernel(*refs):
@@ -220,7 +246,7 @@
         outs[h][...] = total.astype(outs[h].dtype)
 
 
-def border_kernel(blocks, far, place_far, forward, upper, lower, *refs):
+def border_kernel(blocks, far, place_far, forward, tall, *refs):
     wide, pieces = refs[:far], refs[far : far + blocks]
     corrected, sent = refs[far + blocks], refs[far + blocks + 1 : -6]
     place, sem, table, sums, held = refs[-6], refs[-5], refs[-4], refs[-3], refs[-2:]
@@ -228,9 +254,9 @@
     index_copy.start()
     rows = pieces[0].shape[0]
     order = blocks * rows
-    split = upper.shape[0]
-    step = chunk_of(split)
-    count = (split + lower.shape[0]) // step
+    step = chunk_of(tall.shape[0])
+    count = tall.shape[0] // step
+    lanes = place.shape[1]
     for k in range(blocks):
         table[k * rows : (k + 1) * rows, :] = pieces[k][...].astype(F32)
     table[order : order + 8, :] = jnp.zeros((8, table.shape[1]), F32)
@@ -238,16 +264,14 @@
     index_copy.wait()
 
     def gather(k):
-        for t in range(step):
-            held[k % 2][t : t + 1, :] = table[pl.ds(place[k * step + t], 1), :]
+        for t in range(k * step, (k + 1) * step):
+            row = place[t // lanes, t % lanes]
+            held[k % 2][t - k * step : t - k * step + 1, :] = table[pl.ds(row, 1), :]
 
     def multiply(k):
-        first = k * step
-        source = upper if first < split else lower
-        first = first if first < split else first - split
         sums[...] -= lax.dot_general(
             held[k % 2][...].astype(BF16),
-            source[first : first + step, :],
+            tall[k * step : (k + 1) * step, :],
             FIRST,
             preferred_element_type=F32,
         )
@@ -279,11 +303,18 @@
     refs[-1][...] = total.astype(out_dtype)
 
 
-def last_kernel(*refs):
+def turn_kernel(*refs):
     total = refs[0][...].astype(F32)
     for ref in refs[1:-1]:
         total = total + ref[...].astype(F32)
     refs[-1][...] = total.T
+
+
+def last_kernel(kept, *refs):
+    total = refs[0][...].astype(F32)
+    for ref in refs[1:-1]:
+        total = total + ref[...].astype(F32)
+    refs[-1][...] = kept[...] + total.T
 
 
 def like(shape, dtype):
@@ -342,15 +373,8 @@
         jnp.int32
     )
 
-    row = border_rows[0]
-    device, inside = row // own_rows, row % own_rows
-    rel_c = (device % nc - c) % nc
-    rel_y = (device // nc % nr - y) % nr
-    rel_x = (device // (nc * nr) % nx - x) % nx
-    rel_z = (device // (nc * nr * nx) - z) % nz
-    place = (((rel_c * nx + rel_x) * nr + rel_y) * nz + rel_z) * own_rows + inside
-    live = jnp.arange(borders, dtype=jnp.int32) < border_count[0]
-    place = jnp.where(live, place, order).astype(jnp.int32)
+    here = jnp.stack([c, y, x, z, border_count[0]]).astype(jnp.int32)
+    border = border_rows.reshape(borders // 128, 128) if borders % 128 == 0 else border_rows
 
     groups = [(dc, dz) for dc in range(nc) for dz in range(nz)]
     wide = len(groups) * own_rows
@@ -363,14 +387,30 @@
         [owner(dx, dy, dz, dc) for dx, dy in plane for dc, dz in groups]
     ).astype(jnp.int32)
     loads = parts if direct else 0
+    far_count = len(section) - nc
     loaded = kernel_call(
-        functools.partial(load_kernel, nc, loads, len(groups)),
-        [like((rows, rows), BF16)] * nc + [like((own_rows, wide), BF16)] * loads,
-        [block, column, factor, separator_factor],
-        scratch=[pltpu.SemaphoreType.DMA((nc + loads * len(groups),))],
-        apart=(2, 3),
-    )
-    near_blocks, cut = loaded[:nc], loaded[nc:]
+        functools.partial(
+            near_kernel, (nc, nr, nx, nz), nc, far_count, loads, len(groups)
+        ),
+        [
+            like((rows, columns), F32),
+            like(border.shape, jnp.int32),
+            like(coupling.shape, BF16),
+        ]
+        + [like((rows, rows), BF16)] * len(section)
+        + [like((own_rows, wide), BF16)] * loads,
+        [block, column, here, factor, separator_factor, border, coupling, *pieces[:nc]],
+        scratch=[
+            pltpu.VMEM(border.shape, jnp.int32),
+            pltpu.VMEM(rhs.shape, BF16),
+            pltpu.SemaphoreType.DMA((len(section) + loads * len(groups) + 3,)),
+        ],
+        flops=2 * rows * rows * nc * columns,
+        name="near",
+        apart=(3, 4, 5, 6, 7),
+    )
+    near, place, tall, near_blocks = *loaded[:3], loaded[3 : 3 + nc]
+    far_blocks, cut = loaded[3 + nc : 3 + len(section)], loaded[3 + len(section) :]
     if not direct:
         cut = [
             jnp.concatenate(
@@ -396,43 +436,32 @@
         root.append(shift(held[k], dx=-dx, dy=-dy))
 
     half = order // nc
-    far_count = len(section) - nc
-    split = borders // 2
-    loaded = kernel_call(
-        functools.partial(near_kernel, nc, far_count),
-        [like((rows, columns), F32), like((split, rows), BF16)]
-        + [like((rows, rows), BF16)] * far_count,
-        [block, factor, coupling, *near_blocks, *pieces[:nc]],
-        scratch=[pltpu.SemaphoreType.DMA((far_count + 1,))],
-        flops=2 * rows * rows * nc * columns,
-        apart=(1, 2),
-    )
-    near, upper, far_blocks = loaded[0], loaded[1], loaded[2:]
     outs = kernel_call(
         functools.partial(update_kernel, nc, far_count),
         [
             like((rows, columns), BF16),
-            like((borders - split, rows), BF16),
             like((half, columns), F32),
         ]
         + [like((half, columns), BF16)] * (nc - 1),
-        [place, coupling, near, upper, *far_blocks, *pieces[nc:]],
+        [place, tall, near, *far_blocks, *pieces[nc:]],
         scratch=[
             pltpu.SMEM(place.shape, jnp.int32),
-            pltpu.SemaphoreType.DMA((2,)),
+            pltpu.SemaphoreType.DMA((1,)),
             pltpu.VMEM((order + 8, columns), F32),
         ]
-        + [pltpu.VMEM((chunk_of(split), columns), F32)] * 2,
+        + [pltpu.VMEM((chunk_of(borders), columns), F32)] * 2,
         flops=2 * (coupling.size + rows * rows * far_count) * columns,
-        apart=(0, 1),
-    )
-    forward, lower, outs = outs[0], outs[1], outs[2:]
+        name="update",
+        apart=(0,),
+    )
+    forward, outs = outs[0], outs[1:]
     received = [shift(outs[dc], dc=dc) for dc in range(1, nc)]
     size = half // parts
     outs = kernel_call(
         functools.partial(add_kernel, len(received), parts),
         [like((size, columns), F32)] + [like((size, columns), BF16)] * (parts - 1),
         [outs[0], *received],
+        name="add_col",
     )
     received = []
     for k, (dx, dy) in list(enumerate(plane))[1:]:
@@ -441,19 +470,23 @@
         functools.partial(add_kernel, len(received), nz),
         [like((own_rows, columns), F32)] + [like((own_rows, columns), BF16)] * (nz - 1),
         [outs[0], *received],
+        name="add_plane",
     )
     received = send_z(outs)
     gathered = kernel_call(
         functools.partial(gathered_kernel, len(received)),
         [like((own_rows, columns), BF16)],
         [separator_rhs, outs[0], *received],
+        name="gathered",
     )[0]
 
     def along_z(value):
         values = [value]
         for dz in range(1, nz):
             values.append(shift(value, dz=-dz))
-        return kernel_call(stack_kernel, [like((nz * own_rows, columns), BF16)], values)[0]
+        return kernel_call(
+            stack_kernel, [like((nz * own_rows, columns), BF16)], values, name="stack"
+        )[0]
 
     column_block = along_z(gathered)
     right = [column_block] + [shift(column_block, dc=-dc) for dc in range(1, nc)]
@@ -462,6 +495,7 @@
         [like((parts * own_rows, columns), F32), like((parts * own_rows, columns), BF16)],
         [*root, *right],
         flops=2 * parts * own_rows * wide * columns,
+        name="root_forward",
     )
     received, sources = [], []
     for k, (dx, dy) in list(enumerate(plane))[1:]:
@@ -472,19 +506,28 @@
         [like((nz * own_rows, columns), F32)] + [like((nz * own_rows, columns), BF16)] * (nc - 1),
         [*root, kept, *received],
         flops=2 * parts * own_rows * wide * columns,
+        name="root_back",
     )
     received = [shift(outs[dc], dc=dc) for dc in range(1, nc)]
     outs = kernel_call(
         functools.partial(add_kernel, len(received), nz),
         [like((own_rows, columns), F32)] + [like((own_rows, columns), BF16)] * (nz - 1),
         [outs[0], *received],
+        name="add_col2",
     )
     received = send_z(outs)
-    separator_solution, rounded = kernel_call(
+    rounded = kernel_call(
         functools.partial(finish_kernel, len(received)),
-        [like((own_rows, columns), F32), like((own_rows, columns), BF16)],
+        [like((own_rows, columns), BF16)],
         [outs[0], *received],
-    )
+        name="finish",
+    )[0]
+    separator_solution = kernel_call(
+        functools.partial(finish_kernel, len(received)),
+        [like((own_rows, columns), F32)],
+        [outs[0], *received],
+        name="exact",
+    )[0]
     layer = along_z(rounded)
     table = [layer]
     for k, (dx, dy) in list(enumerate(plane))[1:]:
@@ -499,15 +542,16 @@
         functools.partial(border_kernel, len(pieces), len(far)),
         [like((columns, rows), BF16)]
         + [like((columns, rows), F32 if dc == 0 else BF16) for dy, dc in far],
-        [place, forward, upper, lower, *far_blocks, *pieces],
+        [place, forward, tall, *far_blocks, *pieces],
         scratch=[
             pltpu.SMEM(place.shape, jnp.int32),
             pltpu.SemaphoreType.DMA((1,)),
             pltpu.VMEM((order + 8, columns), F32),
             pltpu.VMEM((columns, rows), F32),
         ]
-        + [pltpu.VMEM((chunk_of(split), columns), F32)] * 2,
+        + [pltpu.VMEM((chunk_of(borders), columns), F32)] * 2,
         flops=2 * (coupling.size + factor.size * len(far) // len(section)) * columns,
+        name="border",
         apart=(0,),
     )
     corrected, far_parts = outs[0], dict(zip(far, outs[1:]))
@@ -515,7 +559,7 @@
     for dy in range(1, nr):
         terms = [far_parts[dy, 0]] + [shift(far_parts[dy, dc], dc=dc) for dc in range(1, nc)]
         total = kernel_call(
-            functools.partial(sum_kernel, BF16), [like((columns, rows), BF16)], terms
+            functools.partial(sum_kernel, BF16), [like((columns, rows), BF16)], terms, name="sum_far"
         )[0]
         arrived.append(shift(total, dy=dy))
     outs = kernel_call(
@@ -523,9 +567,14 @@
         [like((columns, rows), F32 if dc == 0 else BF16) for dy, dc in near],
         [corrected, *near_blocks],
         flops=2 * factor.size * len(near) // len(section) * columns,
+        name="own_blocks",
     )
     terms = [outs[0]] + [shift(outs[dc], dc=dc) for dc in range(1, nc)]
-    leaf_solution = kernel_call(last_kernel, [like((rows, columns), F32)], [*terms, *arrived])[0]
+    leaf_solution = kernel_call(turn_kernel, [like((rows, columns), F32)], terms, name="turn")[0]
+    if arrived:
+        leaf_solution = kernel_call(
+            last_kernel, [like((rows, columns), F32)], [leaf_solution, *arrived], name="last"
+        )[0]
     return leaf_solution[None], separator_solution
 
 

time: 111 us -> 113 us (1.018)
  waiting for transfers between devices: 45.5 us -> 49.4 us
  Pallas kernels: 24.9 us -> 23.3 us
    ppermute x37, waiting for transfers between devices: 45.5 us -> 49.4 us  [shift(): return lax.ppermute(value, AXES, pairs)]
    pallas_call x16 -> x17, Pallas kernels: 24.9 us -> 23.3 us  [kernel_call(): pl.pallas_call(body, out_shape=list(outs), in_specs=specs, out_specs=[VM]...]
  transfers between devices with their start and end apart: 37 -> 37, of which waited for: 26 -> 26; matrix products, arithmetic and copies ran while one was open for 0% -> 0% of each run, Pallas kernels for 9% -> 8%
where the time goes in v4:
time: 113 us; the launch traced here: 112 us
  waiting for transfers between devices  49.4 us (44%)
  starting transfers between devices  38 us (34%)
  Pallas kernels  23.3 us (21%)
  between operations  1.46 us (1%)
    ppermute x37, waiting for transfers between devices, shift(): return lax.ppermute(value, AXES, pairs)  49.4 us
    ppermute x37, starting transfers between devices, shift(): return lax.ppermute(value, AXES, pairs)  38 us
    pallas_call x17, Pallas kernels, kernel_call(): pl.pallas_call(body, out_shape=list(outs), in_specs=specs, out_specs=[VM]...  23.3 us
  transfers between devices with their start and end apart: 37, of which 26 were waited for; matrix products, arithmetic and copies ran while one was open for 0% of the time, Pallas kernels for 8%

profile of v4, /device:TPU:0, one launch (start us, length us, event | category | flops | bytes accessed | tf_op | source)
XLA Modules:
  0.0 112.4 jit_solution(7801568122448304153)
XLA Ops:
  0.6 3.1 %collective-permute-start.1 = (bf16[1024,128]{1,0:T(8,128)(2,1)}, bf16[1024,128]{1,0:T(8,128)(2,1)S(1)}, u32[]{:S(2)}, u32[]{:S(2)}) collective-permute-start(bf16[1024,128]{1,0:T(8,128)(2,1)} %bitcast.48), channel_id=1, source_target_pairs={{0,2},{1,3},{2,0},{3,1},{4,6},{5,7},{6,4},{7,5},{8,10},{9,11},{10,... | collective-permute-start | bytes 786440 | tf_op jit(solution)/shard_map/ppermute | solution.py:358
  3.7 6.5 %collective-permute-done.1.refs_2_ = bf16[1024,128]{1,0:T(8,128)(2,1)S(1)} collective-permute-done((bf16[1024,128]{1,0:T(8,128)(2,1)}, bf16[1024,128]{1,0:T(8,128)(2,1)S(1)}, u32[]{:S(2)}, u32[]{:S(2)}) %collective-permute-start.1) | collective-permute-done | bytes 262176 | tf_op jit(solution)/shard_map/ppermute | solution.py:358
  11.1 7.6 %shard_map.86 = (f32[1024,128]{1,0:T(8,128)S(1)}, s32[32,128]{1,0:T(8,128)S(1)}, bf16[4096,1024]{1,0:T(8,128)(2,1)S(1)}, bf16[1024,1024]{1,0:T(8,128)(2,1)S(1)},...) custom-call(s32[4]{0:T(128)S(1)} %pad_add_fusion.block, ...), custom_call_target="tpu_custom_call" | custom-call | flops 536870912 | bytes 36733092 | tf_op jit(solution)/shard_map/pallas_call | solution.py:31
  18.7 6.5 %shard_map.87 = (bf16[1024,128]{1,0:T(8,128)(2,1)S(1)}, f32[2048,128]{1,0:T(8,128)S(1)}, bf16[2048,128]{1,0:T(8,128)(2,1)S(1)}) custom-call(s32[32,128]{1,0:T(8,128)S(1)} %get-tuple-element.40.place_far, bf16[4096,1024]{1,0:T(8,128)(2,1)S(1)} %get-tuple-element.41.tall, f32[1024,128]{1,0:T(8,128)S(1)} %get-tuple-element.42.partial, ...), custom_call_target="tpu_custom_call" | custom-call | flops 1610612736 | bytes 15482880 | tf_op jit(solution)/shard_map/pallas_call | solution.py:31
  27.4 1.8 %collective-permute-start.7 = (bf16[512,128]{1,0:T(8,128)(2,1)S(1)}, bf16[512,128]{1,0:T(8,128)(2,1)S(1)}, u32[]{:S(2)}, u32[]{:S(2)}) collective-permute-start(bf16[512,128]{1,0:T(8,128)(2,1)S(1)} %get-tuple-element.56), channel_id=1, source_target_pairs={{0,2},{1,3},{2,0},{3,1},{4,6},{5,7},{6,4},{7,5},{8,10},{9,11},{10,... | collective-permute-start | bytes 393224 | tf_op jit(solution)/shard_map/ppermute | solution.py:358
  31.0 2.3 %collective-permute-done.7.refs_1_ = bf16[512,128]{1,0:T(8,128)(2,1)S(1)} collective-permute-done((bf16[512,128]{1,0:T(8,128)(2,1)S(1)}, bf16[512,128]{1,0:T(8,128)(2,1)S(1)}, u32[]{:S(2)}, u32[]{:S(2)}) %collective-permute-start.7) | collective-permute-done | bytes 131104 | tf_op jit(solution)/shard_map/ppermute | solution.py:358
  33.3 2.3 %collective-permute-done.8.refs_2_ = bf16[512,128]{1,0:T(8,128)(2,1)S(1)} collective-permute-done((bf16[512,128]{1,0:T(8,128)(2,1)S(1)}, bf16[512,128]{1,0:T(8,128)(2,1)S(1)}, u32[]{:S(2)}, u32[]{:S(2)}) %collective-permute-start.8) | collective-permute-done | bytes 131104 | tf_op jit(solution)/shard_map/ppermute | solution.py:358
  35.6 1.7 %collective-permute-done.9.refs_3_ = bf16[512,128]{1,0:T(8,128)(2,1)S(1)} collective-permute-done((bf16[512,128]{1,0:T(8,128)(2,1)S(1)}, bf16[512,128]{1,0:T(8,128)(2,1)S(1)}, u32[]{:S(2)}, u32[]{:S(2)}) %collective-permute-start.9) | collective-permute-done | bytes 131104 | tf_op jit(solution)/shard_map/ppermute | solution.py:358
  37.4 1.8 %collective-permute-start.10 = (bf16[128,128]{1,0:T(8,128)(2,1)S(1)}, bf16[128,128]{1,0:T(8,128)(2,1)S(1)}, u32[]{:S(2)}, u32[]{:S(2)}) collective-permute-start(bf16[128,128]{1,0:T(8,128)(2,1)S(1)} %get-tuple-element.60), channel_id=1, source_target_pairs={{0,8},{1,9},{2,10},{3,11},{4,12},{5,13},{6,14},{7,15},{8,16},{9,17... | collective-permute-start | bytes 98312 | tf_op jit(solution)/shard_map/ppermute | solution.py:358
  42.7 2.6 %collective-permute-start.11 = (bf16[128,128]{1,0:T(8,128)(2,1)S(1)}, bf16[128,128]{1,0:T(8,128)(2,1)S(1)}, u32[]{:S(2)}, u32[]{:S(2)}) collective-permute-start(bf16[128,128]{1,0:T(8,128)(2,1)S(1)} %get-tuple-element.61), channel_id=1, source_target_pairs={{0,16},{1,17},{2,18},{3,19},{4,20},{5,21},{6,22},{7,23},{8,24},{9,... | collective-permute-start | bytes 98312 | tf_op jit(solution)/shard_map/ppermute | solution.py:358
  49.5 3.5 %collective-permute-start.14 = (bf16[128,128]{1,0:T(8,128)(2,1)S(1)}, bf16[128,128]{1,0:T(8,128)(2,1)S(1)}, u32[]{:S(2)}, u32[]{:S(2)}) collective-permute-start(bf16[128,128]{1,0:T(8,128)(2,1)S(1)} %shard_map.90.refs_0_), channel_id=1, source_target_pairs={{0,16},{1,17},{2,18},{3,19},{4,20},{5,21},{6,22},{7,23},{8,24},{9,... | collective-permute-start | bytes 98312 | tf_op jit(solution)/shard_map/ppermute | solution.py:358
  53.0 2.1 %collective-permute-done.15.refs_3_ = bf16[128,128]{1,0:T(8,128)(2,1)S(1)} collective-permute-done((bf16[128,128]{1,0:T(8,128)(2,1)S(1)}, bf16[128,128]{1,0:T(8,128)(2,1)S(1)}, u32[]{:S(2)}, u32[]{:S(2)}) %collective-permute-start.15) | collective-permute-done | bytes 32800 | tf_op jit(solution)/shard_map/ppermute | solution.py:358
  56.3 2.7 %collective-permute-done.13.refs_1_ = bf16[128,128]{1,0:T(8,128)(2,1)S(1)} collective-permute-done((bf16[128,128]{1,0:T(8,128)(2,1)S(1)}, bf16[128,128]{1,0:T(8,128)(2,1)S(1)}, u32[]{:S(2)}, u32[]{:S(2)}) %collective-permute-start.13) | collective-permute-done | bytes 32800 | tf_op jit(solution)/shard_map/ppermute | solution.py:358
  60.9 2.5 %collective-permute-start.19 = (bf16[512,128]{1,0:T(8,128)(2,1)S(1)}, bf16[512,128]{1,0:T(8,128)(2,1)S(1)}, u32[]{:S(2)}, u32[]{:S(2)}) collective-permute-start(bf16[512,128]{1,0:T(8,128)(2,1)S(1)} %get-tuple-element.64), channel_id=1, source_target_pairs={{0,6},{1,7},{2,4},{3,5},{4,2},{5,3},{6,0},{7,1},{8,14},{9,15},{10,... | collective-permute-start | bytes 393224 | tf_op jit(solution)/shard_map/ppermute | solution.py:358
  64.4 3.8 %collective-permute-done.19.refs_7_ = bf16[512,128]{1,0:T(8,128)(2,1)S(1)} collective-permute-done((bf16[512,128]{1,0:T(8,128)(2,1)S(1)}, bf16[512,128]{1,0:T(8,128)(2,1)S(1)}, u32[]{:S(2)}, u32[]{:S(2)}) %collective-permute-start.19) | collective-permute-done | bytes 131104 | tf_op jit(solution)/shard_map/ppermute | solution.py:358
  68.2 2.0 %collective-permute-done.18.refs_6_ = bf16[512,128]{1,0:T(8,128)(2,1)S(1)} collective-permute-done((bf16[512,128]{1,0:T(8,128)(2,1)S(1)}, bf16[512,128]{1,0:T(8,128)(2,1)S(1)}, u32[]{:S(2)}, u32[]{:S(2)}) %collective-permute-start.18) | collective-permute-done | bytes 131104 | tf_op jit(solution)/shard_map/ppermute | solution.py:358
  72.2 3.6 %collective-permute-start.22 = (bf16[128,128]{1,0:T(8,128)(2,1)S(1)}, bf16[128,128]{1,0:T(8,128)(2,1)S(1)}, u32[]{:S(2)}, u32[]{:S(2)}) collective-permute-start(bf16[128,128]{1,0:T(8,128)(2,1)S(1)} %get-tuple-element.69), channel_id=1, source_target_pairs={{0,16},{1,17},{2,18},{3,19},{4,20},{5,21},{6,22},{7,23},{8,24},{9,... | collective-permute-start | bytes 98312 | tf_op jit(solution)/shard_map/ppermute | solution.py:358
  76.1 2.1 %collective-permute-done.21.refs_1_ = bf16[128,128]{1,0:T(8,128)(2,1)S(1)} collective-permute-done((bf16[128,128]{1,0:T(8,128)(2,1)S(1)}, bf16[128,128]{1,0:T(8,128)(2,1)S(1)}, u32[]{:S(2)}, u32[]{:S(2)}) %collective-permute-start.21) | collective-permute-done | bytes 32800 | tf_op jit(solution)/shard_map/ppermute | solution.py:358
  80.6 2.0 %collective-permute-start.25 = (bf16[128,128]{1,0:T(8,128)(2,1)S(1)}, bf16[128,128]{1,0:T(8,128)(2,1)S(1)}, u32[]{:S(2)}, u32[]{:S(2)}) collective-permute-start(bf16[128,128]{1,0:T(8,128)(2,1)S(1)} %shard_map.95.refs_0_), channel_id=1, source_target_pairs={{0,16},{1,17},{2,18},{3,19},{4,20},{5,21},{6,22},{7,23},{8,24},{9,... | collective-permute-start | bytes 98312 | tf_op jit(solution)/shard_map/ppermute | solution.py:358
  83.7 2.0 %collective-permute-done.26.refs_3_ = bf16[128,128]{1,0:T(8,128)(2,1)S(1)} collective-permute-done((bf16[128,128]{1,0:T(8,128)(2,1)S(1)}, bf16[128,128]{1,0:T(8,128)(2,1)S(1)}, u32[]{:S(2)}, u32[]{:S(2)}) %collective-permute-start.26) | collective-permute-done | bytes 32800 | tf_op jit(solution)/shard_map/ppermute | solution.py:358
  86.5 2.5 %collective-permute-start.29 = (bf16[512,128]{1,0:T(8,128)(2,1)S(1)}, bf16[512,128]{1,0:T(8,128)(2,1)S(1)}, u32[]{:S(2)}, u32[]{:S(2)}) collective-permute-start(bf16[512,128]{1,0:T(8,128)(2,1)S(1)} %shard_map.96.refs_2_), channel_id=1, source_target_pairs={{0,6},{1,7},{2,4},{3,5},{4,2},{5,3},{6,0},{7,1},{8,14},{9,15},{10,... | collective-permute-start | bytes 393224 | tf_op jit(solution)/shard_map/ppermute | solution.py:358
  90.1 2.4 %collective-permute-done.29.refs_5_ = bf16[512,128]{1,0:T(8,128)(2,1)S(1)} collective-permute-done((bf16[512,128]{1,0:T(8,128)(2,1)S(1)}, bf16[512,128]{1,0:T(8,128)(2,1)S(1)}, u32[]{:S(2)}, u32[]{:S(2)}) %collective-permute-start.29) | collective-permute-done | bytes 131104 | tf_op jit(solution)/shard_map/ppermute | solution.py:358
  95.8 5.6 %shard_map.97 = (bf16[128,1024]{1,0:T(8,128)(2,1)S(1)}, f32[128,1024]{1,0:T(8,128)S(1)}, bf16[128,1024]{1,0:T(8,128)(2,1)S(1)}) custom-call(s32[32,128]{1,0:T(8,128)S(1)} %get-tuple-element.40.place_far, bf16[1024,128]{1,0:T(8,128)(2,1)S(1)} %get-tuple-element.48.forward, bf16[4096,1024]{1,0:T(8,128)(2,1)S(1)} %get-tuple-element.41.tall, ...), custom_call_target="tpu_custom_call" | custom-call | flops 1610612736 | bytes 14958592 | tf_op jit(solution)/shard_map/pallas_call | solution.py:31
  104.8 6.7 %collective-permute-done.36.refs_0_ = bf16[128,1024]{1,0:T(8,128)(2,1)S(1)} collective-permute-done((bf16[128,1024]{1,0:T(8,128)(2,1)S(1)}, bf16[128,1024]{1,0:T(8,128)(2,1)S(1)}, u32[]{:S(2)}, u32[]{:S(2)}) %collective-permute-start.36) | collective-permute-done | bytes 262176 | tf_op jit(solution)/shard_map/ppermute | solution.py:358
  (72 shorter events, 31.4 us)
Async XLA Ops:
  0.6 9.6 %collective-permute-start.1 = (bf16[1024,128]{1,0:T(8,128)(2,1)}, bf16[1024,128]{1,0:T(8,128)(2,1)S(1)}, u32[]{:S(2)}, u32[]{:S(2)}) collective-permute-start(bf16[1024,128]{1,0:T(8,128)(2,1)} %bitcast.48), channel_id=1, source_target_pairs={{0,2},{1,3},{2,0},{3,1},{4,6},{5,7},{6,4},{7,5},{8,10},{9,11},{10,... | collective-permute-start | bytes 786440 | tf_op jit(solution)/shard_map/ppermute | solution.py:358
  3.7 7.5 %collective-permute-start = (bf16[1024,128]{1,0:T(8,128)(2,1)}, bf16[1024,128]{1,0:T(8,128)(2,1)S(1)}, u32[]{:S(2)}, u32[]{:S(2)}) collective-permute-start(bf16[1024,128]{1,0:T(8,128)(2,1)} %bitcast.49), channel_id=1, source_target_pairs={{0,1},{1,0},{2,3},{3,2},{4,5},{5,4},{6,7},{7,6},{8,9},{9,8},{10,11... | collective-permute-start | bytes 786440 | tf_op jit(solution)/shard_map/ppermute | solution.py:358
  10.2 8.5 %collective-permute-start.2 = (bf16[1024,128]{1,0:T(8,128)(2,1)S(1)}, bf16[1024,128]{1,0:T(8,128)(2,1)S(1)}, u32[]{:S(2)}, u32[]{:S(2)}) collective-permute-start(bf16[1024,128]{1,0:T(8,128)(2,1)S(1)} %collective-permute-done.1.refs_2_), channel_id=1, source_target_pairs={{0,1},{1,0},{2,3},{3,2},{4,5},{5,4},{6,7},{7,6},{8,9},{9,8},{10,11... | collective-permute-start | bytes 786440 | tf_op jit(solution)/shard_map/ppermute | solution.py:358
  27.4 5.8 %collective-permute-start.7 = (bf16[512,128]{1,0:T(8,128)(2,1)S(1)}, bf16[512,128]{1,0:T(8,128)(2,1)S(1)}, u32[]{:S(2)}, u32[]{:S(2)}) collective-permute-start(bf16[512,128]{1,0:T(8,128)(2,1)S(1)} %get-tuple-element.56), channel_id=1, source_target_pairs={{0,2},{1,3},{2,0},{3,1},{4,6},{5,7},{6,4},{7,5},{8,10},{9,11},{10,... | collective-permute-start | bytes 393224 | tf_op jit(solution)/shard_map/ppermute | solution.py:358
  29.2 6.4 %collective-permute-start.8 = (bf16[512,128]{1,0:T(8,128)(2,1)S(1)}, bf16[512,128]{1,0:T(8,128)(2,1)S(1)}, u32[]{:S(2)}, u32[]{:S(2)}) collective-permute-start(bf16[512,128]{1,0:T(8,128)(2,1)S(1)} %get-tuple-element.57), channel_id=1, source_target_pairs={{0,4},{1,5},{2,6},{3,7},{4,0},{5,1},{6,2},{7,3},{8,12},{9,13},{10,... | collective-permute-start | bytes 393224 | tf_op jit(solution)/shard_map/ppermute | solution.py:358
  30.8 6.6 %collective-permute-start.9 = (bf16[512,128]{1,0:T(8,128)(2,1)S(1)}, bf16[512,128]{1,0:T(8,128)(2,1)S(1)}, u32[]{:S(2)}, u32[]{:S(2)}) collective-permute-start(bf16[512,128]{1,0:T(8,128)(2,1)S(1)} %get-tuple-element.58), channel_id=1, source_target_pairs={{0,6},{1,7},{2,4},{3,5},{4,2},{5,3},{6,0},{7,1},{8,14},{9,15},{10,... | collective-permute-start | bytes 393224 | tf_op jit(solution)/shard_map/ppermute | solution.py:358
  37.4 7.9 %collective-permute-start.10 = (bf16[128,128]{1,0:T(8,128)(2,1)S(1)}, bf16[128,128]{1,0:T(8,128)(2,1)S(1)}, u32[]{:S(2)}, u32[]{:S(2)}) collective-permute-start(bf16[128,128]{1,0:T(8,128)(2,1)S(1)} %get-tuple-element.60), channel_id=1, source_target_pairs={{0,8},{1,9},{2,10},{3,11},{4,12},{5,13},{6,14},{7,15},{8,16},{9,17... | collective-permute-start | bytes 98312 | tf_op jit(solution)/shard_map/ppermute | solution.py:358
  39.2 19.9 %collective-permute-start.3 = (bf16[128,1024]{1,0:T(8,128)(2,1)S(1)}, bf16[128,1024]{1,0:T(8,128)(2,1)S(1)}, u32[]{:S(2)}, u32[]{:S(2)}) collective-permute-start(bf16[128,1024]{1,0:T(8,128)(2,1)S(1)} %get-tuple-element.50), channel_id=1, source_target_pairs={{0,2},{1,3},{2,0},{3,1},{4,6},{5,7},{6,4},{7,5},{8,10},{9,11},{10,... | collective-permute-start | bytes 786440 | tf_op jit(solution)/shard_map/ppermute | solution.py:358
  40.7 18.4 %collective-permute-start.5 = (bf16[128,1024]{1,0:T(8,128)(2,1)S(1)}, bf16[128,1024]{1,0:T(8,128)(2,1)S(1)}, u32[]{:S(2)}, u32[]{:S(2)}) collective-permute-start(bf16[128,1024]{1,0:T(8,128)(2,1)S(1)} %get-tuple-element.52), channel_id=1, source_target_pairs={{0,6},{1,7},{2,4},{3,5},{4,2},{5,3},{6,0},{7,1},{8,14},{9,15},{10,... | collective-permute-start | bytes 786440 | tf_op jit(solution)/shard_map/ppermute | solution.py:358
  42.2 17.0 %collective-permute-start.4 = (bf16[128,1024]{1,0:T(8,128)(2,1)S(1)}, bf16[128,1024]{1,0:T(8,128)(2,1)S(1)}, u32[]{:S(2)}, u32[]{:S(2)}) collective-permute-start(bf16[128,1024]{1,0:T(8,128)(2,1)S(1)} %get-tuple-element.51), channel_id=1, source_target_pairs={{0,4},{1,5},{2,6},{3,7},{4,0},{5,1},{6,2},{7,3},{8,12},{9,13},{10,... | collective-permute-start | bytes 786440 | tf_op jit(solution)/shard_map/ppermute | solution.py:358
  42.7 4.8 %collective-permute-start.11 = (bf16[128,128]{1,0:T(8,128)(2,1)S(1)}, bf16[128,128]{1,0:T(8,128)(2,1)S(1)}, u32[]{:S(2)}, u32[]{:S(2)}) collective-permute-start(bf16[128,128]{1,0:T(8,128)(2,1)S(1)} %get-tuple-element.61), channel_id=1, source_target_pairs={{0,16},{1,17},{2,18},{3,19},{4,20},{5,21},{6,22},{7,23},{8,24},{9,... | collective-permute-start | bytes 98312 | tf_op jit(solution)/shard_map/ppermute | solution.py:358
  49.2 5.9 %collective-permute-start.15 = (bf16[128,128]{1,0:T(8,128)(2,1)S(1)}, bf16[128,128]{1,0:T(8,128)(2,1)S(1)}, u32[]{:S(2)}, u32[]{:S(2)}) collective-permute-start(bf16[128,128]{1,0:T(8,128)(2,1)S(1)} %shard_map.90.refs_0_), channel_id=1, source_target_pairs={{0,8},{1,9},{2,10},{3,11},{4,12},{5,13},{6,14},{7,15},{8,16},{9,17... | collective-permute-start | bytes 98312 | tf_op jit(solution)/shard_map/ppermute | solution.py:358
  49.5 6.9 %collective-permute-start.14 = (bf16[128,128]{1,0:T(8,128)(2,1)S(1)}, bf16[128,128]{1,0:T(8,128)(2,1)S(1)}, u32[]{:S(2)}, u32[]{:S(2)}) collective-permute-start(bf16[128,128]{1,0:T(8,128)(2,1)S(1)} %shard_map.90.refs_0_), channel_id=1, source_target_pairs={{0,16},{1,17},{2,18},{3,19},{4,20},{5,21},{6,22},{7,23},{8,24},{9,... | collective-permute-start | bytes 98312 | tf_op jit(solution)/shard_map/ppermute | solution.py:358
  60.9 7.3 %collective-permute-start.19 = (bf16[512,128]{1,0:T(8,128)(2,1)S(1)}, bf16[512,128]{1,0:T(8,128)(2,1)S(1)}, u32[]{:S(2)}, u32[]{:S(2)}) collective-permute-start(bf16[512,128]{1,0:T(8,128)(2,1)S(1)} %get-tuple-element.64), channel_id=1, source_target_pairs={{0,6},{1,7},{2,4},{3,5},{4,2},{5,3},{6,0},{7,1},{8,14},{9,15},{10,... | collective-permute-start | bytes 393224 | tf_op jit(solution)/shard_map/ppermute | solution.py:358
  63.4 6.9 %collective-permute-start.18 = (bf16[512,128]{1,0:T(8,128)(2,1)S(1)}, bf16[512,128]{1,0:T(8,128)(2,1)S(1)}, u32[]{:S(2)}, u32[]{:S(2)}) collective-permute-start(bf16[512,128]{1,0:T(8,128)(2,1)S(1)} %get-tuple-element.64), channel_id=1, source_target_pairs={{0,4},{1,5},{2,6},{3,7},{4,0},{5,1},{6,2},{7,3},{8,12},{9,13},{10,... | collective-permute-start | bytes 393224 | tf_op jit(solution)/shard_map/ppermute | solution.py:358
  63.9 6.3 %collective-permute-start.17 = (bf16[512,128]{1,0:T(8,128)(2,1)S(1)}, bf16[512,128]{1,0:T(8,128)(2,1)S(1)}, u32[]{:S(2)}, u32[]{:S(2)}) collective-permute-start(bf16[512,128]{1,0:T(8,128)(2,1)S(1)} %get-tuple-element.64), channel_id=1, source_target_pairs={{0,2},{1,3},{2,0},{3,1},{4,6},{5,7},{6,4},{7,5},{8,10},{9,11},{10,... | collective-permute-start | bytes 393224 | tf_op jit(solution)/shard_map/ppermute | solution.py:358
  72.2 5.9 %collective-permute-start.21 = (bf16[128,128]{1,0:T(8,128)(2,1)S(1)}, bf16[128,128]{1,0:T(8,128)(2,1)S(1)}, u32[]{:S(2)}, u32[]{:S(2)}) collective-permute-start(bf16[128,128]{1,0:T(8,128)(2,1)S(1)} %get-tuple-element.68), channel_id=1, source_target_pairs={{0,8},{1,9},{2,10},{3,11},{4,12},{5,13},{6,14},{7,15},{8,16},{9,17... | collective-permute-start | bytes 98312 | tf_op jit(solution)/shard_map/ppermute | solution.py:358
  72.2 6.6 %collective-permute-start.22 = (bf16[128,128]{1,0:T(8,128)(2,1)S(1)}, bf16[128,128]{1,0:T(8,128)(2,1)S(1)}, u32[]{:S(2)}, u32[]{:S(2)}) collective-permute-start(bf16[128,128]{1,0:T(8,128)(2,1)S(1)} %get-tuple-element.69), channel_id=1, source_target_pairs={{0,16},{1,17},{2,18},{3,19},{4,20},{5,21},{6,22},{7,23},{8,24},{9,... | collective-permute-start | bytes 98312 | tf_op jit(solution)/shard_map/ppermute | solution.py:358
  79.8 5.9 %collective-permute-start.26 = (bf16[128,128]{1,0:T(8,128)(2,1)S(1)}, bf16[128,128]{1,0:T(8,128)(2,1)S(1)}, u32[]{:S(2)}, u32[]{:S(2)}) collective-permute-start(bf16[128,128]{1,0:T(8,128)(2,1)S(1)} %shard_map.95.refs_0_), channel_id=1, source_target_pairs={{0,8},{1,9},{2,10},{3,11},{4,12},{5,13},{6,14},{7,15},{8,16},{9,17... | collective-permute-start | bytes 98312 | tf_op jit(solution)/shard_map/ppermute | solution.py:358
  80.6 5.5 %collective-permute-start.25 = (bf16[128,128]{1,0:T(8,128)(2,1)S(1)}, bf16[128,128]{1,0:T(8,128)(2,1)S(1)}, u32[]{:S(2)}, u32[]{:S(2)}) collective-permute-start(bf16[128,128]{1,0:T(8,128)(2,1)S(1)} %shard_map.95.refs_0_), channel_id=1, source_target_pairs={{0,16},{1,17},{2,18},{3,19},{4,20},{5,21},{6,22},{7,23},{8,24},{9,... | collective-permute-start | bytes 98312 | tf_op jit(solution)/shard_map/ppermute | solution.py:358
  86.5 5.9 %collective-permute-start.29 = (bf16[512,128]{1,0:T(8,128)(2,1)S(1)}, bf16[512,128]{1,0:T(8,128)(2,1)S(1)}, u32[]{:S(2)}, u32[]{:S(2)}) collective-permute-start(bf16[512,128]{1,0:T(8,128)(2,1)S(1)} %shard_map.96.refs_2_), channel_id=1, source_target_pairs={{0,6},{1,7},{2,4},{3,5},{4,2},{5,3},{6,0},{7,1},{8,14},{9,15},{10,... | collective-permute-start | bytes 393224 | tf_op jit(solution)/shard_map/ppermute | solution.py:358
  89.0 5.0 %collective-permute-start.28 = (bf16[512,128]{1,0:T(8,128)(2,1)S(1)}, bf16[512,128]{1,0:T(8,128)(2,1)S(1)}, u32[]{:S(2)}, u32[]{:S(2)}) collective-permute-start(bf16[512,128]{1,0:T(8,128)(2,1)S(1)} %shard_map.96.refs_2_), channel_id=1, source_target_pairs={{0,4},{1,5},{2,6},{3,7},{4,0},{5,1},{6,2},{7,3},{8,12},{9,13},{10,... | collective-permute-start | bytes 393224 | tf_op jit(solution)/shard_map/ppermute | solution.py:358
  89.5 5.0 %collective-permute-start.27 = (bf16[512,128]{1,0:T(8,128)(2,1)S(1)}, bf16[512,128]{1,0:T(8,128)(2,1)S(1)}, u32[]{:S(2)}, u32[]{:S(2)}) collective-permute-start(bf16[512,128]{1,0:T(8,128)(2,1)S(1)} %shard_map.96.refs_2_), channel_id=1, source_target_pairs={{0,2},{1,3},{2,0},{3,1},{4,6},{5,7},{6,4},{7,5},{8,10},{9,11},{10,... | collective-permute-start | bytes 393224 | tf_op jit(solution)/shard_map/ppermute | solution.py:358
  103.0 8.4 %collective-permute-start.36 = (bf16[128,1024]{1,0:T(8,128)(2,1)S(1)}, bf16[128,1024]{1,0:T(8,128)(2,1)S(1)}, u32[]{:S(2)}, u32[]{:S(2)}) collective-permute-start(bf16[128,1024]{1,0:T(8,128)(2,1)S(1)} %shard_map.100), channel_id=1, source_target_pairs={{0,2},{1,3},{2,0},{3,1},{4,6},{5,7},{6,4},{7,5},{8,10},{9,11},{10,... | collective-permute-start | bytes 786440 | tf_op jit(solution)/shard_map/ppermute | solution.py:358
  (14 other events, 57.6 us)
